TPU v7x, 32 devices: a whole 2x2x4 slice. The times are simulated.
32 devices in a mesh: dp: 8 (over z, core), seq: 4 (over y, x).
Axes of the slice: x: 2, y: 2, z: 4, core: 2. Of those that a mesh axis runs over, the one named last changes fastest.
Arguments:
- tokens: bfloat16 [4096, 2048], P(('dp', 'seq')), may hold values from -6 to 6
- lengths: int32 [8, 1], P('dp'), may hold values from 512 to 512, as said below
- cotangent: bfloat16 [4096, 2048], P(('dp', 'seq')), may hold values from -6 to 6
- attn_norm_gain: bfloat16 [2048], replicated, may hold values from 0.25 to 1.75
- w_query: bfloat16 [2048, 2048], P('dp', 'seq'), may hold values from -0.125 to 0.125
- w_key: bfloat16 [2048, 2048], P('dp', 'seq'), may hold values from -0.125 to 0.125
- w_value: bfloat16 [2048, 2048], P('dp', 'seq'), may hold values from -0.125 to 0.125
- w_strength: bfloat16 [2048, 16], P('dp', 'seq'), may hold values from -0.125 to 0.125
- conv_weight: bfloat16 [3, 4, 2048], P(None, None, 'seq'), may hold values from -3 to 3
- head_gain: bfloat16 [128], replicated, may hold values from 0.25 to 1.75
- w_output: bfloat16 [2048, 2048], P('seq', 'dp'), may hold values from -0.125 to 0.125
- ffn_norm_gain: bfloat16 [2048], replicated, may hold values from 0.25 to 1.75
- w_gate: bfloat16 [2048, 5632], P('dp', 'seq'), may hold values from -0.125 to 0.125
- w_up: bfloat16 [2048, 5632], P('dp', 'seq'), may hold values from -0.125 to 0.125
- w_down: bfloat16 [5632, 2048], P('seq', 'dp'), may hold values from -0.15625 to 0.15625
Outputs:
- output: bfloat16 [4096, 2048], P(('dp', 'seq'))
- input_grad: float32 [4096, 2048], P(('dp', 'seq'))
- grad_attn_norm_gain: float32 [2048], replicated
- grad_w_query: float32 [2048, 2048], P('dp', 'seq')
- grad_w_key: float32 [2048, 2048], P('dp', 'seq')
- grad_w_value: float32 [2048, 2048], P('dp', 'seq')
- grad_w_strength: float32 [2048, 16], P('dp', 'seq')
- grad_conv_weight: float32 [3, 4, 2048], P(None, None, 'seq')
- grad_head_gain: float32 [128], replicated
- grad_w_output: float32 [2048, 2048], P('seq', 'dp')
- grad_ffn_norm_gain: float32 [2048], replicated
- grad_w_gate: float32 [2048, 5632], P('dp', 'seq')
- grad_w_up: float32 [2048, 5632], P('dp', 'seq')
- grad_w_down: float32 [5632, 2048], P('seq', 'dp')
Inputs may be any that keep to these rules, and one draw needn't show every extreme that they name: Each length is a multiple of 64. In each group the lengths sum to 512 or less, the rest of the group's slots being padding; in every draw some group has no padding and holds a sequence of the greatest length, and some group has every sequence at the least length.
All inputs are finite; a program needn't handle non-finite values.
Results may differ from a plain program's by a relative error of at most 0.035.
Values may be sent and summed in bfloat16 or wider, within the bound.
No kernel may reach another device: no remote copies, remote signals or barrier semaphores. Data moves between devices by JAX's collectives and lax.ppermute only.
A program may use at most 128 MiB of HBM per device.

v0:
```python
import jax
import jax.numpy as jnp
from jax import lax
from jax.sharding import PartitionSpec as P

DH = 128
CONV = 4
SPAN = 64


epsilon = 1e-06
highest = lax.Precision.HIGHEST


def rms_scale(value, gain):
    return value * lax.rsqrt(jnp.mean(value * value, axis=-1, keepdims=True) + epsilon) * gain


def segment_tables(lengths_row, group_tok):
    offsets = jnp.cumsum(lengths_row) - lengths_row
    total = jnp.sum(lengths_row)
    starts = jnp.concatenate([offsets, total[None]])
    places = jnp.arange(group_tok, dtype=jnp.int32)
    seg_start = jnp.max(jnp.where(starts[None, :] <= places[:, None], starts[None, :], 0), axis=1)
    valid = jnp.stack([places - lag >= seg_start for lag in range(CONV)]).astype(jnp.float32)
    block_first = jnp.arange(group_tok // SPAN, dtype=jnp.int32) * SPAN
    reset = jnp.any(block_first[:, None] == starts[None, :], axis=1).astype(jnp.float32)
    live = (places < total).astype(jnp.float32)
    return (valid, reset, live)


def short_conv(values, weight, valid):
    total = weight[0] * values
    for lag in range(1, CONV):
        moved = jnp.concatenate(
            [jnp.zeros((lag, values.shape[1]), jnp.float32), values[:-lag]], axis=0
        )
        total = total + weight[lag] * moved * valid[lag][:, None]
    return jax.nn.silu(total)


def unit_rows(values, heads):
    shaped = values.reshape(values.shape[0], heads, DH)
    return shaped * lax.rsqrt(jnp.sum(shaped * shaped, axis=-1, keepdims=True) + epsilon)


def delta_block(state, pieces):
    query, key, value, strength, restart = pieces
    state = state * (1.0 - restart)
    inner = jnp.einsum("hid,hjd->hij", key, key, precision=highest)
    lower = jnp.tril(inner * strength[:, :, None], -1)
    system = jnp.eye(SPAN, dtype=jnp.float32)[None] + lower
    right = jnp.concatenate([strength[:, :, None] * key, strength[:, :, None] * value], axis=-1)
    solved = jax.scipy.linalg.solve_triangular(system, right, lower=True, unit_diagonal=True)
    wide = solved[..., :DH]
    plain = solved[..., DH:]
    fresh = plain - jnp.einsum("hcd,hde->hce", wide, state, precision=highest)
    scores = jnp.tril(jnp.einsum("hid,hjd->hij", query, key, precision=highest))
    output = jnp.einsum("hcd,hde->hce", query, state, precision=highest) + jnp.einsum(
        "hij,hje->hie", scores, fresh, precision=highest
    )
    state = state + jnp.einsum("hcd,hce->hde", key, fresh, precision=highest)
    return (state, output)


def mixer(query, key, value, strength, conv_part, valid, reset):
    width = query.shape[1]
    heads = width // DH
    length = query.shape[0]
    query = unit_rows(short_conv(query, conv_part[0], valid), heads)
    key = unit_rows(short_conv(key, conv_part[1], valid), heads)
    value = short_conv(value, conv_part[2], valid).reshape(length, heads, DH)
    blocks = length // SPAN

    def blockify(values):
        return values.reshape(blocks, SPAN, heads, DH).transpose(0, 2, 1, 3)

    gates = strength.reshape(blocks, SPAN, heads).transpose(0, 2, 1)
    initial = jnp.zeros((heads, DH, DH), jnp.float32)
    final_state, outputs = lax.scan(
        jax.checkpoint(delta_block),
        initial,
        (blockify(query), blockify(key), blockify(value), gates, reset),
    )
    return outputs.transpose(0, 2, 1, 3).reshape(length, width)


def swiglu(gate, upper):
    return jax.nn.silu(gate) * upper


def group_rows(values):
    return lax.all_gather(values, "seq", axis=0, tiled=True)


def row_sum(lefts, rights, flipped):
    total = None
    for left, right in zip(lefts, rights):
        if flipped:
            product = jnp.einsum("te,de->td", left, right, preferred_element_type=jnp.float32)
        else:
            product = jnp.dot(left, right, preferred_element_type=jnp.float32)
        total = product if total is None else total + product
    return lax.psum_scatter(total, "seq", scatter_dimension=0, tiled=True)


def shards(
    tokens,
    lengths,
    cotangent,
    attn_norm_gain,
    w_query,
    w_key,
    w_value,
    w_strength,
    conv_weight,
    head_gain,
    w_output,
    ffn_norm_gain,
    w_gate,
    w_up,
    w_down,
):
    local_tok = tokens.shape[0]
    model_width = tokens.shape[1]
    seq_parts = lax.axis_size("seq")
    seq_place = lax.axis_index("seq")
    group_tok = local_tok * seq_parts
    valid, reset, live = segment_tables(lengths[0], group_tok)
    own_live = lax.dynamic_slice_in_dim(live, seq_place * local_tok, local_tok)
    conv_local = conv_weight.astype(jnp.float32)
    head_width = conv_weight.shape[2]
    head_dim = head_gain.shape[0]
    x_float = tokens.astype(jnp.float32)
    hidden_float, first_pull = jax.vjp(rms_scale, x_float, attn_norm_gain.astype(jnp.float32))
    hidden = hidden_float.astype(jnp.bfloat16)
    d_final = cotangent.astype(jnp.float32) * own_live[:, None]
    d_ffo = d_final.astype(jnp.bfloat16)

    def head_norm(values, gain):
        rows = values.shape[0]
        width = values.shape[1]
        return rms_scale(values.reshape(rows, width // head_dim, head_dim), gain).reshape(
            rows, width
        )

    def mixer_local(query_h, key_h, value_h, strength_h, conv_h):
        return mixer(query_h, key_h, value_h, strength_h, conv_h, valid, reset)

    sliced_weights = (
        lax.all_gather(w_query, "dp", axis=0, tiled=True),
        lax.all_gather(w_key, "dp", axis=0, tiled=True),
        lax.all_gather(w_value, "dp", axis=0, tiled=True),
        lax.all_gather(w_strength, "dp", axis=0, tiled=True),
        lax.all_gather(w_output, "dp", axis=1, tiled=True),
        lax.all_gather(w_gate, "dp", axis=0, tiled=True),
        lax.all_gather(w_up, "dp", axis=0, tiled=True),
        lax.all_gather(w_down, "dp", axis=1, tiled=True),
    )
    query_cols, key_cols, value_cols, strength_cols, output_rows, gate_cols, up_cols, down_rows = (
        sliced_weights
    )
    hidden_group = group_rows(hidden)
    query_h = jnp.dot(hidden_group, query_cols, preferred_element_type=jnp.float32).astype(
        jnp.bfloat16
    )
    key_h = jnp.dot(hidden_group, key_cols, preferred_element_type=jnp.float32).astype(jnp.bfloat16)
    value_h = jnp.dot(hidden_group, value_cols, preferred_element_type=jnp.float32).astype(
        jnp.bfloat16
    )
    sigma = jax.nn.sigmoid(jnp.dot(hidden_group, strength_cols, preferred_element_type=jnp.float32))
    strength_h = sigma.astype(jnp.bfloat16)
    mixer_inputs = (
        query_h.astype(jnp.float32),
        key_h.astype(jnp.float32),
        value_h.astype(jnp.float32),
        strength_h.astype(jnp.float32),
        conv_local,
    )
    mixed = mixer_local(
        mixer_inputs[0], mixer_inputs[1], mixer_inputs[2], mixer_inputs[3], mixer_inputs[4]
    )
    mixed_low = mixed.astype(jnp.bfloat16)
    normed_float, head_pull = jax.vjp(
        head_norm, mixed_low.astype(jnp.float32), head_gain.astype(jnp.float32)
    )
    normed = normed_float.astype(jnp.bfloat16)
    resid = x_float + row_sum((normed,), (output_rows,), False)
    second_float, second_pull = jax.vjp(rms_scale, resid, ffn_norm_gain.astype(jnp.float32))
    second = second_float.astype(jnp.bfloat16)
    second_group = group_rows(second)
    gate = jnp.dot(second_group, gate_cols, preferred_element_type=jnp.float32)
    upper = jnp.dot(second_group, up_cols, preferred_element_type=jnp.float32)
    act_float, act_pull = jax.vjp(swiglu, gate, upper)
    act = act_float.astype(jnp.bfloat16)
    final = resid + row_sum((act,), (down_rows,), False)
    d_ffo_group = group_rows(d_ffo)
    grad_down = jnp.einsum("tf,td->fd", act, d_ffo_group, preferred_element_type=jnp.float32)
    d_act = jnp.einsum("td,fd->tf", d_ffo_group, down_rows, preferred_element_type=jnp.float32)
    d_gate_float, d_up_float = act_pull(d_act)
    d_gate = d_gate_float.astype(jnp.bfloat16)
    d_up = d_up_float.astype(jnp.bfloat16)
    grad_gate = jnp.einsum("td,tf->df", second_group, d_gate, preferred_element_type=jnp.float32)
    grad_up = jnp.einsum("td,tf->df", second_group, d_up, preferred_element_type=jnp.float32)
    d_second = row_sum((d_gate, d_up), (gate_cols, up_cols), True)
    d_resid_norm, grad_gain_two = second_pull(d_second)
    d_resid = d_final + d_resid_norm
    d_branch = d_resid.astype(jnp.bfloat16)
    d_branch_group = group_rows(d_branch)
    grad_output = jnp.einsum(
        "td,te->de", normed, d_branch_group, preferred_element_type=jnp.float32
    )
    d_normed = jnp.einsum(
        "te,de->td", d_branch_group, output_rows, preferred_element_type=jnp.float32
    )
    d_mixed_float, grad_head_part = head_pull(d_normed)
    d_mixed = d_mixed_float.astype(jnp.bfloat16)
    output = (final * own_live[:, None]).astype(jnp.bfloat16)
    unused, pull_again = jax.vjp(
        mixer_local,
        mixer_inputs[0],
        mixer_inputs[1],
        mixer_inputs[2],
        mixer_inputs[3],
        mixer_inputs[4],
    )
    mixer_grads = pull_again(d_mixed.astype(jnp.float32))
    d_query_h, d_key_h, d_value_h, d_strength_h, d_conv_h = mixer_grads
    d_query = d_query_h.astype(jnp.bfloat16)
    d_key = d_key_h.astype(jnp.bfloat16)
    d_value = d_value_h.astype(jnp.bfloat16)
    d_strength = d_strength_h.astype(jnp.bfloat16)
    d_logit = (d_strength.astype(jnp.float32) * sigma * (1.0 - sigma)).astype(jnp.bfloat16)
    grad_query = jnp.einsum("td,te->de", hidden_group, d_query, preferred_element_type=jnp.float32)
    grad_key = jnp.einsum("td,te->de", hidden_group, d_key, preferred_element_type=jnp.float32)
    grad_value = jnp.einsum("td,te->de", hidden_group, d_value, preferred_element_type=jnp.float32)
    grad_strength = jnp.einsum(
        "td,th->dh", hidden_group, d_logit, preferred_element_type=jnp.float32
    )
    d_hidden = row_sum(
        (d_query, d_key, d_value, d_logit), (query_cols, key_cols, value_cols, strength_cols), True
    )
    d_x_norm, grad_gain_one = first_pull(d_hidden)
    input_grad = d_resid + d_x_norm
    grads = (
        lax.psum_scatter(
            grad_query.astype(jnp.bfloat16), "dp", scatter_dimension=0, tiled=True
        ).astype(jnp.float32),
        lax.psum_scatter(
            grad_key.astype(jnp.bfloat16), "dp", scatter_dimension=0, tiled=True
        ).astype(jnp.float32),
        lax.psum_scatter(
            grad_value.astype(jnp.bfloat16), "dp", scatter_dimension=0, tiled=True
        ).astype(jnp.float32),
        lax.psum_scatter(
            grad_strength.astype(jnp.bfloat16), "dp", scatter_dimension=0, tiled=True
        ).astype(jnp.float32),
        lax.psum_scatter(
            grad_output.astype(jnp.bfloat16), "dp", scatter_dimension=1, tiled=True
        ).astype(jnp.float32),
        lax.psum_scatter(
            grad_gate.astype(jnp.bfloat16), "dp", scatter_dimension=0, tiled=True
        ).astype(jnp.float32),
        lax.psum_scatter(
            grad_up.astype(jnp.bfloat16), "dp", scatter_dimension=0, tiled=True
        ).astype(jnp.float32),
        lax.psum_scatter(
            grad_down.astype(jnp.bfloat16), "dp", scatter_dimension=1, tiled=True
        ).astype(jnp.float32),
    )
    conv_whole = jnp.zeros((3, CONV, model_width), jnp.float32)
    conv_whole = lax.dynamic_update_slice_in_dim(conv_whole, d_conv_h, seq_place * head_width, 2)
    small = lax.psum((grad_gain_one, grad_gain_two, grad_head_part, conv_whole), ("dp", "seq"))
    conv_grad = lax.dynamic_slice_in_dim(small[3], seq_place * head_width, head_width, 2)
    return (
        output,
        input_grad,
        small[0],
        grads[0],
        grads[1],
        grads[2],
        grads[3],
        conv_grad,
        small[2],
        grads[4],
        small[1],
        grads[5],
        grads[6],
        grads[7],
    )


def solution(mesh):
    placed = (
        P(("dp", "seq"), None),
        P("dp", None),
        P(("dp", "seq"), None),
        P(),
        P("dp", "seq"),
        P("dp", "seq"),
        P("dp", "seq"),
        P("dp", "seq"),
        P(None, None, "seq"),
        P(),
        P("seq", "dp"),
        P(),
        P("dp", "seq"),
        P("dp", "seq"),
        P("seq", "dp"),
    )
    return jax.shard_map(
        shards,
        mesh=mesh,
        in_specs=placed,
        out_specs=(
            P(("dp", "seq"), None),
            P(("dp", "seq"), None),
            P(),
            P("dp", "seq"),
            P("dp", "seq"),
            P("dp", "seq"),
            P("dp", "seq"),
            P(None, None, "seq"),
            P(),
            P("seq", "dp"),
            P(),
            P("dp", "seq"),
            P("dp", "seq"),
            P("seq", "dp"),
        ),
        check_vma=False,
    )
```

profile of v0, /device:TPU:0, one launch (start us, length us, event | category | flops | bytes accessed | tf_op | source)
XLA Modules:
  0.0 1854.5 jit_solution(18328247162261016771)
XLA Ops:
  53.4 27.2 %all-gather.18.cloned.1.call-done = bf16[2048,512]{1,0:T(8,128)(2,1)} async-done(((bf16[256,512]{1,0:T(8,128)(2,1)}), bf16[2048,512]{1,0:T(8,128)(2,1)}) %all-gather.18.cloned.1.call-update) | async-done | bytes 2097168 | tf_op jit(solution)/shard_map/all_gather | solution.py:151
  84.2 26.7 %all-gather.14.cloned.1.call-done = bf16[2048,512]{1,0:T(8,128)(2,1)} async-done(((bf16[256,512]{1,0:T(8,128)(2,1)}), bf16[2048,512]{1,0:T(8,128)(2,1)}) %all-gather.14.cloned.1.call-update) | async-done | bytes 2097168 | tf_op jit(solution)/shard_map/all_gather | solution.py:152
  153.1 234.9 %while.50 = (s32[]{:T(128)}, f32[4,128,128]{2,1,0:T(8,128)S(1)}, bf16[8,4,64,128]{3,2,1,0:T(8,128)(2,1)S(1)}, f32[8]{0:T(128)S(1)}, f32[8,4,64,128]{3,2,1,0:T(8,...) while((s32[]{:T(128)}, f32[4,128,128]{2,1,0:T(8,128)S(1)}, ...), condition=%wide.region_6.8_spmd.clone, body=%wide.region_5.7_spmd.clone.sunk | while | flops 277602368 | bytes 4154013 | solution.py:80
  155.2 19.7 %custom-call.29 = f32[4,1,64,64]{2,3,1,0:T(8,128)S(1)} custom-call(f32[4,1,64,64]{3,2,1,0:T(8,128)S(1)} %fusion.328), custom_call_target="InvertDiagBlocksLowerTriangular" | custom-call | tf_op jit(solution)/shard_map/while/body/eval_jaxpr/checkpoint/jit(_solve_triangular)/vmap()/triangular_solve/custom-call.1 | solution.py:54
  213.9 19.7 %custom-call.29 = f32[4,1,64,64]{2,3,1,0:T(8,128)S(1)} custom-call(f32[4,1,64,64]{3,2,1,0:T(8,128)S(1)} %fusion.328), custom_call_target="InvertDiagBlocksLowerTriangular" | custom-call | tf_op jit(solution)/shard_map/while/body/eval_jaxpr/checkpoint/jit(_solve_triangular)/vmap()/triangular_solve/custom-call.1 | solution.py:54
  243.2 19.7 %custom-call.29 = f32[4,1,64,64]{2,3,1,0:T(8,128)S(1)} custom-call(f32[4,1,64,64]{3,2,1,0:T(8,128)S(1)} %fusion.328), custom_call_target="InvertDiagBlocksLowerTriangular" | custom-call | tf_op jit(solution)/shard_map/while/body/eval_jaxpr/checkpoint/jit(_solve_triangular)/vmap()/triangular_solve/custom-call.1 | solution.py:54
  272.5 19.7 %custom-call.29 = f32[4,1,64,64]{2,3,1,0:T(8,128)S(1)} custom-call(f32[4,1,64,64]{3,2,1,0:T(8,128)S(1)} %fusion.328), custom_call_target="InvertDiagBlocksLowerTriangular" | custom-call | tf_op jit(solution)/shard_map/while/body/eval_jaxpr/checkpoint/jit(_solve_triangular)/vmap()/triangular_solve/custom-call.1 | solution.py:54
  399.1 51.5 %reduce-scatter.15.cloned.1.call-done = f32[128,2048]{1,0:T(8,128)} async-done(((f32[512,2048]{1,0:T(8,128)}), f32[128,2048]{1,0:T(8,128)}) %reduce-scatter.15.cloned.1.call-update) | async-done | bytes 1048592 | tf_op jit(solution)/shard_map/reduce_scatter | solution.py:104
  456.9 55.9 %all-gather.24.cloned.1.call-done = bf16[2048,1408]{1,0:T(8,128)(2,1)} async-done(((bf16[256,1408]{1,0:T(8,128)(2,1)}), bf16[2048,1408]{1,0:T(8,128)(2,1)}) %all-gather.24.cloned.1.call-update) | async-done | bytes 5767184 | tf_op jit(solution)/shard_map/all_gather | solution.py:156
  512.9 36.6 %all-gather.22.cloned.1.call-done = bf16[512,2048]{1,0:T(8,128)(2,1)} async-done(((bf16[128,2048]{1,0:T(8,128)(2,1)}), bf16[512,2048]{1,0:T(8,128)(2,1)}) %all-gather.22.cloned.1.call-update) | async-done | bytes 2097168 | tf_op jit(solution)/shard_map/all_gather | solution.py:93
  557.7 54.0 %all-gather.26.cloned.1.call-done = bf16[2048,1408]{1,0:T(8,128)(2,1)} async-done(((bf16[256,1408]{1,0:T(8,128)(2,1)}), bf16[2048,1408]{1,0:T(8,128)(2,1)}) %all-gather.26.cloned.1.call-update) | async-done | bytes 5767184 | tf_op jit(solution)/shard_map/all_gather | solution.py:157
  619.9 28.2 %all-gather.30.cloned.1.call-done = bf16[512,2048]{1,0:T(8,128)(2,1)} async-done(((bf16[128,2048]{1,0:T(8,128)(2,1)}), bf16[512,2048]{1,0:T(8,128)(2,1)}) %all-gather.30.cloned.1.call-update) | async-done | bytes 2097168 | tf_op jit(solution)/shard_map/all_gather | solution.py:93
  648.1 62.5 %all-gather.28.cloned.1.call-done = bf16[1408,2048]{1,0:T(8,128)(2,1)} async-done(((bf16[1408,256]{1,0:T(8,128)(2,1)}), bf16[1408,2048]{1,0:T(8,128)(2,1)}) %all-gather.28.cloned.1.call-update) | async-done | bytes 5767184 | tf_op jit(solution)/shard_map/all_gather | solution.py:158
  741.9 42.5 %reduce-scatter.19.cloned.1.call-done = f32[128,2048]{1,0:T(8,128)} async-done(((f32[512,2048]{1,0:T(8,128)}), f32[128,2048]{1,0:T(8,128)}) %reduce-scatter.19.cloned.1.call-update) | async-done | bytes 1048592 | tf_op jit(solution)/shard_map/reduce_scatter | solution.py:104
  786.5 53.6 %reduce-scatter.17.cloned.1.call-done = f32[128,2048]{1,0:T(8,128)} async-done(((f32[512,2048]{1,0:T(8,128)}), f32[128,2048]{1,0:T(8,128)}) %reduce-scatter.17.cloned.1.call-update) | async-done | bytes 1048592 | tf_op jit(solution)/shard_map/reduce_scatter | solution.py:104
  863.9 217.6 %while.51 = (s32[]{:T(128)}, f32[4,128,128]{2,1,0:T(8,128)S(1)}, f32[8,4,128,128]{3,2,1,0:T(8,128)}, f32[8]{0:T(128)S(1)}, f32[8,4,64,128]{3,2,1,0:T(8,128)}, /*...) while((s32[]{:T(128)}, f32[4,128,128]{2,1,0:T(8,128)S(1)}, ...), condition=%wide.region_15.17_spmd.clone, body=%wide.region_14.16_spmd.clone.sunk | while | flops 176820288 | bytes 3361437 | solution.py:80
  1107.9 293.0 %while.52 = (s32[]{:T(128)}, f32[4,128,128]{2,1,0:T(8,128)S(1)}, f32[8,4,64,128]{3,2,1,0:T(8,128)}, f32[8,4,64,128]{3,2,1,0:T(8,128)}, f32[8,4,64,128]{3,2,1,0:T...) while((s32[]{:T(128)}, f32[4,128,128]{2,1,0:T(8,128)S(1)}, ...), condition=%wide.region_20.22_spmd.clone, body=%wide.region_16.21_spmd.clone.sunk | while | flops 718692160 | bytes 13050987 | solution.py:80
  1489.4 111.9 %all-reduce.39.cloned.1.call-done = f32[3,4,2048]{2,1,0:T(4,128)} async-done(((f32[3,4,2048]{2,1,0:T(4,128)}), f32[3,4,2048]{2,1,0:T(4,128)}) %all-reduce.39.cloned.1.call-update) | async-done | bytes 98320 | tf_op jit(solution)/shard_map/psum | solution.py:273
  1602.7 37.6 %reduce-scatter.25.cloned.1.call-done = bf16[256,512]{1,0:T(8,128)(2,1)} async-done(((bf16[2048,512]{1,0:T(8,128)(2,1)}), bf16[256,512]{1,0:T(8,128)(2,1)}) %reduce-scatter.25.cloned.1.call-update) | async-done | bytes 262160 | tf_op jit(solution)/shard_map/reduce_scatter | solution.py:249
  1642.0 35.1 %reduce-scatter.23.cloned.1.call-done = bf16[256,512]{1,0:T(8,128)(2,1)} async-done(((bf16[2048,512]{1,0:T(8,128)(2,1)}), bf16[256,512]{1,0:T(8,128)(2,1)}) %reduce-scatter.23.cloned.1.call-update) | async-done | bytes 262160 | tf_op jit(solution)/shard_map/reduce_scatter | solution.py:246
  1678.9 35.0 %reduce-scatter.27.cloned.1.call-done = bf16[256,512]{1,0:T(8,128)(2,1)} async-done(((bf16[2048,512]{1,0:T(8,128)(2,1)}), bf16[256,512]{1,0:T(8,128)(2,1)}) %reduce-scatter.27.cloned.1.call-update) | async-done | bytes 262160 | tf_op jit(solution)/shard_map/reduce_scatter | solution.py:252
  1715.7 35.0 %reduce-scatter.29.cloned.1.call-done = bf16[512,256]{1,0:T(8,128)(2,1)} async-done(((bf16[512,2048]{1,0:T(8,128)(2,1)}), bf16[512,256]{1,0:T(8,128)(2,1)}) %reduce-scatter.29.cloned.1.call-update) | async-done | bytes 262160 | tf_op jit(solution)/shard_map/reduce_scatter | solution.py:258
  1752.5 52.2 %reduce-scatter.21.cloned.1.call-done = f32[128,2048]{1,0:T(8,128)} async-done(((f32[512,2048]{1,0:T(8,128)}), f32[128,2048]{1,0:T(8,128)}) %reduce-scatter.21.cloned.1.call-update) | async-done | bytes 1048592 | tf_op jit(solution)/shard_map/reduce_scatter | solution.py:104
  1806.4 39.8 %all-reduce.36 = (f32[2048]{0:T(1024)}, f32[128]{0:T(128)}, f32[2048]{0:T(1024)}) all-reduce(f32[2048]{0:T(1024)S(1)} %get-tuple-element.666, f32[128]{0:T(128)S(1)} %bitcast_reduce_fusion, f32[2048]{0:T(1024)S(1)} %copy-done.57), channel_id=1, replica_groups=mesh['dp'=8,'seq'=4] {'dp','seq'}, use_global_device_ids=true, to_apply=%region_26.28 | all-reduce | flops 4224 | bytes 33792 | tf_op jit(solution)/shard_map/psum | solution.py:273
  (946 shorter events, 954.9 us)
Async XLA Ops:
  7.2 42.7 %all-gather.12.cloned.1.call-start = ((), (), s32[]{:S(2)}) async-start(), calls=%async_computation.12 | async-start | bytes 2621440 | tf_op jit(solution)/shard_map/all_gather | solution.py:93
  11.7 69.0 %all-gather.18.cloned.1.call-start = ((), (), s32[]{:S(2)}) async-start(), calls=%async_computation.15 | async-start | bytes 2359296 | tf_op jit(solution)/shard_map/all_gather | solution.py:151
  12.5 98.4 %all-gather.14.cloned.1.call-start = ((), (), s32[]{:S(2)}) async-start(), calls=%async_computation.13 | async-start | bytes 2359296 | tf_op jit(solution)/shard_map/all_gather | solution.py:152
  13.2 127.8 %all-gather.16.cloned.1.call-start = ((), (), s32[]{:S(2)}) async-start(), calls=%async_computation.14 | async-start | bytes 2359296 | tf_op jit(solution)/shard_map/all_gather | solution.py:153
  13.8 379.4 %all-gather.20.cloned.1.call-start = ((), (), s32[]{:S(2)}) async-start(), calls=%async_computation.16 | async-start | bytes 2359296 | tf_op jit(solution)/shard_map/all_gather | solution.py:155
  14.4 436.3 %reduce-scatter.15.cloned.1.call-start = ((), (), s32[]{:S(2)}) async-start(), calls=%async_computation.17 | async-start | bytes 5242880 | tf_op jit(solution)/shard_map/reduce_scatter | solution.py:104
  398.3 114.5 %all-gather.24.cloned.1.call-start = ((), (), s32[]{:S(2)}) async-start(), calls=%async_computation.19 | async-start | bytes 6488064 | tf_op jit(solution)/shard_map/all_gather | solution.py:156
  399.1 150.4 %all-gather.22.cloned.1.call-start = ((), (), s32[]{:S(2)}) async-start(), calls=%async_computation.18 | async-start | bytes 2621440 | tf_op jit(solution)/shard_map/all_gather | solution.py:93
  453.3 158.4 %all-gather.26.cloned.1.call-start = ((), (), s32[]{:S(2)}) async-start(), calls=%async_computation.20 | async-start | bytes 6488064 | tf_op jit(solution)/shard_map/all_gather | solution.py:157
  454.0 194.1 %all-gather.30.cloned.1.call-start = ((), (), s32[]{:S(2)}) async-start(), calls=%async_computation.23 | async-start | bytes 2621440 | tf_op jit(solution)/shard_map/all_gather | solution.py:93
  456.1 254.5 %all-gather.28.cloned.1.call-start = ((), (), s32[]{:S(2)}) async-start(), calls=%async_computation.21 | async-start | bytes 6488064 | tf_op jit(solution)/shard_map/all_gather | solution.py:158
  456.9 327.6 %reduce-scatter.19.cloned.1.call-start = ((), (), s32[]{:S(2)}) async-start(), calls=%async_computation.24 | async-start | bytes 5242880 | tf_op jit(solution)/shard_map/reduce_scatter | solution.py:104
  733.4 106.7 %reduce-scatter.17.cloned.1.call-start = ((), (), s32[]{:S(2)}) async-start(), calls=%async_computation.22 | async-start | bytes 5242880 | tf_op jit(solution)/shard_map/reduce_scatter | solution.py:104
  741.9 347.4 %all-gather.32.cloned.1.call-start = ((), (), s32[]{:S(2)}) async-start(), calls=%async_computation.25 | async-start | bytes 2621440 | tf_op jit(solution)/shard_map/all_gather | solution.py:93
  843.6 637.2 %reduce-scatter.31.cloned.1.call-start = ((), (), s32[]{:S(2)}) async-start(), calls=%async_computation.32 | async-start | bytes 6488064 | tf_op jit(solution)/shard_map/reduce_scatter | solution.py:261
  851.7 631.5 %reduce-scatter.33.cloned.1.call-start = ((), (), s32[]{:S(2)}) async-start(), calls=%async_computation.33 | async-start | bytes 6488064 | tf_op jit(solution)/shard_map/reduce_scatter | solution.py:264
  863.9 621.6 %reduce-scatter.35.cloned.1.call-start = ((), (), s32[]{:S(2)}) async-start(), calls=%async_computation.34 | async-start | bytes 6488064 | tf_op jit(solution)/shard_map/reduce_scatter | solution.py:267
  1089.2 398.6 %reduce-scatter.37.cloned.1.call-start = ((), (), s32[]{:S(2)}) async-start(), calls=%async_computation.35 | async-start | bytes 589824
  1445.4 155.9 %all-reduce.39.cloned.1.call-start = ((), (), s32[]{:S(2)}) async-start(), calls=%async_computation.30 | async-start | bytes 196608 | tf_op jit(solution)/shard_map/psum | solution.py:273
  1453.4 186.8 %reduce-scatter.25.cloned.1.call-start = ((), (), s32[]{:S(2)}) async-start(), calls=%async_computation.28 | async-start | bytes 2359296 | tf_op jit(solution)/shard_map/reduce_scatter | solution.py:249
  1457.8 219.3 %reduce-scatter.23.cloned.1.call-start = ((), (), s32[]{:S(2)}) async-start(), calls=%async_computation.27 | async-start | bytes 2359296 | tf_op jit(solution)/shard_map/reduce_scatter | solution.py:246
  1462.0 251.9 %reduce-scatter.27.cloned.1.call-start = ((), (), s32[]{:S(2)}) async-start(), calls=%async_computation.29 | async-start | bytes 2359296 | tf_op jit(solution)/shard_map/reduce_scatter | solution.py:252
  1465.7 285.0 %reduce-scatter.29.cloned.1.call-start = ((), (), s32[]{:S(2)}) async-start(), calls=%async_computation.31 | async-start | bytes 2359296 | tf_op jit(solution)/shard_map/reduce_scatter | solution.py:258
  1471.0 333.7 %reduce-scatter.21.cloned.1.call-start = ((), (), s32[]{:S(2)}) async-start(), calls=%async_computation.26 | async-start | bytes 5242880 | tf_op jit(solution)/shard_map/reduce_scatter | solution.py:104
  (128 other events, 3474.6 us)
Sparse Core Ops, SparseCore 0:
  11.8 38.0 all-gather.11
  51.5 29.1 all-gather.17
  82.3 28.5 all-gather.13
  112.4 28.5 all-gather.15
  142.4 30.5 all-gather.19
  398.4 52.1 reduce-scatter.14
  452.4 60.4 all-gather.23
  515.4 33.9 all-gather.21
  551.2 60.4 all-gather.25
  614.1 33.9 all-gather.29
  649.8 60.8 all-gather.27
  733.5 50.9 reduce-scatter.18
  787.4 52.6 reduce-scatter.16
  843.8 35.3 all-gather.31
  881.4 64.9 reduce-scatter.30
  948.6 63.2 reduce-scatter.32
  1089.3 64.7 reduce-scatter.34
  1445.5 30.8 reduce-scatter.36
  1482.6 118.7 all-reduce.38
  1603.5 36.7 reduce-scatter.24
  1642.5 34.5 reduce-scatter.22
  1679.4 34.4 reduce-scatter.26
  1716.2 34.4 reduce-scatter.28
  1753.6 51.0 reduce-scatter.20
where the time goes:
time: 1860 us; the launch traced here: 1850 us
  waiting for transfers between devices  777 us (42%)
  other arithmetic  591 us (32%)
  matrix products  274 us (15%)
  local copies, waits for them, and re-layouts  121 us (7%)
  blocking collectives  54.2 us (3%)
  loops' own time  19.2 us (1%)
    another operation x96, other arithmetic, delta_block(): jax.scipy.linalg.solve_triangular(system, right, lower=True, unit_diagona...  475 us
    reduce_scatter x4, waiting for transfers between devices, row_sum(): return lax.psum_scatter(total, 'seq', scatter_dimension=0, tiled=True)  200 us
    psum x1, waiting for transfers between devices, shards(): lax.psum((grad_gain_one, grad_gain_two, grad_head_part, conv_whole), ('dp...  112 us
    all_gather x4, waiting for transfers between devices, group_rows(): return lax.all_gather(values, 'seq', axis=0, tiled=True)  83.7 us
    all_gather x1, waiting for transfers between devices, shards(): lax.all_gather(w_down, 'dp', axis=1, tiled=True)  62.5 us
    all_gather x1, waiting for transfers between devices, shards(): lax.all_gather(w_gate, 'dp', axis=0, tiled=True)  55.9 us
    all_gather x1, waiting for transfers between devices, shards(): lax.all_gather(w_up, 'dp', axis=0, tiled=True)  54 us
    psum x1, blocking collectives, shards(): lax.psum((grad_gain_one, grad_gain_two, grad_head_part, conv_whole), ('dp...  39.8 us
  transfers between devices with their start and end apart: 24, of which 18 were waited for; matrix products, arithmetic and copies ran while one was open for 50% of the time, Pallas kernels for 0%

commit v1 on v0

v1 whole, which is shorter than its diff:
```python
import functools

import jax
import jax.numpy as jnp
from jax import lax
from jax.experimental import pallas as pl
from jax.experimental.pallas import tpu as pltpu
from jax.sharding import PartitionSpec as P

DH = 128
CONV = 4
SPAN = 64
HALO = 8
epsilon = 1e-06
f32 = jnp.float32
bf16 = jnp.bfloat16

NN = (((1,), (0,)), ((), ()))
NT = (((1,), (1,)), ((), ()))
TN = (((0,), (0,)), ((), ()))


def mm(left, right, dims=NN):
    return lax.dot_general(left.astype(bf16), right.astype(bf16), dims, preferred_element_type=f32)


def mm3(left, right, dims=NN):
    lh = left.astype(bf16)
    ll = (left - lh.astype(f32)).astype(bf16)
    rh = right.astype(bf16)
    rl = (right - rh.astype(f32)).astype(bf16)
    out = lax.dot_general(ll, rh, dims, preferred_element_type=f32)
    out = out + lax.dot_general(lh, rl, dims, preferred_element_type=f32)
    return out + lax.dot_general(lh, rh, dims, preferred_element_type=f32)


def tri_masks(rows):
    r = lax.broadcasted_iota(jnp.int32, (rows, rows), 0)
    c = lax.broadcasted_iota(jnp.int32, (rows, rows), 1)
    same = (r // SPAN) == (c // SPAN)
    return r, c, same


def unit_lower_inverse(lower, r, c):
    eye = (r == c).astype(f32)
    half = 1
    inverse = eye
    while half < SPAN:
        pair = ((r // (2 * half)) == (c // (2 * half))) & ((r // half) != (c // half))
        corner = jnp.where(pair, lower, 0.0)
        if half == 1:
            inverse = eye - corner
        else:
            inverse = inverse - mm(mm(inverse, corner), inverse)
        half *= 2
    resid = eye - inverse - mm3(lower, inverse)
    return inverse + mm(inverse, resid)


def rolled(block, halo_before, lag):
    if lag == 0:
        return block
    whole = jnp.concatenate([halo_before, block], axis=0)
    return pltpu.roll(whole, lag, 0)[HALO:]


def rolled_back(block, halo_after, lag):
    if lag == 0:
        return block
    whole = jnp.concatenate([block, halo_after], axis=0)
    return pltpu.roll(whole, whole.shape[0] - lag, 0)[: block.shape[0]]


def sigmoid(v):
    return 1.0 / (1.0 + jnp.exp(-v))


def row_start(place_ref, c, per):
    chunk = lax.div(c, per)
    return pl.multiple_of(((chunk ^ place_ref[0]) * per + lax.rem(c, per)) * SPAN, SPAN)


def conv_block(x_ref, conv_ref, start, before, keep, part, head, width):
    cols = pl.ds(part * width + head * DH, DH)
    block = x_ref[pl.ds(start, SPAN), cols].astype(f32)
    halo = x_ref[pl.ds(before, 16), cols].astype(f32)[16 - HALO :] * keep
    shifted = [rolled(block, halo, lag) for lag in range(CONV)]
    taps = [conv_ref[pl.ds(part * CONV + lag, 1), pl.ds(head * DH, DH)] for lag in range(CONV)]
    total = taps[0] * shifted[0]
    for lag in range(1, CONV):
        total = total + taps[lag] * shifted[lag]
    return total, shifted, taps


def strengths(logit_ref, start, heads):
    block = sigmoid(logit_ref[pl.ds(start, SPAN), :]).astype(bf16).astype(f32)
    return jnp.concatenate([block[:, h : h + 1] for h in range(heads)], axis=0)


def fwd_kernel(per, reset_ref, place_ref, x_ref, logit_ref, conv_ref, gain_ref, normed_ref, mixed_ref, t_ref, s_ref, n_ref, q_s, k_s, u_s, w_s, p_s, state):
    length = x_ref.shape[0]
    width = x_ref.shape[1] // 3
    heads = width // DH
    blocks = length // SPAN
    rows = heads * SPAN
    r, c_, same = tri_masks(rows)
    strict = same & (r > c_)
    incl = same & (r >= c_)

    def local(c, carry):
        keep = 1.0 - reset_ref[c]
        start = row_start(place_ref, c, per)
        before = pl.multiple_of(row_start(place_ref, jnp.maximum(c - 1, 0), per) + (SPAN - 16), 16)
        parts = []
        for part in range(3):
            pieces = []
            for h in range(heads):
                z, _, _ = conv_block(x_ref, conv_ref, start, before, keep, part, h, width)
                pieces.append(z)
            z = jnp.concatenate(pieces, axis=0)
            parts.append(z * sigmoid(z))
        q, k, v = parts
        q = q * lax.rsqrt(jnp.sum(q * q, axis=-1, keepdims=True) + epsilon)
        k = k * lax.rsqrt(jnp.sum(k * k, axis=-1, keepdims=True) + epsilon)
        b = strengths(logit_ref, start, heads)
        gram = mm3(k, k, NT)
        lower = jnp.where(strict, gram * b, 0.0)
        inverse = unit_lower_inverse(lower, r, c_)
        p_s[c] = jnp.where(incl, mm(q, k, NT), 0.0).astype(bf16)
        t_ref[c] = inverse.astype(bf16)
        solved = mm(inverse, jnp.concatenate([b * k, b * v], axis=1))
        w_s[c] = solved[:, :DH].astype(bf16)
        u_s[c] = solved[:, DH:]
        q_s[c] = q.astype(bf16)
        k_s[c] = k.astype(bf16)
        return carry

    lax.fori_loop(0, blocks, local, 0)
    state[...] = jnp.zeros_like(state)
    gain = gain_ref[...]

    def scan(c, carry):
        keep = 1.0 - reset_ref[c]
        start = row_start(place_ref, c, per)
        news = []
        reads = []
        for h in range(heads):
            s = state[pl.ds(h * DH, DH), :] * keep
            low = s.astype(bf16)
            s_ref[c, pl.ds(h * DH, DH), :] = low
            both = jnp.concatenate([w_s[c, pl.ds(h * SPAN, SPAN), :], q_s[c, pl.ds(h * SPAN, SPAN), :]], axis=0)
            got = mm(both, low)
            fresh = u_s[c, pl.ds(h * SPAN, SPAN), :] - got[:SPAN]
            state[pl.ds(h * DH, DH), :] = s + mm(k_s[c, pl.ds(h * SPAN, SPAN), :], fresh, TN)
            news.append(fresh)
            reads.append(got[SPAN:])
        fresh = jnp.concatenate(news, axis=0).astype(bf16)
        n_ref[c] = fresh
        out = jnp.concatenate(reads, axis=0) + mm(p_s[c], fresh)
        mixed = out.astype(bf16)
        wide = mixed.astype(f32)
        normed = (wide * lax.rsqrt(jnp.mean(wide * wide, axis=-1, keepdims=True) + epsilon) * gain).astype(bf16)
        for h in range(heads):
            cols = pl.ds(h * DH, DH)
            mixed_ref[pl.ds(start, SPAN), cols] = mixed[h * SPAN : (h + 1) * SPAN]
            normed_ref[pl.ds(start, SPAN), cols] = normed[h * SPAN : (h + 1) * SPAN]
        return carry

    lax.fori_loop(0, blocks, scan, 0)


def delta_forward(per, reset, place, x, logit, conv, gain):
    length = x.shape[0]
    width = x.shape[1] // 3
    heads = width // DH
    blocks = length // SPAN
    rows = heads * SPAN
    shape = jax.ShapeDtypeStruct
    vmem = pl.BlockSpec(memory_space=pltpu.VMEM)
    smem = pl.BlockSpec(memory_space=pltpu.SMEM)
    return pl.pallas_call(
        functools.partial(fwd_kernel, per),
        out_shape=(
            shape((length, width), bf16),
            shape((length, width), bf16),
            shape((blocks, rows, rows), bf16),
            shape((blocks, heads * DH, DH), bf16),
            shape((blocks, rows, DH), bf16),
        ),
        in_specs=[smem, smem] + [vmem] * 4,
        out_specs=(vmem,) * 5,
        scratch_shapes=[
            pltpu.VMEM((blocks, rows, DH), bf16),
            pltpu.VMEM((blocks, rows, DH), bf16),
            pltpu.VMEM((blocks, rows, DH), f32),
            pltpu.VMEM((blocks, rows, DH), bf16),
            pltpu.VMEM((blocks, rows, rows), bf16),
            pltpu.VMEM((heads * DH, DH), f32),
        ],
        name="delta_forward",
    )(reset, place, x, logit, conv, gain)


def bwd_kernel(per, reset_ref, place_ref, x_ref, logit_ref, conv_ref, gain_ref, mixed_ref, dnorm_ref, t_ref, s_ref, n_ref, dx_ref, dlogit_ref, dconv_ref, dgain_ref,
               q_s, k_s, v_s, iq_s, ik_s, do_s, g_s, kt_s, ds_s, dstate):
    length = x_ref.shape[0]
    width = x_ref.shape[1] // 3
    heads = width // DH
    blocks = length // SPAN
    rows = heads * SPAN
    r, c_, same = tri_masks(rows)
    strict = same & (r > c_)
    incl = same & (r >= c_)
    gain = gain_ref[...]

    def stack(ref, start):
        return jnp.concatenate([ref[pl.ds(start, SPAN), pl.ds(h * DH, DH)] for h in range(heads)], axis=0)

    def local(c, total):
        keep = 1.0 - reset_ref[c]
        start = row_start(place_ref, c, per)
        before = pl.multiple_of(row_start(place_ref, jnp.maximum(c - 1, 0), per) + (SPAN - 16), 16)
        parts = []
        for part in range(3):
            pieces = []
            for h in range(heads):
                z, _, _ = conv_block(x_ref, conv_ref, start, before, keep, part, h, width)
                pieces.append(z)
            z = jnp.concatenate(pieces, axis=0)
            parts.append(z * sigmoid(z))
        q, k, v = parts
        iq = lax.rsqrt(jnp.sum(q * q, axis=-1, keepdims=True) + epsilon)
        ik = lax.rsqrt(jnp.sum(k * k, axis=-1, keepdims=True) + epsilon)
        q = q * iq
        k = k * ik
        q_s[c] = q
        k_s[c] = k
        v_s[c] = v
        iq_s[c] = jnp.broadcast_to(iq, (rows, DH))
        ik_s[c] = jnp.broadcast_to(ik, (rows, DH))
        mixed = stack(mixed_ref, start).astype(f32)
        dnorm = stack(dnorm_ref, start)
        inv = lax.rsqrt(jnp.mean(mixed * mixed, axis=-1, keepdims=True) + epsilon)
        u = mixed * inv
        total = total + jnp.sum(dnorm * u, axis=0, keepdims=True)
        dg = dnorm * gain
        do = ((dg - u * jnp.mean(dg * u, axis=-1, keepdims=True)) * inv).astype(bf16)
        do_s[c] = do
        p = jnp.where(incl, mm(q, k, NT), 0.0)
        t = t_ref[c]
        pre = mm(p, do, TN)
        got = mm(t, jnp.concatenate([pre, k], axis=1), TN)
        g_s[c] = got[:, :DH]
        kt_s[c] = got[:, DH:].astype(bf16)
        return total

    dgain_ref[...] = lax.fori_loop(0, blocks, local, jnp.zeros((1, DH), f32))
    dstate[...] = jnp.zeros_like(dstate)

    def scan(i, carry):
        c = blocks - 1 - i
        keep = 1.0 - reset_ref[c]
        start = row_start(place_ref, c, per)
        b = strengths(logit_ref, start, heads)
        k = k_s[c]
        bk = (b * k).astype(bf16)
        for h in range(heads):
            hr = pl.ds(h * SPAN, SPAN)
            ds = dstate[pl.ds(h * DH, DH), :]
            low = ds.astype(bf16)
            ds_s[c, pl.ds(h * DH, DH), :] = low
            g = g_s[c, hr, :] + mm(kt_s[c, hr, :], low)
            g_s[c, hr, :] = g
            ql = q_s[c, hr, :].astype(bf16)
            both = jnp.concatenate([ql, bk[h * SPAN : (h + 1) * SPAN]], axis=0)
            other = jnp.concatenate([do_s[c, hr, :], (-g).astype(bf16)], axis=0)
            dstate[pl.ds(h * DH, DH), :] = (ds + mm(both, other, TN)) * keep
        return carry

    lax.fori_loop(0, blocks, scan, 0)
    dconv_ref[...] = jnp.zeros_like(dconv_ref)
    lane = lax.broadcasted_iota(jnp.int32, (SPAN, heads), 1)

    def last(i, carry):
        c = blocks - 1 - i
        keep = 1.0 - reset_ref[c]
        start = row_start(place_ref, c, per)
        before = pl.multiple_of(row_start(place_ref, jnp.maximum(c - 1, 0), per) + (SPAN - 16), 16)
        b = strengths(logit_ref, start, heads)
        q, k, v = q_s[c], k_s[c], v_s[c]
        g, n, do = g_s[c], n_ref[c], do_s[c]
        gl = g.astype(bf16)
        both = jnp.concatenate([do, gl], axis=0)
        outer = mm(both, n, NT)
        dp = jnp.where(incl, outer[:rows], 0.0).astype(bf16)
        da = jnp.where(strict, -outer[rows:], 0.0).astype(bf16)
        down = mm(jnp.concatenate([dp, da], axis=0), k)
        up = mm(jnp.concatenate([dp, da], axis=0), jnp.concatenate([q, b * k], axis=0), TN)
        sides = []
        nds = []
        for h in range(heads):
            s = s_ref[c, pl.ds(h * DH, DH), :]
            hr = slice(h * SPAN, (h + 1) * SPAN)
            sides.append(mm(jnp.concatenate([do[hr], gl[hr]], axis=0), s, NT))
            nds.append(mm(n[hr], ds_s[c, pl.ds(h * DH, DH), :], NT))
        dos = jnp.concatenate([x[:SPAN] for x in sides], axis=0)
        gs = jnp.concatenate([x[SPAN:] for x in sides], axis=0)
        dq = dos + down[:rows]
        y = down[rows:] - gs
        dk = up + jnp.concatenate(nds, axis=0) + b * y
        dv = b * g
        db = jnp.sum(k * y + v * g, axis=-1, keepdims=True)
        dq = (dq - q * jnp.sum(q * dq, axis=-1, keepdims=True)) * iq_s[c]
        dk = (dk - k * jnp.sum(k * dk, axis=-1, keepdims=True)) * ik_s[c]
        row = jnp.zeros((SPAN, heads), f32)
        for h in range(heads):
            row = jnp.where(lane == h, db[h * SPAN : (h + 1) * SPAN], row)
        sg = sigmoid(logit_ref[pl.ds(start, SPAN), :])
        dlogit_ref[pl.ds(start, SPAN), :] = (row.astype(bf16).astype(f32) * sg * (1.0 - sg)).astype(bf16)
        new_carry = []
        for part, grad in enumerate((dq, dk, dv)):
            for h in range(heads):
                z, shifted, taps = conv_block(x_ref, conv_ref, start, before, keep, part, h, width)
                sz = sigmoid(z)
                dz = grad[h * SPAN : (h + 1) * SPAN] * (sz * (1.0 + z * (1.0 - sz)))
                after = carry[part * heads + h]
                total = taps[0] * dz
                for lag in range(1, CONV):
                    total = total + taps[lag] * rolled_back(dz, after, lag)
                dx_ref[pl.ds(start, SPAN), pl.ds(part * width + h * DH, DH)] = total.astype(bf16)
                for lag in range(CONV):
                    at = pl.ds(part * CONV + lag, 1), pl.ds(h * DH, DH)
                    dconv_ref[at] = dconv_ref[at] + jnp.sum(dz * shifted[lag], axis=0, keepdims=True)
                new_carry.append(dz[:HALO] * keep)
        return tuple(new_carry)

    zero = jnp.zeros((HALO, DH), f32)
    lax.fori_loop(0, blocks, last, (zero,) * (3 * heads))


def delta_backward(per, reset, place, x, logit, conv, gain, mixed, dnorm, t, s, n):
    length = x.shape[0]
    width = x.shape[1] // 3
    heads = width // DH
    blocks = length // SPAN
    rows = heads * SPAN
    shape = jax.ShapeDtypeStruct
    vmem = pl.BlockSpec(memory_space=pltpu.VMEM)
    smem = pl.BlockSpec(memory_space=pltpu.SMEM)
    return pl.pallas_call(
        functools.partial(bwd_kernel, per),
        out_shape=(
            shape((length, 3 * width), bf16),
            shape((length, heads), bf16),
            shape((3 * CONV, width), f32),
            shape((1, DH), f32),
        ),
        in_specs=[smem, smem] + [vmem] * 9,
        out_specs=(vmem,) * 4,
        scratch_shapes=[pltpu.VMEM((blocks, rows, DH), f32)] * 5
        + [
            pltpu.VMEM((blocks, rows, DH), bf16),
            pltpu.VMEM((blocks, rows, DH), f32),
            pltpu.VMEM((blocks, rows, DH), bf16),
            pltpu.VMEM((blocks, heads * DH, DH), bf16),
            pltpu.VMEM((heads * DH, DH), f32),
        ],
        name="delta_backward",
    )(reset, place, x, logit, conv, gain, mixed, dnorm, t, s, n)


def rms_scale(value, gain):
    return value * lax.rsqrt(jnp.mean(value * value, axis=-1, keepdims=True) + epsilon) * gain


def segment_tables(lengths_row, group_tok):
    offsets = jnp.cumsum(lengths_row) - lengths_row
    total = jnp.sum(lengths_row)
    starts = jnp.concatenate([offsets, total[None]])
    block_first = jnp.arange(group_tok // SPAN, dtype=jnp.int32) * SPAN
    reset = jnp.any(block_first[:, None] == starts[None, :], axis=1).astype(f32)
    live = (jnp.arange(group_tok, dtype=jnp.int32) < total).astype(f32)
    return reset, live


def swap(values, axis, mask):
    size = lax.axis_size(axis)
    return lax.ppermute(values, axis, [(i, i ^ mask) for i in range(size)])


def group_rows(values):
    size = lax.axis_size("seq")
    return jnp.concatenate([values] + [swap(values, "seq", k) for k in range(1, size)], axis=0)


def dot(left, right, dims, kind=f32):
    return lax.dot_general(left, right, dims, preferred_element_type=f32).astype(kind)


def row_sum(left, right, dims, local):
    size = lax.axis_size("seq")
    others = dot(left[local:], right, dims, bf16)
    sent = [
        swap(others[(k - 1) * local : k * local], "seq", k) for k in range(1, size)
    ]
    total = dot(left[:local], right, dims)
    for piece in sent:
        total = total + piece.astype(f32)
    return total


def doubled(values, axis):
    size = lax.axis_size(axis)
    mask = 1
    while mask < size:
        values = values + swap(values, axis, mask)
        mask *= 2
    return values


def gathered(values):
    return lax.all_gather(values, "dp", axis=0, tiled=True)


def scattered(values):
    return lax.psum_scatter(values, "dp", scatter_dimension=0, tiled=True)


def shards(
    tokens,
    lengths,
    cotangent,
    attn_norm_gain,
    w_query,
    w_key,
    w_value,
    w_strength,
    conv_weight,
    head_gain,
    w_output,
    ffn_norm_gain,
    w_gate,
    w_up,
    w_down,
):
    local = tokens.shape[0]
    model = tokens.shape[1]
    seq_parts = lax.axis_size("seq")
    seq_place = lax.axis_index("seq")
    dp_parts = lax.axis_size("dp")
    dp_place = lax.axis_index("dp")
    group_tok = local * seq_parts
    width = w_query.shape[1]
    heads = w_strength.shape[1]
    hidden_units = w_gate.shape[1]
    depth = w_query.shape[0]
    per = local // SPAN

    wide_qkv = gathered(jnp.concatenate([w_query, w_key, w_value], axis=1))
    second_set = gathered(jnp.concatenate([w_output.T, w_gate, w_up], axis=1))
    wide_out = second_set[:, :width]
    wide_gu = second_set[:, width:]
    wide_down = gathered(w_down.T)

    strength = w_strength.T
    strengths_all = strength
    mask = 1
    while mask < dp_parts:
        other = swap(strengths_all, "dp", mask)
        low = (dp_place & mask) == 0
        first = jnp.where(low, strengths_all, other)
        last = jnp.where(low, other, strengths_all)
        strengths_all = jnp.concatenate([first, last], axis=1)
        mask *= 2

    reset, live = segment_tables(lengths[0], group_tok)
    own_live = lax.dynamic_slice_in_dim(live, seq_place * local, local)
    place = jnp.full((1,), seq_place, jnp.int32)
    taps = conv_weight.astype(f32).reshape(3 * CONV, width)
    gain_h = head_gain.astype(f32)[None]
    x_float = tokens.astype(f32)
    hidden_float, first_pull = jax.vjp(rms_scale, x_float, attn_norm_gain.astype(f32))
    d_final = cotangent.astype(f32) * own_live[:, None]
    hidden = group_rows(hidden_float.astype(bf16))
    d_ffo = group_rows(d_final.astype(bf16))

    x_mix = dot(hidden, wide_qkv, NN, bf16)
    logit = dot(hidden, strengths_all, NT)
    normed, mixed, kept_t, kept_s, kept_n = delta_forward(per, reset, place, x_mix, logit, taps, gain_h)
    resid = x_float + row_sum(normed, wide_out, NT, local)
    second_float, second_pull = jax.vjp(rms_scale, resid, ffn_norm_gain.astype(f32))
    second = group_rows(second_float.astype(bf16))
    gate_up = dot(second, wide_gu, NN)
    gate = gate_up[:, :hidden_units]
    upper = gate_up[:, hidden_units:]
    sg = jax.nn.sigmoid(gate)
    act = (gate * sg * upper).astype(bf16)
    grad_down = scattered(dot(d_ffo, act, TN, bf16)).astype(f32).T
    d_act = dot(d_ffo, wide_down, NN)
    d_gate = (d_act * upper * (sg * (1.0 + gate * (1.0 - sg)))).astype(bf16)
    d_up = (d_act * gate * sg).astype(bf16)
    d_gu = jnp.concatenate([d_gate, d_up], axis=1)
    d_second = row_sum(d_gu, wide_gu, NT, local)
    grad_gu = scattered(dot(second, d_gu, TN, bf16)).astype(f32)
    final = resid + row_sum(act, wide_down, NT, local)
    output = (final * own_live[:, None]).astype(bf16)
    d_resid_norm, grad_gain_two = second_pull(d_second)
    d_resid = d_final + d_resid_norm
    d_branch = group_rows(d_resid.astype(bf16))
    d_normed = dot(d_branch, wide_out, NN)
    grad_out = scattered(dot(d_branch, normed, TN, bf16)).astype(f32).T
    d_mix, d_logit, d_taps, grad_head = delta_backward(
        per, reset, place, x_mix, logit, taps, gain_h, mixed, d_normed, kept_t, kept_s, kept_n
    )
    grad_qkv = scattered(dot(hidden, d_mix, TN, bf16)).astype(f32)
    grad_strength = dot(d_logit, hidden, TN)
    others = dot(d_mix[local:], wide_qkv, NT) + dot(d_logit[local:], strengths_all, NN)
    others = others.astype(bf16)
    sent = [swap(others[(k - 1) * local : k * local], "seq", k) for k in range(1, seq_parts)]
    d_hidden = dot(d_mix[:local], wide_qkv, NT) + dot(d_logit[:local], strengths_all, NN)
    for piece in sent:
        d_hidden = d_hidden + piece.astype(f32)
    d_x_norm, grad_gain_one = first_pull(d_hidden)
    input_grad = d_resid + d_x_norm

    early = doubled(
        jnp.concatenate([d_taps.reshape(-1), grad_strength.reshape(-1)]).reshape(-1, DH), "dp"
    ).reshape(-1)
    conv_grad = early[: 3 * CONV * width].reshape(3, CONV, width)
    strength_sum = early[3 * CONV * width :].reshape(heads, model)
    strength_grad = lax.dynamic_slice_in_dim(strength_sum, dp_place * depth, depth, 1).T
    gains = jnp.concatenate([grad_gain_one, grad_gain_two, grad_head[0]]).reshape(-1, DH)
    gains = doubled(doubled(gains, "dp"), "seq").reshape(-1)
    return (
        output,
        input_grad,
        gains[:model],
        grad_qkv[:, :width],
        grad_qkv[:, width : 2 * width],
        grad_qkv[:, 2 * width :],
        strength_grad,
        conv_grad,
        gains[2 * model :],
        grad_out,
        gains[model : 2 * model],
        grad_gu[:, :hidden_units],
        grad_gu[:, hidden_units:],
        grad_down,
    )


def solution(mesh):
    placed = (
        P(("dp", "seq"), None),
        P("dp", None),
        P(("dp", "seq"), None),
        P(),
        P("dp", "seq"),
        P("dp", "seq"),
        P("dp", "seq"),
        P("dp", "seq"),
        P(None, None, "seq"),
        P(),
        P("seq", "dp"),
        P(),
        P("dp", "seq"),
        P("dp", "seq"),
        P("seq", "dp"),
    )
    return jax.shard_map(
        shards,
        mesh=mesh,
        in_specs=placed,
        out_specs=(
            P(("dp", "seq"), None),
            P(("dp", "seq"), None),
            P(),
            P("dp", "seq"),
            P("dp", "seq"),
            P("dp", "seq"),
            P("dp", "seq"),
            P(None, None, "seq"),
            P(),
            P("seq", "dp"),
            P(),
            P("dp", "seq"),
            P("dp", "seq"),
            P("seq", "dp"),
        ),
        check_vma=False,
    )
```

time: 1860 us -> 679 us (0.37)
  other arithmetic: 591 us -> 10.6 us
  waiting for transfers between devices: 777 us -> 421 us
  matrix products: 274 us -> 109 us
  local copies, waits for them, and re-layouts: 121 us -> 17.9 us
  blocking collectives: 54.2 us -> 0 us
  Pallas kernels: 0 us -> 50.5 us
  starting transfers between devices: 1.32 us -> 45.1 us
  loops' own time: 19.2 us -> 0 us
    another operation x104 -> x0, other arithmetic: 475 us -> none  [the longest x96 475 us: delta_block(): jax.scipy.linalg.solve_triangular(system, right, lower=True, unit_diagona...]
    reduce_scatter x11 -> x4, waiting for transfers between devices: 342 us -> 144 us  [scattered(): return lax.psum_scatter(values, 'dp', scatter_dimension=0, tiled=True)]
    all_gather x11 -> x3, waiting for transfers between devices: 318 us -> 125 us  [gathered(): return lax.all_gather(values, 'dp', axis=0, tiled=True)]
    ppermute x0 -> x35, waiting for transfers between devices: none -> 151 us  [swap(): return lax.ppermute(values, axis, [(i, i ^ mask) for i in range(size)])]
    dot_general x224 -> x20, matrix products: 258 us -> 109 us  [dot(): lax.dot_general(left, right, dims, preferred_element_type=f32).astype(kind)]
    psum x1 -> x0, waiting for transfers between devices: 112 us -> none  [shards(): lax.psum((grad_gain_one, grad_gain_two, grad_head_part, conv_whole), ('dp...]
    pallas_call x0 -> x2, Pallas kernels: none -> 50.5 us  [the longest x1 27.4 us: delta_forward(): pl.pallas_call(functools.partial(fwd_kernel, per), out_shape=(shape((leng...]
    ppermute x0 -> x35, starting transfers between devices: none -> 44.4 us  [swap(): return lax.ppermute(values, axis, [(i, i ^ mask) for i in range(size)])]
  transfers between devices with their start and end apart: 24 -> 42, of which waited for: 18 -> 29; matrix products, arithmetic and copies ran while one was open for 50% -> 15% of each run, Pallas kernels for 0% -> 8%
where the time goes in v1:
time: 679 us; the launch traced here: 670 us
  waiting for transfers between devices  421 us (62%)
  matrix products  109 us (16%)
  Pallas kernels  50.5 us (7%)
  starting transfers between devices  45.1 us (7%)
  local copies, waits for them, and re-layouts  17.9 us (3%)
  between operations  15.9 us (2%)
  other arithmetic  10.6 us (2%)
    ppermute x35, waiting for transfers between devices, swap(): return lax.ppermute(values, axis, [(i, i ^ mask) for i in range(size)])  151 us
    reduce_scatter x4, waiting for transfers between devices, scattered(): return lax.psum_scatter(values, 'dp', scatter_dimension=0, tiled=True)  144 us
    all_gather x3, waiting for transfers between devices, gathered(): return lax.all_gather(values, 'dp', axis=0, tiled=True)  125 us
    dot_general x20, matrix products, dot(): lax.dot_general(left, right, dims, preferred_element_type=f32).astype(kind)  109 us
    ppermute x35, starting transfers between devices, swap(): return lax.ppermute(values, axis, [(i, i ^ mask) for i in range(size)])  44.4 us
    pallas_call x1, Pallas kernels, delta_forward(): pl.pallas_call(functools.partial(fwd_kernel, per), out_shape=(shape((leng...  27.4 us
    pallas_call x1, Pallas kernels, delta_backward(): pl.pallas_call(functools.partial(bwd_kernel, per), out_shape=(shape((leng...  23 us
  transfers between devices with their start and end apart: 42, of which 29 were waited for; matrix products, arithmetic and copies ran while one was open for 15% of the time, Pallas kernels for 8%

profile of v1, /device:TPU:0, one launch (start us, length us, event | category | flops | bytes accessed | tf_op | source)
XLA Modules:
  0.0 670.3 jit_solution(736115263036115459)
XLA Ops:
  30.0 10.4 %collective-permute-done.1 = bf16[128,2048]{1,0:T(8,128)(2,1)S(1)} collective-permute-done((bf16[128,2048]{1,0:T(8,128)(2,1)S(1)}, bf16[128,2048]{1,0:T(8,128)(2,1)S(1)}, u32[]{:S(2)}, u32[]{:S(2)}) %collective-permute-start.1) | collective-permute-done | bytes 524320 | tf_op jit(solution)/shard_map/ppermute | solution.py:388
  42.0 36.0 %all-gather.4.cloned.1.call-done = bf16[2048,1536]{1,0:T(8,128)(2,1)} async-done(((bf16[256,1536]{1,0:T(8,128)(2,1)}), bf16[2048,1536]{1,0:T(8,128)(2,1)}) %all-gather.4.cloned.1.call-update) | async-done | bytes 6291472 | tf_op jit(solution)/shard_map/all_gather | solution.py:422
  78.1 8.9 %convolution_convert_fusion.4.x_ref = bf16[512,1536]{1,0:T(8,128)(2,1)} fusion(bf16[2048,1536]{1,0:T(8,128)(2,1)} %all-gather.4.cloned.1.call-done, bf16[128,2048]{1,0:T(8,128)(2,1)S(1)} %collective-permute-done.2, bf16[128,2048]{1,0:T(8,128)(2,1)S(1)} %collective-permute-done.1, bf16[128,2048]{1,0:T(8,128)(2,1)S(1)} %collective-permute-done, ...), kind=kOutput, calls=%fused_computation.11 | convolution fusion | flops 3230400512 | bytes 9961472 | tf_op jit(solution)/shard_map/dot_general | solution.py:397
  87.0 27.4 %delta_forward.1 = (bf16[512,512]{1,0:T(8,128)(2,1)}, bf16[512,512]{1,0:T(8,128)(2,1)}, bf16[8,256,256]{2,1,0:T(8,128)(2,1)}, bf16[8,512,128]{2,1,0:T(8,128)(2,1)}, bf16[8,256,128]{2,1,0:T(8,128)(2,1)}) custom-call(f32[8]{0:T(128)} %convert_element_type.116.reset_ref, s32[1]{0:T(128)} %bitcast.1.place_ref, ...), custom_call_target="tpu_custom_call" | custom-call | tf_op jit(solution)/shard_map/delta_forward/pallas_call | solution.py:181
  114.5 89.2 %all-gather.6.cloned.1.call-done = bf16[2048,3328]{1,0:T(8,128)(2,1)} async-done(((bf16[256,3328]{1,0:T(8,128)(2,1)}), bf16[2048,3328]{1,0:T(8,128)(2,1)}) %all-gather.6.cloned.1.call-update) | async-done | bytes 13631504 | tf_op jit(solution)/shard_map/all_gather | solution.py:422
  210.1 11.3 %collective-permute-done.6 = bf16[128,2048]{1,0:T(8,128)(2,1)S(1)} collective-permute-done((bf16[128,2048]{1,0:T(8,128)(2,1)S(1)}, bf16[128,2048]{1,0:T(8,128)(2,1)S(1)}, u32[]{:S(2)}, u32[]{:S(2)}) %collective-permute-start.6) | collective-permute-done | bytes 524320 | tf_op jit(solution)/shard_map/ppermute | solution.py:388
  221.3 11.6 %collective-permute-done.8 = bf16[128,2048]{1,0:T(8,128)(2,1)S(1)} collective-permute-done((bf16[128,2048]{1,0:T(8,128)(2,1)S(1)}, bf16[128,2048]{1,0:T(8,128)(2,1)S(1)}, u32[]{:S(2)}, u32[]{:S(2)}) %collective-permute-start.8) | collective-permute-done | bytes 524320 | tf_op jit(solution)/shard_map/ppermute | solution.py:388
  244.0 9.1 %collective-permute-done.11 = bf16[128,2048]{1,0:T(8,128)(2,1)} collective-permute-done((bf16[128,2048]{1,0:T(8,128)(2,1)S(1)}, bf16[128,2048]{1,0:T(8,128)(2,1)}, u32[]{:S(2)}, u32[]{:S(2)}) %collective-permute-start.11) | collective-permute-done | bytes 524320 | tf_op jit(solution)/shard_map/ppermute | solution.py:388
  254.6 9.8 %collective-permute-done.10 = bf16[128,2048]{1,0:T(8,128)(2,1)} collective-permute-done((bf16[128,2048]{1,0:T(8,128)(2,1)S(1)}, bf16[128,2048]{1,0:T(8,128)(2,1)}, u32[]{:S(2)}, u32[]{:S(2)}) %collective-permute-start.10) | collective-permute-done | bytes 524320 | tf_op jit(solution)/shard_map/ppermute | solution.py:388
  264.4 11.7 %fusion.4 = f32[512,2816]{1,0:T(8,128)} fusion(bf16[2048,3328]{1,0:T(8,128)(2,1)} %all-gather.6.cloned.1.call-done, bf16[128,2048]{1,0:T(8,128)(2,1)} %collective-permute-done.11, bf16[128,2048]{1,0:T(8,128)(2,1)} %collective-permute-done.10, bf16[128,2048]{1,0:T(8,128)(2,1)} %collective-permute-done.9, bf16[128,2048]{1,0:T(8,128)(2,1)S(1)} %multiply_convert_fusion.4), kind=kOutput, calls=%fused_computation.5 | convolution fusion | flops 5913968640 | bytes 19398656 | tf_op jit(solution)/shard_map/dot_general | solution.py:397
  276.2 8.5 %collective-permute-done.16 = bf16[128,2048]{1,0:T(8,128)(2,1)S(1)} collective-permute-done((bf16[128,2048]{1,0:T(8,128)(2,1)S(1)}, bf16[128,2048]{1,0:T(8,128)(2,1)S(1)}, u32[]{:S(2)}, u32[]{:S(2)}) %collective-permute-start.16) | collective-permute-done | bytes 524320 | tf_op jit(solution)/shard_map/ppermute | solution.py:388
  285.4 10.2 %multiply_convert_fusion.1 = (bf16[512,1408]{1,0:T(8,128)(2,1)S(1)}, bf16[512,1408]{1,0:T(8,128)(2,1)S(1)}, bf16[512,1408]{1,0:T(8,128)(2,1)}) fusion(f32[512,2816]{1,0:T(8,128)} %fusion.4, bf16[2048,1408]{0,1:T(8,128)(2,1)} %all-gather.8.cloned.1.call-done, bf16[128,2048]{1,0:T(8,128)(2,1)} %copy-done.26, bf16[128,2048]{1,0:T(8,128)(2,1)} %copy-done.27, ...), kind=kOutput, calls=%fused_computation.16 | convolution fusion | flops 2972712960 | bytes 17956864 | tf_op jit(solution)/shard_map/dot_general | solution.py:397
  295.6 10.0 %fusion.9 = bf16[384,2048]{1,0:T(8,128)(2,1)S(1)} fusion(bf16[2048,3328]{1,0:T(8,128)(2,1)} %all-gather.6.cloned.1.call-done, bf16[512,1408]{1,0:T(8,128)(2,1)S(1)} %get-tuple-element.67, bf16[512,1408]{1,0:T(8,128)(2,1)S(1)} %get-tuple-element.66), kind=kOutput, calls=%fused_computation.19 | convolution fusion | flops 4434296832 | bytes 15990784 | tf_op jit(solution)/shard_map/dot_general | solution.py:397
  309.4 11.3 %collective-permute-done.18 = bf16[128,2048]{1,0:T(8,128)(2,1)S(1)} collective-permute-done((bf16[128,2048]{1,0:T(8,128)(2,1)S(1)}, bf16[128,2048]{1,0:T(8,128)(2,1)S(1)}, u32[]{:S(2)}, u32[]{:S(2)}) %collective-permute-start.18) | collective-permute-done | bytes 524320 | tf_op jit(solution)/shard_map/ppermute | solution.py:388
  320.7 10.5 %collective-permute-done.20 = bf16[128,2048]{1,0:T(8,128)(2,1)S(1)} collective-permute-done((bf16[128,2048]{1,0:T(8,128)(2,1)S(1)}, bf16[128,2048]{1,0:T(8,128)(2,1)S(1)}, u32[]{:S(2)}, u32[]{:S(2)}) %collective-permute-start.20) | collective-permute-done | bytes 524320 | tf_op jit(solution)/shard_map/ppermute | solution.py:388
  343.5 12.3 %collective-permute-done.23 = bf16[128,2048]{1,0:T(8,128)(2,1)S(1)} collective-permute-done((bf16[128,2048]{1,0:T(8,128)(2,1)S(1)}, bf16[128,2048]{1,0:T(8,128)(2,1)S(1)}, u32[]{:S(2)}, u32[]{:S(2)}) %collective-permute-start.23) | collective-permute-done | bytes 524320 | tf_op jit(solution)/shard_map/ppermute | solution.py:388
  355.8 8.1 %collective-permute-done.22 = bf16[128,2048]{1,0:T(8,128)(2,1)S(1)} collective-permute-done((bf16[128,2048]{1,0:T(8,128)(2,1)S(1)}, bf16[128,2048]{1,0:T(8,128)(2,1)S(1)}, u32[]{:S(2)}, u32[]{:S(2)}) %collective-permute-start.22) | collective-permute-done | bytes 524320 | tf_op jit(solution)/shard_map/ppermute | solution.py:388
  381.6 23.0 %delta_backward.1 = (bf16[512,1536]{1,0:T(8,128)(2,1)}, bf16[512,4]{1,0:T(8,128)(2,1)}, f32[12,512]{1,0:T(8,128)}, f32[1,128]{1,0:T(1,128)}) custom-call(f32[8]{0:T(128)} %convert_element_type.116.reset_ref, s32[1]{0:T(128)} %bitcast.1.place_ref, bf16[512,1536]{1,0:T(8,128)(2,1)} %convolution_convert_fusion.4.x_ref, f32[512,4]{1,0:T(8,128)} %fusion.69.logit_ref, ...), custom_call_target="tpu_custom_call" | custom-call | tf_op jit(solution)/shard_map/delta_backward/pallas_call | solution.py:350
  413.7 11.0 %convolution_convert_fusion = bf16[2048,2816]{1,0:T(8,128)(2,1)} fusion(bf16[512,1408]{1,0:T(8,128)(2,1)} %copy-done.33, bf16[512,1408]{1,0:T(8,128)(2,1)} %copy-done.32, bf16[128,2048]{1,0:T(8,128)(2,1)} %collective-permute-done.11, bf16[128,2048]{1,0:T(8,128)(2,1)} %collective-permute-done.10, bf16[128,2048]{1,0:T(8,128)(2,1)} %collective-permute-done.9, ...), kind=kOutput, calls=%fused_computation | convolution fusion | flops 5925502976 | bytes 16515072 | tf_op jit(solution)/shard_map/dot_general | solution.py:397
  448.6 9.2 %collective-permute-done.24 = bf16[128,2048]{1,0:T(8,128)(2,1)S(1)} collective-permute-done((bf16[128,2048]{1,0:T(8,128)(2,1)S(1)}, bf16[128,2048]{1,0:T(8,128)(2,1)S(1)}, u32[]{:S(2)}, u32[]{:S(2)}) %collective-permute-start.24) | collective-permute-done | bytes 524320 | tf_op jit(solution)/shard_map/ppermute | solution.py:388
  459.1 10.8 %collective-permute-done.26 = bf16[128,2048]{1,0:T(8,128)(2,1)S(1)} collective-permute-done((bf16[128,2048]{1,0:T(8,128)(2,1)S(1)}, bf16[128,2048]{1,0:T(8,128)(2,1)S(1)}, u32[]{:S(2)}, u32[]{:S(2)}) %collective-permute-start.26) | collective-permute-done | bytes 524320 | tf_op jit(solution)/shard_map/ppermute | solution.py:388
  480.2 11.1 %collective-permute-done.13 = bf16[128,2048]{1,0:T(8,128)(2,1)S(1)} collective-permute-done((bf16[128,2048]{1,0:T(8,128)(2,1)S(1)}, bf16[128,2048]{1,0:T(8,128)(2,1)S(1)}, u32[]{:S(2)}, u32[]{:S(2)}) %collective-permute-start.13) | collective-permute-done | bytes 524320 | tf_op jit(solution)/shard_map/ppermute | solution.py:388
  513.7 25.9 %reduce-scatter.5.cloned.1.call-done = bf16[256,1536]{1,0:T(8,128)(2,1)} async-done(((bf16[2048,1536]{1,0:T(8,128)(2,1)}), bf16[256,1536]{1,0:T(8,128)(2,1)}) %reduce-scatter.5.cloned.1.call-update) | async-done | bytes 786448 | tf_op jit(solution)/shard_map/reduce_scatter | solution.py:426
  541.9 118.0 %reduce-scatter.9.cloned.1.call-done = bf16[256,2816]{1,0:T(8,128)(2,1)} async-done(((bf16[2048,2816]{1,0:T(8,128)(2,1)}), bf16[256,2816]{1,0:T(8,128)(2,1)}) %reduce-scatter.9.cloned.1.call-update) | async-done | bytes 1441808 | tf_op jit(solution)/shard_map/reduce_scatter | solution.py:426
  (224 shorter events, 149.2 us)
Async XLA Ops:
  7.2 70.9 %all-gather.4.cloned.1.call-start = ((), (), s32[]{:S(2)}) async-start(), calls=%async_computation.4 | async-start | bytes 7077888 | tf_op jit(solution)/shard_map/all_gather | solution.py:422
  9.4 194.2 %all-gather.6.cloned.1.call-start = ((), (), s32[]{:S(2)}) async-start(), calls=%async_computation.5 | async-start | bytes 15335424 | tf_op jit(solution)/shard_map/all_gather | solution.py:422
  12.0 273.4 %all-gather.8.cloned.1.call-start = ((), (), s32[]{:S(2)}) async-start(), calls=%async_computation.6 | async-start | bytes 6488064 | tf_op jit(solution)/shard_map/all_gather | solution.py:422
  12.7 496.2 %reduce-scatter.7.cloned.1.call-start = ((), (), s32[]{:S(2)}) async-start(), calls=%async_computation.8 | async-start | bytes 2359296 | tf_op jit(solution)/shard_map/reduce_scatter | solution.py:426
  17.2 23.2 %collective-permute-start.1 = (bf16[128,2048]{1,0:T(8,128)(2,1)S(1)}, bf16[128,2048]{1,0:T(8,128)(2,1)S(1)}, u32[]{:S(2)}, u32[]{:S(2)}) collective-permute-start(bf16[128,2048]{1,0:T(8,128)(2,1)S(1)} %fusion.28), channel_id=1, source_target_pairs={{0,2},{1,3},{2,0},{3,1},{4,6},{5,7},{6,4},{7,5},{8,10},{9,11},{10,... | collective-permute-start | bytes 1572872 | tf_op jit(solution)/shard_map/ppermute | solution.py:388
  17.7 22.9 %collective-permute-start = (bf16[128,2048]{1,0:T(8,128)(2,1)S(1)}, bf16[128,2048]{1,0:T(8,128)(2,1)S(1)}, u32[]{:S(2)}, u32[]{:S(2)}) collective-permute-start(bf16[128,2048]{1,0:T(8,128)(2,1)S(1)} %fusion.28), channel_id=1, source_target_pairs={{0,1},{1,0},{2,3},{3,2},{4,5},{5,4},{6,7},{7,6},{8,9},{9,8},{10,11... | collective-permute-start | bytes 1572872 | tf_op jit(solution)/shard_map/ppermute | solution.py:388
  208.1 24.9 %collective-permute-start.8 = (bf16[128,2048]{1,0:T(8,128)(2,1)S(1)}, bf16[128,2048]{1,0:T(8,128)(2,1)S(1)}, u32[]{:S(2)}, u32[]{:S(2)}) collective-permute-start(bf16[128,2048]{1,0:T(8,128)(2,1)S(1)} %get-tuple-element.79), channel_id=1, source_target_pairs={{0,3},{1,2},{2,1},{3,0},{4,7},{5,6},{6,5},{7,4},{8,11},{9,10},{10,... | collective-permute-start | bytes 1572872 | tf_op jit(solution)/shard_map/ppermute | solution.py:388
  209.5 24.8 %collective-permute-start.7 = (bf16[128,2048]{1,0:T(8,128)(2,1)S(1)}, bf16[128,2048]{1,0:T(8,128)(2,1)S(1)}, u32[]{:S(2)}, u32[]{:S(2)}) collective-permute-start(bf16[128,2048]{1,0:T(8,128)(2,1)S(1)} %get-tuple-element.80), channel_id=1, source_target_pairs={{0,2},{1,3},{2,0},{3,1},{4,6},{5,7},{6,4},{7,5},{8,10},{9,11},{10,... | collective-permute-start | bytes 1572872 | tf_op jit(solution)/shard_map/ppermute | solution.py:388
  238.7 25.7 %collective-permute-start.10 = (bf16[128,2048]{1,0:T(8,128)(2,1)S(1)}, bf16[128,2048]{1,0:T(8,128)(2,1)}, u32[]{:S(2)}, u32[]{:S(2)}) collective-permute-start(bf16[128,2048]{1,0:T(8,128)(2,1)S(1)} %multiply_convert_fusion.4), channel_id=1, source_target_pairs={{0,2},{1,3},{2,0},{3,1},{4,6},{5,7},{6,4},{7,5},{8,10},{9,11},{10,... | collective-permute-start | bytes 1572872 | tf_op jit(solution)/shard_map/ppermute | solution.py:388
  240.2 24.3 %collective-permute-start.9 = (bf16[128,2048]{1,0:T(8,128)(2,1)S(1)}, bf16[128,2048]{1,0:T(8,128)(2,1)}, u32[]{:S(2)}, u32[]{:S(2)}) collective-permute-start(bf16[128,2048]{1,0:T(8,128)(2,1)S(1)} %multiply_convert_fusion.4), channel_id=1, source_target_pairs={{0,1},{1,0},{2,3},{3,2},{4,5},{5,4},{6,7},{7,6},{8,9},{9,8},{10,11... | collective-permute-start | bytes 1572872 | tf_op jit(solution)/shard_map/ppermute | solution.py:388
  241.0 35.1 %collective-permute-start.17 = (bf16[128,2048]{1,0:T(8,128)(2,1)S(1)}, bf16[128,2048]{1,0:T(8,128)(2,1)S(1)}, u32[]{:S(2)}, u32[]{:S(2)}) collective-permute-start(bf16[128,2048]{1,0:T(8,128)(2,1)S(1)} %fusion.34), channel_id=1, source_target_pairs={{0,3},{1,2},{2,1},{3,0},{4,7},{5,6},{6,5},{7,4},{8,11},{9,10},{10,... | collective-permute-start | bytes 1572872 | tf_op jit(solution)/shard_map/ppermute | solution.py:388
  242.5 42.1 %collective-permute-start.16 = (bf16[128,2048]{1,0:T(8,128)(2,1)S(1)}, bf16[128,2048]{1,0:T(8,128)(2,1)S(1)}, u32[]{:S(2)}, u32[]{:S(2)}) collective-permute-start(bf16[128,2048]{1,0:T(8,128)(2,1)S(1)} %fusion.34), channel_id=1, source_target_pairs={{0,2},{1,3},{2,0},{3,1},{4,6},{5,7},{6,4},{7,5},{8,10},{9,11},{10,... | collective-permute-start | bytes 1572872 | tf_op jit(solution)/shard_map/ppermute | solution.py:388
  253.1 32.3 %collective-permute-start.15 = (bf16[128,2048]{1,0:T(8,128)(2,1)S(1)}, bf16[128,2048]{1,0:T(8,128)(2,1)}, u32[]{:S(2)}, u32[]{:S(2)}) collective-permute-start(bf16[128,2048]{1,0:T(8,128)(2,1)S(1)} %fusion.34), channel_id=1, source_target_pairs={{0,1},{1,0},{2,3},{3,2},{4,5},{5,4},{6,7},{7,6},{8,9},{9,8},{10,11... | collective-permute-start | bytes 1572872 | tf_op jit(solution)/shard_map/ppermute | solution.py:388
  306.9 24.3 %collective-permute-start.20 = (bf16[128,2048]{1,0:T(8,128)(2,1)S(1)}, bf16[128,2048]{1,0:T(8,128)(2,1)S(1)}, u32[]{:S(2)}, u32[]{:S(2)}) collective-permute-start(bf16[128,2048]{1,0:T(8,128)(2,1)S(1)} %get-tuple-element.73), channel_id=1, source_target_pairs={{0,3},{1,2},{2,1},{3,0},{4,7},{5,6},{6,5},{7,4},{8,11},{9,10},{10,... | collective-permute-start | bytes 1572872 | tf_op jit(solution)/shard_map/ppermute | solution.py:388
  307.9 24.6 %collective-permute-start.19 = (bf16[128,2048]{1,0:T(8,128)(2,1)S(1)}, bf16[128,2048]{1,0:T(8,128)(2,1)S(1)}, u32[]{:S(2)}, u32[]{:S(2)}) collective-permute-start(bf16[128,2048]{1,0:T(8,128)(2,1)S(1)} %get-tuple-element.74), channel_id=1, source_target_pairs={{0,2},{1,3},{2,0},{3,1},{4,6},{5,7},{6,4},{7,5},{8,10},{9,11},{10,... | collective-permute-start | bytes 1572872 | tf_op jit(solution)/shard_map/ppermute | solution.py:388
  341.1 22.7 %collective-permute-start.22 = (bf16[128,2048]{1,0:T(8,128)(2,1)S(1)}, bf16[128,2048]{1,0:T(8,128)(2,1)S(1)}, u32[]{:S(2)}, u32[]{:S(2)}) collective-permute-start(bf16[128,2048]{1,0:T(8,128)(2,1)S(1)} %get-tuple-element.64), channel_id=1, source_target_pairs={{0,2},{1,3},{2,0},{3,1},{4,6},{5,7},{6,4},{7,5},{8,10},{9,11},{10,... | collective-permute-start | bytes 1572872 | tf_op jit(solution)/shard_map/ppermute | solution.py:388
  368.1 142.9 %reduce-scatter.11.cloned.1.call-start = ((), (), s32[]{:S(2)}) async-start(), calls=%async_computation.10 | async-start | bytes 6488064 | tf_op jit(solution)/shard_map/reduce_scatter | solution.py:426
  376.2 163.3 %reduce-scatter.5.cloned.1.call-start = ((), (), s32[]{:S(2)}) async-start(), calls=%async_computation.7 | async-start | bytes 7077888 | tf_op jit(solution)/shard_map/reduce_scatter | solution.py:426
  412.7 247.1 %reduce-scatter.9.cloned.1.call-start = ((), (), s32[]{:S(2)}) async-start(), calls=%async_computation.9 | async-start | bytes 12976128 | tf_op jit(solution)/shard_map/reduce_scatter | solution.py:426
  431.6 48.5 %collective-permute-start.12 = (bf16[128,2048]{1,0:T(8,128)(2,1)}, bf16[128,2048]{1,0:T(8,128)(2,1)S(1)}, u32[]{:S(2)}, u32[]{:S(2)}) collective-permute-start(bf16[128,2048]{1,0:T(8,128)(2,1)} %get-tuple-element.75), channel_id=1, source_target_pairs={{0,1},{1,0},{2,3},{3,2},{4,5},{5,4},{6,7},{7,6},{8,9},{9,8},{10,11... | collective-permute-start | bytes 1572872 | tf_op jit(solution)/shard_map/ppermute | solution.py:388
  442.2 27.7 %collective-permute-start.26 = (bf16[128,2048]{1,0:T(8,128)(2,1)S(1)}, bf16[128,2048]{1,0:T(8,128)(2,1)S(1)}, u32[]{:S(2)}, u32[]{:S(2)}) collective-permute-start(bf16[128,2048]{1,0:T(8,128)(2,1)S(1)} %get-tuple-element.70), channel_id=1, source_target_pairs={{0,3},{1,2},{2,1},{3,0},{4,7},{5,6},{6,5},{7,4},{8,11},{9,10},{10,... | collective-permute-start | bytes 1572872 | tf_op jit(solution)/shard_map/ppermute | solution.py:388
  443.0 26.9 %collective-permute-start.25 = (bf16[128,2048]{1,0:T(8,128)(2,1)S(1)}, bf16[128,2048]{1,0:T(8,128)(2,1)S(1)}, u32[]{:S(2)}, u32[]{:S(2)}) collective-permute-start(bf16[128,2048]{1,0:T(8,128)(2,1)S(1)} %get-tuple-element.71), channel_id=1, source_target_pairs={{0,2},{1,3},{2,0},{3,1},{4,6},{5,7},{6,4},{7,5},{8,10},{9,11},{10,... | collective-permute-start | bytes 1572872 | tf_op jit(solution)/shard_map/ppermute | solution.py:388
  447.3 32.9 %collective-permute-start.14 = (bf16[128,2048]{1,0:T(8,128)(2,1)S(1)}, bf16[128,2048]{1,0:T(8,128)(2,1)S(1)}, u32[]{:S(2)}, u32[]{:S(2)}) collective-permute-start(bf16[128,2048]{1,0:T(8,128)(2,1)S(1)} %copy-done.13), channel_id=1, source_target_pairs={{0,3},{1,2},{2,1},{3,0},{4,7},{5,6},{6,5},{7,4},{8,11},{9,10},{10,... | collective-permute-start | bytes 1572872 | tf_op jit(solution)/shard_map/ppermute | solution.py:388
  457.8 33.5 %collective-permute-start.13 = (bf16[128,2048]{1,0:T(8,128)(2,1)S(1)}, bf16[128,2048]{1,0:T(8,128)(2,1)S(1)}, u32[]{:S(2)}, u32[]{:S(2)}) collective-permute-start(bf16[128,2048]{1,0:T(8,128)(2,1)S(1)} %copy-done.12), channel_id=1, source_target_pairs={{0,2},{1,3},{2,0},{3,1},{4,6},{5,7},{6,4},{7,5},{8,10},{9,11},{10,... | collective-permute-start | bytes 1572872 | tf_op jit(solution)/shard_map/ppermute | solution.py:388
  (56 other events, 913.3 us)
Sparse Core Ops, SparseCore 0:
  10.2 67.7 all-gather.3
  79.7 123.8 all-gather.5
  205.2 59.0 all-gather.7
  368.2 33.0 reduce-scatter.6
  403.5 63.5 reduce-scatter.10
  469.2 70.2 reduce-scatter.4
  541.9 117.9 reduce-scatter.8

commit v2 on v1

v2 whole, which is shorter than its diff:
```python
import functools

import jax
import jax.numpy as jnp
from jax import lax
from jax.experimental import pallas as pl
from jax.experimental.pallas import tpu as pltpu
from jax.sharding import PartitionSpec as P

DH = 128
CONV = 4
SPAN = 64
HALO = 8
epsilon = 1e-06
f32 = jnp.float32
bf16 = jnp.bfloat16

NN = (((1,), (0,)), ((), ()))
NT = (((1,), (1,)), ((), ()))
TN = (((0,), (0,)), ((), ()))


def mm(left, right, dims=NN):
    return lax.dot_general(left.astype(bf16), right.astype(bf16), dims, preferred_element_type=f32)


def mm3(left, right, dims=NN):
    lh = left.astype(bf16)
    ll = (left - lh.astype(f32)).astype(bf16)
    rh = right.astype(bf16)
    rl = (right - rh.astype(f32)).astype(bf16)
    out = lax.dot_general(ll, rh, dims, preferred_element_type=f32)
    out = out + lax.dot_general(lh, rl, dims, preferred_element_type=f32)
    return out + lax.dot_general(lh, rh, dims, preferred_element_type=f32)


def tri_masks(rows):
    r = lax.broadcasted_iota(jnp.int32, (rows, rows), 0)
    c = lax.broadcasted_iota(jnp.int32, (rows, rows), 1)
    same = (r // SPAN) == (c // SPAN)
    return r, c, same


def unit_lower_inverse(lower, r, c):
    eye = (r == c).astype(f32)
    half = 1
    inverse = eye
    while half < SPAN:
        pair = ((r // (2 * half)) == (c // (2 * half))) & ((r // half) != (c // half))
        corner = jnp.where(pair, lower, 0.0)
        if half == 1:
            inverse = eye - corner
        else:
            inverse = inverse - mm(mm(inverse, corner), inverse)
        half *= 2
    resid = eye - inverse - mm3(lower, inverse)
    return inverse + mm(inverse, resid)


def rolled(block, halo_before, lag):
    if lag == 0:
        return block
    whole = jnp.concatenate([halo_before, block], axis=0)
    return pltpu.roll(whole, lag, 0)[HALO:]


def rolled_back(block, halo_after, lag):
    if lag == 0:
        return block
    whole = jnp.concatenate([block, halo_after], axis=0)
    return pltpu.roll(whole, whole.shape[0] - lag, 0)[: block.shape[0]]


def sigmoid(v):
    return 1.0 / (1.0 + jnp.exp(-v))


def row_start(place_ref, c, per):
    chunk = lax.div(c, per)
    return pl.multiple_of(((chunk ^ place_ref[0]) * per + lax.rem(c, per)) * SPAN, SPAN)


def conv_block(x_ref, conv_ref, start, before, keep, part, head, width):
    cols = pl.ds(part * width + head * DH, DH)
    block = x_ref[pl.ds(start, SPAN), cols].astype(f32)
    halo = x_ref[pl.ds(before, 16), cols].astype(f32)[16 - HALO :] * keep
    shifted = [rolled(block, halo, lag) for lag in range(CONV)]
    taps = [conv_ref[pl.ds(part * CONV + lag, 1), pl.ds(head * DH, DH)] for lag in range(CONV)]
    total = taps[0] * shifted[0]
    for lag in range(1, CONV):
        total = total + taps[lag] * shifted[lag]
    return total, shifted, taps


def strengths(logit_refs, start, heads):
    columns = []
    for logit_ref in logit_refs:
        block = sigmoid(logit_ref[pl.ds(start, SPAN), :]).astype(bf16).astype(f32)
        columns += [block[:, h : h + 1] for h in range(heads)]
    return jnp.concatenate(columns, axis=0)


def fwd_kernel(per, groups, reset_ref, place_ref, conv_ref, gain_ref, *refs):
    x_refs, logit_refs = refs[:groups], refs[groups : 2 * groups]
    normed_refs, mixed_refs = refs[2 * groups : 3 * groups], refs[3 * groups : 4 * groups]
    t_ref, s_ref, n_ref, q_s, k_s, u_s, w_s, p_s, state = refs[4 * groups :]
    length = x_refs[0].shape[0]
    width = x_refs[0].shape[1] // 3
    heads = width // DH
    blocks = length // SPAN
    pairs = [(g, h) for g in range(groups) for h in range(heads)]
    rows = len(pairs) * SPAN
    r, c_, same = tri_masks(rows)
    strict = same & (r > c_)
    incl = same & (r >= c_)

    def local(c, carry):
        start = row_start(place_ref, c, per)
        before = pl.multiple_of(row_start(place_ref, jnp.maximum(c - 1, 0), per) + (SPAN - 16), 16)
        parts = []
        for part in range(3):
            pieces = []
            for g, h in pairs:
                keep = 1.0 - reset_ref[g * blocks + c]
                z, _, _ = conv_block(x_refs[g], conv_ref, start, before, keep, part, h, width)
                pieces.append(z)
            z = jnp.concatenate(pieces, axis=0)
            parts.append(z * sigmoid(z))
        q, k, v = parts
        q = q * lax.rsqrt(jnp.sum(q * q, axis=-1, keepdims=True) + epsilon)
        k = k * lax.rsqrt(jnp.sum(k * k, axis=-1, keepdims=True) + epsilon)
        b = strengths(logit_refs, start, heads)
        gram = mm3(k, k, NT)
        lower = jnp.where(strict, gram * b, 0.0)
        inverse = unit_lower_inverse(lower, r, c_)
        p_s[c] = jnp.where(incl, mm(q, k, NT), 0.0).astype(bf16)
        t_ref[c] = inverse.astype(bf16)
        solved = mm(inverse, jnp.concatenate([b * k, b * v], axis=1))
        w_s[c] = solved[:, :DH].astype(bf16)
        u_s[c] = solved[:, DH:]
        q_s[c] = q.astype(bf16)
        k_s[c] = k.astype(bf16)
        return carry

    lax.fori_loop(0, blocks, local, 0)
    state[...] = jnp.zeros_like(state)
    gain = gain_ref[...]

    def scan(c, carry):
        start = row_start(place_ref, c, per)
        news = []
        reads = []
        for at, (g, h) in enumerate(pairs):
            keep = 1.0 - reset_ref[g * blocks + c]
            here = pl.ds(at * SPAN, SPAN)
            s = state[pl.ds(at * DH, DH), :] * keep
            low = s.astype(bf16)
            s_ref[c, pl.ds(at * DH, DH), :] = low
            both = jnp.concatenate([w_s[c, here, :], q_s[c, here, :]], axis=0)
            got = mm(both, low)
            fresh = u_s[c, here, :] - got[:SPAN]
            state[pl.ds(at * DH, DH), :] = s + mm(k_s[c, here, :], fresh, TN)
            news.append(fresh)
            reads.append(got[SPAN:])
        fresh = jnp.concatenate(news, axis=0).astype(bf16)
        n_ref[c] = fresh
        out = jnp.concatenate(reads, axis=0) + mm(p_s[c], fresh)
        mixed = out.astype(bf16)
        wide = mixed.astype(f32)
        normed = (wide * lax.rsqrt(jnp.mean(wide * wide, axis=-1, keepdims=True) + epsilon) * gain).astype(bf16)
        for at, (g, h) in enumerate(pairs):
            cols = pl.ds(h * DH, DH)
            mixed_refs[g][pl.ds(start, SPAN), cols] = mixed[at * SPAN : (at + 1) * SPAN]
            normed_refs[g][pl.ds(start, SPAN), cols] = normed[at * SPAN : (at + 1) * SPAN]
        return carry

    lax.fori_loop(0, blocks, scan, 0)


def delta_forward(per, reset, place, xs, logits, conv, gain):
    groups = len(xs)
    length = xs[0].shape[0]
    width = xs[0].shape[1] // 3
    heads = groups * (width // DH)
    blocks = length // SPAN
    rows = heads * SPAN
    shape = jax.ShapeDtypeStruct
    vmem = pl.BlockSpec(memory_space=pltpu.VMEM)
    smem = pl.BlockSpec(memory_space=pltpu.SMEM)
    out = pl.pallas_call(
        functools.partial(fwd_kernel, per, groups),
        out_shape=(shape((length, width), bf16),) * (2 * groups)
        + (
            shape((blocks, rows, rows), bf16),
            shape((blocks, heads * DH, DH), bf16),
            shape((blocks, rows, DH), bf16),
        ),
        in_specs=[smem, smem] + [vmem] * (2 + 2 * groups),
        out_specs=(vmem,) * (2 * groups + 3),
        scratch_shapes=[
            pltpu.VMEM((blocks, rows, DH), bf16),
            pltpu.VMEM((blocks, rows, DH), bf16),
            pltpu.VMEM((blocks, rows, DH), f32),
            pltpu.VMEM((blocks, rows, DH), bf16),
            pltpu.VMEM((blocks, rows, rows), bf16),
            pltpu.VMEM((heads * DH, DH), f32),
        ],
        name="delta_forward",
    )(reset, place, conv, gain, *xs, *logits)
    return out[:groups], out[groups : 2 * groups], out[2 * groups :]


def bwd_kernel(per, groups, reset_ref, place_ref, conv_ref, gain_ref, *refs):
    x_refs, logit_refs = refs[:groups], refs[groups : 2 * groups]
    mixed_refs, dnorm_refs = refs[2 * groups : 3 * groups], refs[3 * groups : 4 * groups]
    t_ref, s_ref, n_ref = refs[4 * groups : 4 * groups + 3]
    dx_refs = refs[4 * groups + 3 : 5 * groups + 3]
    dconv_ref, dgain_ref, q_s, k_s, v_s, iq_s, ik_s, do_s, g_s, kt_s, ds_s, dstate = refs[5 * groups + 3 :]
    length = x_refs[0].shape[0]
    width = x_refs[0].shape[1] // 3
    heads = width // DH
    blocks = length // SPAN
    pairs = [(g, h) for g in range(groups) for h in range(heads)]
    rows = len(pairs) * SPAN
    r, c_, same = tri_masks(rows)
    strict = same & (r > c_)
    incl = same & (r >= c_)
    gain = gain_ref[...]

    def stack(some, start):
        return jnp.concatenate([some[g][pl.ds(start, SPAN), pl.ds(h * DH, DH)] for g, h in pairs], axis=0)

    def local(c, total):
        start = row_start(place_ref, c, per)
        before = pl.multiple_of(row_start(place_ref, jnp.maximum(c - 1, 0), per) + (SPAN - 16), 16)
        parts = []
        for part in range(3):
            pieces = []
            for g, h in pairs:
                keep = 1.0 - reset_ref[g * blocks + c]
                z, _, _ = conv_block(x_refs[g], conv_ref, start, before, keep, part, h, width)
                pieces.append(z)
            z = jnp.concatenate(pieces, axis=0)
            parts.append(z * sigmoid(z))
        q, k, v = parts
        iq = lax.rsqrt(jnp.sum(q * q, axis=-1, keepdims=True) + epsilon)
        ik = lax.rsqrt(jnp.sum(k * k, axis=-1, keepdims=True) + epsilon)
        q = q * iq
        k = k * ik
        q_s[c] = q
        k_s[c] = k
        v_s[c] = v
        iq_s[c] = jnp.broadcast_to(iq, (rows, DH))
        ik_s[c] = jnp.broadcast_to(ik, (rows, DH))
        mixed = stack(mixed_refs, start).astype(f32)
        dnorm = stack(dnorm_refs, start)
        inv = lax.rsqrt(jnp.mean(mixed * mixed, axis=-1, keepdims=True) + epsilon)
        u = mixed * inv
        total = total + jnp.sum(dnorm * u, axis=0, keepdims=True)
        dg = dnorm * gain
        do = ((dg - u * jnp.mean(dg * u, axis=-1, keepdims=True)) * inv).astype(bf16)
        do_s[c] = do
        p = jnp.where(incl, mm(q, k, NT), 0.0)
        t = t_ref[c]
        pre = mm(p, do, TN)
        got = mm(t, jnp.concatenate([pre, k], axis=1), TN)
        g_s[c] = got[:, :DH]
        kt_s[c] = got[:, DH:].astype(bf16)
        return total

    dgain_ref[...] = lax.fori_loop(0, blocks, local, jnp.zeros((1, DH), f32))
    dstate[...] = jnp.zeros_like(dstate)

    def scan(i, carry):
        c = blocks - 1 - i
        start = row_start(place_ref, c, per)
        b = strengths(logit_refs, start, heads)
        k = k_s[c]
        bk = (b * k).astype(bf16)
        for at, (g_, h) in enumerate(pairs):
            keep = 1.0 - reset_ref[g_ * blocks + c]
            hr = pl.ds(at * SPAN, SPAN)
            ds = dstate[pl.ds(at * DH, DH), :]
            low = ds.astype(bf16)
            ds_s[c, pl.ds(at * DH, DH), :] = low
            g = g_s[c, hr, :] + mm(kt_s[c, hr, :], low)
            g_s[c, hr, :] = g
            ql = q_s[c, hr, :].astype(bf16)
            both = jnp.concatenate([ql, bk[at * SPAN : (at + 1) * SPAN]], axis=0)
            other = jnp.concatenate([do_s[c, hr, :], (-g).astype(bf16)], axis=0)
            dstate[pl.ds(at * DH, DH), :] = (ds + mm(both, other, TN)) * keep
        return carry

    lax.fori_loop(0, blocks, scan, 0)
    dconv_ref[...] = jnp.zeros_like(dconv_ref)
    extra = dx_refs[0].shape[1] - 3 * width
    lane = lax.broadcasted_iota(jnp.int32, (SPAN, extra), 1)

    def last(i, carry):
        c = blocks - 1 - i
        start = row_start(place_ref, c, per)
        before = pl.multiple_of(row_start(place_ref, jnp.maximum(c - 1, 0), per) + (SPAN - 16), 16)
        b = strengths(logit_refs, start, heads)
        q, k, v = q_s[c], k_s[c], v_s[c]
        g, n, do = g_s[c], n_ref[c], do_s[c]
        gl = g.astype(bf16)
        both = jnp.concatenate([do, gl], axis=0)
        outer = mm(both, n, NT)
        dp = jnp.where(incl, outer[:rows], 0.0).astype(bf16)
        da = jnp.where(strict, -outer[rows:], 0.0).astype(bf16)
        down = mm(jnp.concatenate([dp, da], axis=0), k)
        up = mm(jnp.concatenate([dp, da], axis=0), jnp.concatenate([q, b * k], axis=0), TN)
        sides = []
        nds = []
        for at in range(len(pairs)):
            s = s_ref[c, pl.ds(at * DH, DH), :]
            hr = slice(at * SPAN, (at + 1) * SPAN)
            sides.append(mm(jnp.concatenate([do[hr], gl[hr]], axis=0), s, NT))
            nds.append(mm(n[hr], ds_s[c, pl.ds(at * DH, DH), :], NT))
        dos = jnp.concatenate([x[:SPAN] for x in sides], axis=0)
        gs = jnp.concatenate([x[SPAN:] for x in sides], axis=0)
        dq = dos + down[:rows]
        y = down[rows:] - gs
        dk = up + jnp.concatenate(nds, axis=0) + b * y
        dv = b * g
        db = jnp.sum(k * y + v * g, axis=-1, keepdims=True)
        dq = (dq - q * jnp.sum(q * dq, axis=-1, keepdims=True)) * iq_s[c]
        dk = (dk - k * jnp.sum(k * dk, axis=-1, keepdims=True)) * ik_s[c]
        for g_ in range(groups):
            row = jnp.zeros((SPAN, extra), f32)
            for h in range(heads):
                at = g_ * heads + h
                row = jnp.where(lane == h, db[at * SPAN : (at + 1) * SPAN], row)
            sg = sigmoid(logit_refs[g_][pl.ds(start, SPAN), :])
            dl = (row.astype(bf16).astype(f32) * sg * (1.0 - sg)).astype(bf16)
            dx_refs[g_][pl.ds(start, SPAN), pl.ds(3 * width, extra)] = dl
        new_carry = []
        for part, grad in enumerate((dq, dk, dv)):
            for at, (g_, h) in enumerate(pairs):
                keep = 1.0 - reset_ref[g_ * blocks + c]
                z, shifted, taps = conv_block(x_refs[g_], conv_ref, start, before, keep, part, h, width)
                sz = sigmoid(z)
                dz = grad[at * SPAN : (at + 1) * SPAN] * (sz * (1.0 + z * (1.0 - sz)))
                rest = carry[part * len(pairs) + at]
                total = taps[0] * dz
                for lag in range(1, CONV):
                    total = total + taps[lag] * rolled_back(dz, rest, lag)
                dx_refs[g_][pl.ds(start, SPAN), pl.ds(part * width + h * DH, DH)] = total.astype(bf16)
                for lag in range(CONV):
                    spot = pl.ds(part * CONV + lag, 1), pl.ds(h * DH, DH)
                    dconv_ref[spot] = dconv_ref[spot] + jnp.sum(dz * shifted[lag], axis=0, keepdims=True)
                new_carry.append(dz[:HALO] * keep)
        return tuple(new_carry)

    zero = jnp.zeros((HALO, DH), f32)
    lax.fori_loop(0, blocks, last, (zero,) * (3 * len(pairs)))


def delta_backward(per, reset, place, xs, logits, conv, gain, mixeds, dnorms, kept):
    groups = len(xs)
    length = xs[0].shape[0]
    width = xs[0].shape[1] // 3
    extra = logits[0].shape[1]
    heads = groups * (width // DH)
    blocks = length // SPAN
    rows = heads * SPAN
    shape = jax.ShapeDtypeStruct
    vmem = pl.BlockSpec(memory_space=pltpu.VMEM)
    smem = pl.BlockSpec(memory_space=pltpu.SMEM)
    out = pl.pallas_call(
        functools.partial(bwd_kernel, per, groups),
        out_shape=(shape((length, 3 * width + extra), bf16),) * groups
        + (shape((3 * CONV, width), f32), shape((1, DH), f32)),
        in_specs=[smem, smem] + [vmem] * (2 + 4 * groups + 3),
        out_specs=(vmem,) * (groups + 2),
        scratch_shapes=[pltpu.VMEM((blocks, rows, DH), f32)] * 5
        + [
            pltpu.VMEM((blocks, rows, DH), bf16),
            pltpu.VMEM((blocks, rows, DH), f32),
            pltpu.VMEM((blocks, rows, DH), bf16),
            pltpu.VMEM((blocks, heads * DH, DH), bf16),
            pltpu.VMEM((heads * DH, DH), f32),
        ],
        name="delta_backward",
    )(reset, place, conv, gain, *xs, *logits, *mixeds, *dnorms, *kept)
    return out[:groups], out[groups], out[groups + 1]


def slot_of(block, core, parts):
    return ((block & 1) ^ core) * (parts // 2) + block // 2


def put_columns(values, out_ref, core, parts):
    depth = values.shape[1] // parts
    for block in range(parts):
        start = pl.multiple_of(slot_of(block, core, parts) * depth, depth)
        out_ref[:, pl.ds(start, depth)] = values[:, block * depth : (block + 1) * depth]


def column_sum(pieces, core, parts):
    depth = pieces[0].shape[1] // parts
    blocks = []
    for block in range(parts):
        start = pl.multiple_of(slot_of(block, core, parts) * depth, depth)
        total = pieces[0][:, pl.ds(start, depth)].astype(f32)
        for piece in pieces[1:]:
            total = total + piece[:, pl.ds(start, depth)].astype(f32)
        blocks.append(total)
    return jnp.concatenate(blocks, axis=1)


def on_core(kernel, name, shapes, core, *arrays):
    vmem = pl.BlockSpec(memory_space=pltpu.VMEM)
    smem = pl.BlockSpec(memory_space=pltpu.SMEM)
    return pl.pallas_call(
        kernel,
        out_shape=shapes,
        in_specs=[smem] + [vmem] * len(arrays),
        out_specs=(vmem,) * len(shapes),
        name=name,
    )(core, *arrays)


def first_kernel(parts, core_ref, x_ref, gain_ref, cot_ref, live_ref, hidden_ref, d_ffo_ref):
    x = x_ref[...].astype(f32)
    scale = lax.rsqrt(jnp.mean(x * x, axis=-1, keepdims=True) + epsilon)
    put_columns((x * scale * gain_ref[...]).astype(bf16), hidden_ref, core_ref[0], parts)
    put_columns((cot_ref[...].astype(f32) * live_ref[...]).astype(bf16), d_ffo_ref, core_ref[0], parts)


def middle_kernel(parts, core_ref, x_ref, gain_ref, *refs):
    pieces, (resid_ref, second_ref) = refs[:-2], refs[-2:]
    resid = x_ref[...].astype(f32) + column_sum(pieces, core_ref[0], parts)
    resid_ref[...] = resid
    scale = lax.rsqrt(jnp.mean(resid * resid, axis=-1, keepdims=True) + epsilon)
    put_columns((resid * scale * gain_ref[...]).astype(bf16), second_ref, core_ref[0], parts)


def norm_back(base, gain, grad):
    scale = lax.rsqrt(jnp.mean(base * base, axis=-1, keepdims=True) + epsilon)
    unit = base * scale
    d_unit = grad * gain
    d_base = (d_unit - unit * jnp.mean(d_unit * unit, axis=-1, keepdims=True)) * scale
    return d_base, jnp.sum(grad * unit, axis=0, keepdims=True)


def back_kernel(parts, core_ref, resid_ref, gain_ref, cot_ref, live_ref, *refs):
    pieces, (d_resid_ref, d_branch_ref, d_gain_ref) = refs[:-3], refs[-3:]
    d_norm, d_gain_ref[...] = norm_back(resid_ref[...], gain_ref[...], column_sum(pieces, core_ref[0], parts))
    d_resid = cot_ref[...].astype(f32) * live_ref[...] + d_norm
    d_resid_ref[...] = d_resid
    put_columns(d_resid.astype(bf16), d_branch_ref, core_ref[0], parts)


def last_kernel(parts, core_ref, x_ref, gain_ref, d_resid_ref, *refs):
    pieces, (grad_ref, d_gain_ref) = refs[:-2], refs[-2:]
    d_norm, d_gain_ref[...] = norm_back(
        x_ref[...].astype(f32), gain_ref[...], column_sum(pieces, core_ref[0], parts)
    )
    grad_ref[...] = d_resid_ref[...] + d_norm


def finish_kernel(parts, core_ref, resid_ref, live_ref, *refs):
    pieces, out_ref = refs[:-1], refs[-1]
    out_ref[...] = ((resid_ref[...] + column_sum(pieces, core_ref[0], parts)) * live_ref[...]).astype(bf16)


def row_copies(pieces, whole, sems):
    rows = pieces[0].shape[0]
    return [
        pltpu.make_async_copy(piece, whole.at[pl.ds(j * rows, rows), :], sems.at[j])
        for j, piece in enumerate(pieces)
    ]


def weight_copies(packs, whole, sems, lines, first, units):
    depth = packs[0].shape[1]
    stride = packs[0].shape[0] // lines
    copies = []
    for side, pack in enumerate(packs):
        for k in range(lines):
            start = (side * lines + k) * depth
            copies.append(
                pltpu.make_async_copy(
                    pack.at[pl.ds(k * stride + first, units), :],
                    whole.at[:, pl.ds(start, depth)],
                    sems.at[side * lines + k],
                )
            )
    return copies


def started(copies):
    for copy in copies:
        copy.start()
    return copies


def waited(copies):
    for copy in copies:
        copy.wait()


def mix_kernel(lines, count, width, near, far, *refs):
    pieces, (rows_ref, x_ref, logit_ref, buf, row_sems, sems) = refs[:count], refs[count:]
    copies = started(row_copies(pieces, rows_ref, row_sems))
    copies += started(weight_copies((near, far), buf, sems, lines, 0, buf.shape[0]))
    waited(copies)
    out = lax.dot_general(rows_ref[...], buf[...], NT, preferred_element_type=f32)
    x_ref[...] = out[:, :width].astype(bf16)
    logit_ref[...] = out[:, width:]


def mix_product(lines, pieces, packs, width, extra):
    vmem = pl.BlockSpec(memory_space=pltpu.VMEM)
    smem = pl.BlockSpec(memory_space=pltpu.SMEM)
    hbm = pl.BlockSpec(memory_space=pl.ANY)
    tokens = pieces[0].shape[0] * len(pieces)
    model = pieces[0].shape[1]
    shape = jax.ShapeDtypeStruct
    return pl.pallas_call(
        functools.partial(mix_kernel, lines, len(pieces), width),
        out_shape=(shape((tokens, model), bf16), shape((tokens, width), bf16), shape((tokens, extra), f32)),
        in_specs=[hbm] * (2 + len(pieces)),
        out_specs=(vmem,) * 3,
        scratch_shapes=[
            pltpu.VMEM((width + extra, model), bf16),
            pltpu.SemaphoreType.DMA((len(pieces),)),
            pltpu.SemaphoreType.DMA((2 * lines,)),
        ],
        cost_estimate=pl.CostEstimate(
            flops=2 * tokens * model * (width + extra), bytes_accessed=2 * model * (2 * tokens + width), transcendentals=0
        ),
        name="mix_product",
    )(*packs, *pieces)


def branch_kernel(lines, count, first, near, far, *refs):
    pieces, (rows_ref, out_ref, buf, row_sems, sems) = refs[:count], refs[count:]
    copies = started(row_copies(pieces, rows_ref, row_sems))
    copies += started(weight_copies((near, far), buf, sems, lines, first, buf.shape[0]))
    waited(copies)
    out_ref[...] = lax.dot_general(rows_ref[...], buf[...], NT, preferred_element_type=f32)


def branch_back(lines, pieces, packs, first, units):
    vmem = pl.BlockSpec(memory_space=pltpu.VMEM)
    smem = pl.BlockSpec(memory_space=pltpu.SMEM)
    hbm = pl.BlockSpec(memory_space=pl.ANY)
    tokens = pieces[0].shape[0] * len(pieces)
    model = pieces[0].shape[1]
    shape = jax.ShapeDtypeStruct
    return pl.pallas_call(
        functools.partial(branch_kernel, lines, len(pieces), first),
        out_shape=(shape((tokens, model), bf16), shape((tokens, units), f32)),
        in_specs=[hbm] * (2 + len(pieces)),
        out_specs=(vmem,) * 2,
        scratch_shapes=[
            pltpu.VMEM((units, model), bf16),
            pltpu.SemaphoreType.DMA((len(pieces),)),
            pltpu.SemaphoreType.DMA((2 * lines,)),
        ],
        cost_estimate=pl.CostEstimate(
            flops=2 * tokens * model * units, bytes_accessed=2 * model * (2 * tokens + units), transcendentals=0
        ),
        name="branch_back",
    )(*packs, *pieces)


def ffn_kernel(lines, count, half, seq_ref, near, far, cots, *refs):
    seconds = refs[:count]
    s_ref, f_ref, act_ref, dgate_ref, dup_ref = refs[count : count + 5]
    chunk_refs, (bufs, row_sems, sems) = refs[count + 5 : 2 * count + 5], refs[2 * count + 5 :]
    rows = seconds[0].shape[0]
    units = act_ref.shape[1]
    first = started(row_copies(seconds, s_ref, row_sems.at[0]))
    weights = []
    for j in range(3):
        weights.append(
            started(weight_copies((near, far), bufs.at[j], sems.at[j], lines, j * units, units))
        )
    later = []
    for j in range(count):
        start = pl.multiple_of(((seq_ref[0] ^ j) * 2 + half) * rows, rows)
        later.append(
            pltpu.make_async_copy(
                cots.at[pl.ds(start, rows), :], f_ref.at[pl.ds(j * rows, rows), :], row_sems.at[1, j]
            )
        )
    started(later)
    waited(first + weights[0])
    gate = lax.dot_general(s_ref[...], bufs[0], NT, preferred_element_type=f32)
    waited(weights[1])
    upper = lax.dot_general(s_ref[...], bufs[1], NT, preferred_element_type=f32)
    sg = sigmoid(gate)
    soft = gate * sg
    act_ref[...] = (soft * upper).astype(bf16)
    slope = upper * (sg * (1.0 + gate * (1.0 - sg)))
    waited(later + weights[2])
    d_act = lax.dot_general(f_ref[...], bufs[2], NT, preferred_element_type=f32)
    d_gate = (d_act * slope).astype(bf16)
    d_up = (d_act * soft).astype(bf16)
    dgate_ref[...] = d_gate
    dup_ref[...] = d_up
    tile = s_ref.shape[1] // 4
    for t in range(4):
        cols = slice(t * tile, (t + 1) * tile)
        out = lax.dot_general(d_gate, bufs[0, :, cols], NN, preferred_element_type=f32)
        out = out + lax.dot_general(d_up, bufs[1, :, cols], NN, preferred_element_type=f32)
        for j, chunk in enumerate(chunk_refs):
            chunk[:, cols] = out[j * rows : (j + 1) * rows].astype(bf16)


def ffn_part(lines, half, seq, seconds, cots, packs):
    vmem = pl.BlockSpec(memory_space=pltpu.VMEM)
    smem = pl.BlockSpec(memory_space=pltpu.SMEM)
    hbm = pl.BlockSpec(memory_space=pl.ANY)
    count = len(seconds)
    tokens = seconds[0].shape[0] * count
    model = seconds[0].shape[1]
    units = packs[0].shape[0] // (3 * lines)
    shape = jax.ShapeDtypeStruct
    return pl.pallas_call(
        functools.partial(ffn_kernel, lines, count, half),
        out_shape=(shape((tokens, model), bf16),) * 2
        + (shape((tokens, units), bf16),) * 3
        + (shape((tokens // count, model), bf16),) * count,
        in_specs=[smem] + [hbm] * (3 + count),
        out_specs=(vmem,) * (5 + count),
        scratch_shapes=[
            pltpu.VMEM((3, units, model), bf16),
            pltpu.SemaphoreType.DMA((2, count)),
            pltpu.SemaphoreType.DMA((3, 2 * lines)),
        ],
        cost_estimate=pl.CostEstimate(
            flops=10 * tokens * units * model, bytes_accessed=6 * units * model + 8 * tokens * model, transcendentals=tokens * units
        ),
        name="ffn_part",
    )(seq, *packs, cots, *seconds)


def product_kernel(halves, spans, steps, fold, stride, count, *refs):
    terms = len(spans)
    lefts = refs[: halves * terms]
    near_ref, far_ref = refs[halves * terms : halves * terms + 2]
    outs = refs[halves * terms + 2 :]
    step = pl.program_id(0)
    rows = outs[0].shape[0]
    depth = near_ref.shape[1]

    def run(pack):
        for half in range(halves):
            for k in range(fold):
                total = None
                for left, (first, units) in zip(lefts[half * terms : (half + 1) * terms], spans):
                    at = k * stride + first
                    part = lax.dot_general(left[...], pack[at : at + units, :], NN, preferred_element_type=f32)
                    total = part if total is None else total + part
                for j in range(count):
                    outs[half * count + j][:, k * depth : (k + 1) * depth] = total[j * rows : (j + 1) * rows].astype(bf16)

    @pl.when(step < steps)
    def _():
        run(near_ref)

    @pl.when(step >= steps)
    def _():
        run(far_ref)


def team_product(lines, lefts, spans, packs, count):
    halves = len(lefts)
    flat = [left for half in lefts for left in half]
    tokens = flat[0].shape[0]
    fold = 2
    stride = packs[0].shape[0] // lines
    depth = packs[0].shape[1]
    steps = lines // fold
    rows = tokens // count
    units = sum(n for _, n in spans)
    out = pl.pallas_call(
        functools.partial(product_kernel, halves, spans, steps, fold, stride, count),
        grid=(2 * steps,),
        in_specs=[pl.BlockSpec(left.shape, lambda t: (0, 0)) for left in flat]
        + [
            pl.BlockSpec((fold * stride, depth), lambda t: (jnp.minimum(t, steps - 1), 0)),
            pl.BlockSpec((fold * stride, depth), lambda t: (jnp.maximum(t - steps, 0), 0)),
        ],
        out_specs=[pl.BlockSpec((rows, fold * depth), lambda t: (0, t))] * (count * halves),
        out_shape=[jax.ShapeDtypeStruct((rows, 2 * lines * depth), bf16)] * (count * halves),
        cost_estimate=pl.CostEstimate(
            flops=4 * halves * tokens * units * lines * depth,
            bytes_accessed=4 * stride * lines * depth + 4 * halves * tokens * lines * depth,
            transcendentals=0,
        ),
        name="team_product",
    )(*flat, *packs)
    return [out[half * count : (half + 1) * count] for half in range(halves)]


def finish_product_kernel(halves, first, units, steps, fold, stride, count, seq_ref, *refs):
    lefts = refs[:halves]
    near_ref, far_ref, out_ref = refs[halves:]
    step = pl.program_id(0)
    rows = lefts[0].shape[0] // count
    depth = near_ref.shape[1]

    def run(pack):
        for half, left in enumerate(lefts):
            for k in range(fold):
                at = k * stride + first
                total = lax.dot_general(left[...], pack[at : at + units, :], NN, preferred_element_type=f32)
                for j in range(count):
                    start = pl.multiple_of(((seq_ref[0] ^ j) * halves + half) * rows, rows)
                    out_ref[pl.ds(start, rows), k * depth : (k + 1) * depth] = total[j * rows : (j + 1) * rows].astype(bf16)

    @pl.when(step < steps)
    def _():
        run(near_ref)

    @pl.when(step >= steps)
    def _():
        run(far_ref)


def finish_product(lines, seq, lefts, span, packs, count):
    first, units = span
    tokens = lefts[0].shape[0]
    fold = 2
    stride = packs[0].shape[0] // lines
    depth = packs[0].shape[1]
    steps = lines // fold
    whole = tokens * len(lefts)
    grid_spec = pltpu.PrefetchScalarGridSpec(
        num_scalar_prefetch=1,
        grid=(2 * steps,),
        in_specs=[pl.BlockSpec(left.shape, lambda t, s: (0, 0)) for left in lefts]
        + [
            pl.BlockSpec((fold * stride, depth), lambda t, s: (jnp.minimum(t, steps - 1), 0)),
            pl.BlockSpec((fold * stride, depth), lambda t, s: (jnp.maximum(t - steps, 0), 0)),
        ],
        out_specs=pl.BlockSpec((whole, fold * depth), lambda t, s: (0, t)),
    )
    return pl.pallas_call(
        functools.partial(finish_product_kernel, len(lefts), first, units, steps, fold, stride, count),
        grid_spec=grid_spec,
        out_shape=jax.ShapeDtypeStruct((whole, 2 * lines * depth), bf16),
        cost_estimate=pl.CostEstimate(
            flops=4 * whole * units * lines * depth,
            bytes_accessed=4 * stride * lines * depth + 4 * whole * lines * depth,
            transcendentals=0,
        ),
        name="finish_product",
    )(seq, *lefts, *packs)


def cut_kernel(lines, count, *refs):
    kept, got, out_ref = refs[:count], refs[count : 2 * count], refs[2 * count]
    depth = out_ref.shape[1]
    stride = out_ref.shape[0] // lines
    first = 0
    for left, right in zip(kept, got):
        rows = left.shape[0]
        for k in range(lines):
            cols = slice(k * depth, (k + 1) * depth)
            out_ref[k * stride + first : k * stride + first + rows, :] = (
                left[:, cols].astype(f32) + right[:, cols].astype(f32)
            ).astype(bf16)
        first += rows


def line_cut(lines, kept, got):
    vmem = pl.BlockSpec(memory_space=pltpu.VMEM)
    rows = sum(left.shape[0] for left in kept)
    return pl.pallas_call(
        functools.partial(cut_kernel, lines, len(kept)),
        out_shape=jax.ShapeDtypeStruct((lines * rows, kept[0].shape[1] // lines), bf16),
        in_specs=[vmem] * (2 * len(kept)),
        out_specs=vmem,
        name="line_cut",
    )(*kept, *got)


def rms_scale(value, gain):
    return value * lax.rsqrt(jnp.mean(value * value, axis=-1, keepdims=True) + epsilon) * gain


def segment_tables(lengths_row, group_tok):
    offsets = jnp.cumsum(lengths_row) - lengths_row
    total = jnp.sum(lengths_row)
    starts = jnp.concatenate([offsets, total[None]])
    block_first = jnp.arange(group_tok // SPAN, dtype=jnp.int32) * SPAN
    reset = jnp.any(block_first[:, None] == starts[None, :], axis=1).astype(f32)
    live = (jnp.arange(group_tok, dtype=jnp.int32) < total).astype(f32)
    return reset, live


def swap(values, axis, mask):
    size = lax.axis_size(axis)
    return lax.ppermute(values, axis, [(i, i ^ mask) for i in range(size)])


def dot(left, right, dims, kind=f32):
    return lax.dot_general(left, right, dims, preferred_element_type=f32).astype(kind)


def after(values, *others):
    return lax.optimization_barrier((values, *others))[0]


def added(first, second):
    return (first.astype(f32) + second.astype(f32)).astype(bf16)


def seq_pieces(values):
    return [values] + [swap(values, "seq", k) for k in range(1, lax.axis_size("seq"))]


def seq_relayed(values, upward):
    pieces = [values]
    for k in range(1, lax.axis_size("seq")):
        hop = 1 << (k.bit_length() - 1) if upward else k & -k
        pieces.append(swap(pieces[k ^ hop], "seq", hop))
    return pieces


def twin_rows(values):
    return swap(values, "dp", 2)


def returned(chunks):
    return [chunks[0]] + [swap(chunks[j], "seq", j) for j in range(1, len(chunks))]


def summed(pieces):
    total = pieces[0].astype(f32)
    for piece in pieces[1:]:
        total = total + piece.astype(f32)
    return total


def halves_of(arrays, half):
    picked = []
    for array in arrays:
        rows = array.shape[0] // 2
        picked.append(array[half * rows : (half + 1) * rows])
    return jnp.concatenate(picked, axis=0)


def line_exchange(values):
    dp_parts = lax.axis_size("dp")
    groups = [list(range(c, dp_parts, 2)) for c in (0, 1)]
    return lax.all_to_all(values, "dp", 0, 0, tiled=True, axis_index_groups=groups)


def line_pack(arrays, lines, *others):
    both = jnp.concatenate([halves_of(arrays, 0), halves_of(arrays, 1)], axis=0)
    return line_exchange(after(jnp.concatenate([both] * (lines // 2), axis=0), *others))


def line_total(pieces, lines, spans):
    rows = pieces.shape[0] // lines
    split = [pieces[k * rows : (k + 1) * rows] for k in range(lines)]
    low = summed(split[0::2])
    high = summed(split[1::2])
    return [
        jnp.concatenate([low[first : first + n], high[first : first + n]], axis=0) for first, n in spans
    ]


def doubled(values, axis):
    size = lax.axis_size(axis)
    mask = 1
    while mask < size:
        values = values + swap(values, axis, mask)
        mask *= 2
    return values


def all_sum(values):
    seq_parts, dp_parts = lax.axis_size("seq"), lax.axis_size("dp")
    values = summed([values] + [swap(values, "seq", k) for k in range(1, seq_parts)])
    values = summed([values] + [swap(values, "dp", k) for k in range(2, dp_parts, 2)])
    return values + swap(values, "dp", 1)


def shards(
    tokens,
    lengths,
    cotangent,
    attn_norm_gain,
    w_query,
    w_key,
    w_value,
    w_strength,
    conv_weight,
    head_gain,
    w_output,
    ffn_norm_gain,
    w_gate,
    w_up,
    w_down,
):
    local, model = tokens.shape
    seq_parts = lax.axis_size("seq")
    seq_place = lax.axis_index("seq")
    dp_parts = lax.axis_size("dp")
    dp_place = lax.axis_index("dp")
    lines = dp_parts // 2
    group_tok = local * seq_parts
    full_width = w_query.shape[1]
    full_heads = w_strength.shape[1]
    width = full_width // 2
    heads = full_heads // 2
    extra = 16
    units = w_gate.shape[1] // 2
    side = model // 2
    per = local // SPAN
    odd = dp_place >> 1 & 1

    def scalar(value):
        return jnp.full((1,), value, jnp.int32)

    def twin(values):
        return swap(values, "dp", 1)

    core = scalar(dp_place & 1)
    place = scalar(seq_place)
    rows_f32 = jax.ShapeDtypeStruct((local, model), f32)
    rows_b16 = jax.ShapeDtypeStruct((local, model), bf16)
    gain_f32 = jax.ShapeDtypeStruct((1, model), f32)

    reset_own, live = segment_tables(lengths[0], group_tok)
    live_col = lax.dynamic_slice_in_dim(live, seq_place * local, local)[:, None]
    taps = lax.dynamic_slice_in_dim(conv_weight.astype(f32).reshape(3 * CONV, full_width), odd * width, width, 1)
    gain_h = head_gain.astype(f32)[None]
    gain_one = attn_norm_gain.astype(f32)[None]
    gain_two = ffn_norm_gain.astype(f32)[None]

    hidden_own, d_ffo_own = on_core(
        functools.partial(first_kernel, dp_parts), "first_norm", (rows_b16,) * 2, core, tokens, gain_one, cotangent, live_col
    )
    hidden_twin = twin_rows(hidden_own)
    reset_twin = twin_rows(reset_own)
    pad = jnp.zeros((extra - heads, w_strength.shape[0]), bf16)
    strength_t = w_strength.T
    strength_rows = jnp.concatenate([strength_t[:heads], pad, strength_t[heads:], pad], axis=0)
    mix_in = line_pack(
        (w_query.T, w_key.T, w_value.T, strength_rows, w_output), lines, hidden_twin, reset_twin
    )
    near_hidden = seq_relayed(hidden_own, True)
    far_hidden = seq_relayed(hidden_twin, False)
    reset = jnp.concatenate([reset_own, reset_twin])
    mix_near = after(mix_in, tuple(near_hidden), tuple(far_hidden))
    mix_packs = (mix_near, twin(mix_near))
    o_first = 3 * width + extra

    d_ffo_twin = twin_rows(after(d_ffo_own, mix_packs[1]))
    hidden_0, x_0, logit_0 = mix_product(lines, near_hidden, mix_packs, 3 * width, extra)
    late_cot = after(jnp.concatenate([d_ffo_own, d_ffo_twin], axis=0), x_0)
    ffn_in = line_pack((w_gate.T, w_up.T, w_down), lines, late_cot)
    cots_all = lax.all_gather(late_cot, "seq", axis=0, tiled=True)
    hidden_1, x_1, logit_1 = mix_product(lines, after(tuple(far_hidden), late_cot), mix_packs, 3 * width, extra)
    normed, mixed, kept = delta_forward(per, reset, place, (x_0, x_1), (logit_0, logit_1), taps, gain_h)
    o_span = ((o_first, width),)
    far_chunks, near_chunks = team_product(lines, ((normed[1],), (normed[0],)), o_span, mix_packs, seq_parts)
    far_sum = summed(returned(far_chunks)).astype(bf16)
    near_got = returned(near_chunks)
    resid, second_own = on_core(
        functools.partial(middle_kernel, dp_parts),
        "middle_norm",
        (rows_f32, rows_b16),
        core,
        tokens,
        gain_two,
        *near_got,
        twin_rows(far_sum),
    )
    second_twin = twin_rows(second_own)
    near_second = seq_pieces(second_own)
    far_second = seq_pieces(second_twin)
    ffn_near = after(ffn_in, second_own)
    ffn_packs = (ffn_near, twin(ffn_near))
    s_0, f_0, act_0, d_gate_0, d_up_0, *near_chunks = ffn_part(lines, 0, place, near_second, cots_all, ffn_packs)
    near_got = returned(near_chunks)
    far_second = after(tuple(far_second), near_chunks[0])
    s_1, f_1, act_1, d_gate_1, d_up_1, *far_chunks = ffn_part(lines, 1, place, far_second, cots_all, ffn_packs)
    acts, d_gates, d_ups, far_chunks = lax.optimization_barrier(
        ((act_0, act_1), (d_gate_0, d_gate_1), (d_up_0, d_up_1), tuple(far_chunks), tuple(near_got))
    )[:4]
    far_got = returned(far_chunks)

    def kept_sum(lefts, rights):
        def product(first, kind):
            return (
                dot(lefts[0], rights[0][:, first : first + side], TN)
                + dot(lefts[1], rights[1][:, first : first + side], TN)
            ).astype(kind)

        return product(0, bf16), product(side, bf16)

    seconds, cots = (s_0, s_1), (f_0, f_1)
    gate_kept, gate_sent = kept_sum(d_gates, seconds)
    up_kept, up_sent = kept_sum(d_ups, seconds)
    down_kept, down_sent = kept_sum(acts, cots)
    far_got = after(tuple(far_got), gate_sent, up_sent, down_sent)
    far_sum = summed(far_got).astype(bf16)
    back = twin_rows(far_sum)
    ffn_cut = line_cut(
        lines, (gate_kept, up_kept, down_kept), after((twin(gate_sent), twin(up_sent), twin(down_sent)), far_sum)
    )
    back = after(back, ffn_cut)
    d_resid, d_branch_own, grad_gain_two = on_core(
        functools.partial(back_kernel, dp_parts),
        "middle_back",
        (rows_f32, rows_b16, gain_f32),
        core,
        resid,
        gain_two,
        cotangent,
        live_col,
        *near_got,
        back,
    )
    d_branch_twin = twin_rows(d_branch_own)
    near_branch = seq_pieces(d_branch_own)
    far_branch = seq_pieces(d_branch_twin)
    ffn_back = line_exchange(after(ffn_cut, d_branch_twin))
    final = finish_product(
        lines, place, after((act_0, act_1), d_branch_own), (2 * units, units), ffn_packs, seq_parts
    )
    far_branch = after(tuple(far_branch), final)
    near_branch = after(tuple(near_branch), far_branch)
    b_0, d_normed_0 = branch_back(lines, near_branch, mix_packs, o_first, width)
    b_1, d_normed_1 = branch_back(lines, far_branch, mix_packs, o_first, width)
    final_sums = lax.psum_scatter(after(final, d_normed_0, d_normed_1), "seq", scatter_dimension=0, tiled=True)
    (d_x_0, d_x_1), d_taps, grad_head = delta_backward(
        per,
        reset,
        place,
        (x_0, x_1),
        (logit_0, logit_1),
        taps,
        gain_h,
        mixed,
        (d_normed_0, d_normed_1),
        kept,
    )
    x_kept, x_sent = kept_sum((d_x_0, d_x_1), (hidden_0, hidden_1))
    x_got = twin(x_sent)
    o_kept, o_sent = kept_sum(normed, after((b_0, b_1), x_sent))
    o_got = twin(o_sent)
    d_x_0, d_x_1 = lax.optimization_barrier((d_x_0, d_x_1, x_sent, x_kept, o_sent, o_kept))[:2]
    x_span = ((0, 3 * width + extra),)
    far_chunks, near_chunks = team_product(lines, ((d_x_1,), (d_x_0,)), x_span, mix_packs, seq_parts)
    far_got = returned(far_chunks)
    near_got = returned(near_chunks)
    grad_gate, grad_up, grad_down = line_total(
        ffn_back, lines, ((0, units), (units, units), (2 * units, units))
    )
    mix_cut = line_cut(lines, (x_kept, o_kept), after((x_got, o_got), near_chunks[0], grad_gate, grad_up, grad_down))
    mix_back = line_exchange(mix_cut)
    mix_spans = (
        (0, width),
        (width, width),
        (2 * width, width),
        (3 * width, heads),
        (o_first, width),
    )
    grad_query, grad_key, grad_value, grad_strength, grad_out = line_total(mix_back, lines, mix_spans)
    far_sum = summed(after(tuple(far_got), mix_cut, tuple(near_got))).astype(bf16)
    back = twin_rows(far_sum)
    final_twin = twin_rows(after(final_sums, far_sum)[local:])
    output = on_core(
        functools.partial(finish_kernel, dp_parts),
        "finish_rows",
        (rows_b16,),
        core,
        resid,
        live_col,
        final_sums[:local],
        final_twin,
    )[0]
    back = after(back, grad_query)
    input_grad, grad_gain_one = on_core(
        functools.partial(last_kernel, dp_parts),
        "last_norm",
        (rows_f32, gain_f32),
        core,
        tokens,
        gain_one,
        d_resid,
        *near_got,
        back,
    )
    early = jnp.zeros((3 * CONV, model), f32)
    early = lax.dynamic_update_slice_in_dim(early, d_taps, seq_place * full_width + odd * width, 1)
    gains = jnp.concatenate([grad_gain_one, grad_gain_two, early], axis=0).reshape(-1, DH)
    gains = all_sum(after(jnp.concatenate([gains, grad_head], axis=0), final_twin))
    wide = gains[:-1].reshape(-1, model)
    conv_grad = lax.dynamic_slice_in_dim(wide[2:], seq_place * full_width, full_width, 1)
    conv_grad = conv_grad.reshape(3, CONV, full_width)
    return (
        output,
        input_grad,
        wide[0],
        grad_query.T,
        grad_key.T,
        grad_value.T,
        grad_strength.T,
        conv_grad,
        gains[-1],
        grad_out,
        wide[1],
        grad_gate.T,
        grad_up.T,
        grad_down,
    )


def solution(mesh):
    placed = (
        P(("dp", "seq"), None),
        P("dp", None),
        P(("dp", "seq"), None),
        P(),
        P("dp", "seq"),
        P("dp", "seq"),
        P("dp", "seq"),
        P("dp", "seq"),
        P(None, None, "seq"),
        P(),
        P("seq", "dp"),
        P(),
        P("dp", "seq"),
        P("dp", "seq"),
        P("seq", "dp"),
    )
    return jax.shard_map(
        shards,
        mesh=mesh,
        in_specs=placed,
        out_specs=(
            P(("dp", "seq"), None),
            P(("dp", "seq"), None),
            P(),
            P("dp", "seq"),
            P("dp", "seq"),
            P("dp", "seq"),
            P("dp", "seq"),
            P(None, None, "seq"),
            P(),
            P("seq", "dp"),
            P(),
            P("dp", "seq"),
            P("dp", "seq"),
            P("seq", "dp"),
        ),
        check_vma=False,
    )
```

time: 679 us -> 599 us (0.88)
  waiting for transfers between devices: 421 us -> 251 us
  Pallas kernels: 50.5 us -> 152 us
  matrix products: 109 us -> 28.6 us
  starting transfers between devices: 45.1 us -> 80.4 us
  local copies, waits for them, and re-layouts: 17.9 us -> 42.3 us
  other arithmetic: 10.6 us -> 20.1 us
    reduce_scatter x4 -> x1, waiting for transfers between devices: 144 us -> 0.01 us  [shards(): lax.psum_scatter(after(final, d_normed_0, d_normed_1), 'seq', scatter_dim...]
    all_gather x3 -> x1, waiting for transfers between devices: 125 us -> 0.01 us  [shards(): cots_all = lax.all_gather(late_cot, 'seq', axis=0, tiled=True)]
    pallas_call x2 -> x18, Pallas kernels: 50.5 us -> 152 us  [the longest x2 30.8 us: ffn_part(): pl.pallas_call(functools.partial(ffn_kernel, lines, count, half), out_sha...]
    ppermute x35 -> x59, waiting for transfers between devices: 151 us -> 239 us  [swap(): return lax.ppermute(values, axis, [(i, i ^ mask) for i in range(size)])]
    dot_general x20, matrix products: 109 us -> 28.6 us  [dot(): lax.dot_general(left, right, dims, preferred_element_type=f32).astype(kind)]
    unnamed x80 -> x174, local copies, waits for them, and re-layouts: 7.85 us -> 33.8 us
    all_to_all x0 -> x4, starting transfers between devices: none -> 18.8 us  [line_exchange(): lax.all_to_all(values, 'dp', 0, 0, tiled=True, axis_index_groups=groups)]
    ppermute x35 -> x59, starting transfers between devices: 44.4 us -> 61.5 us  [swap(): return lax.ppermute(values, axis, [(i, i ^ mask) for i in range(size)])]
  transfers between devices with their start and end apart: 42 -> 65, of which waited for: 29 -> 31; matrix products, arithmetic and copies ran while one was open for 15% -> 12% of each run, Pallas kernels for 8% -> 25%
where the time goes in v2:
time: 599 us; the launch traced here: 590 us
  waiting for transfers between devices  251 us (42%)
  Pallas kernels  152 us (25%)
  starting transfers between devices  80.4 us (13%)
  local copies, waits for them, and re-layouts  42.3 us (7%)
  matrix products  28.6 us (5%)
  other arithmetic  20.1 us (3%)
  between operations  16 us (3%)
    ppermute x59, waiting for transfers between devices, swap(): return lax.ppermute(values, axis, [(i, i ^ mask) for i in range(size)])  239 us
    ppermute x59, starting transfers between devices, swap(): return lax.ppermute(values, axis, [(i, i ^ mask) for i in range(size)])  61.5 us
    unnamed x174, local copies, waits for them, and re-layouts  33.8 us
    pallas_call x2, Pallas kernels, ffn_part(): pl.pallas_call(functools.partial(ffn_kernel, lines, count, half), out_sha...  30.8 us
    dot_general x20, matrix products, dot(): lax.dot_general(left, right, dims, preferred_element_type=f32).astype(kind)  28.6 us
    pallas_call x1, Pallas kernels, delta_forward(): pl.pallas_call(functools.partial(fwd_kernel, per, groups), out_shape=(sha...  27.3 us
    pallas_call x1, Pallas kernels, delta_backward(): pl.pallas_call(functools.partial(bwd_kernel, per, groups), out_shape=(sha...  23.5 us
    all_to_all x4, starting transfers between devices, line_exchange(): lax.all_to_all(values, 'dp', 0, 0, tiled=True, axis_index_groups=groups)  18.8 us
  transfers between devices with their start and end apart: 65, of which 31 were waited for; matrix products, arithmetic and copies ran while one was open for 12% of the time, Pallas kernels for 25%

profile of v2, /device:TPU:0, one launch (start us, length us, event | category | flops | bytes accessed | tf_op | source)
XLA Modules:
  0.0 590.1 jit_solution(15898709577327739151)
XLA Ops:
  17.6 11.9 %collective-permute-done.1.refs_0_ = bf16[128,2048]{1,0:T(8,128)(2,1)} collective-permute-done((bf16[128,2048]{1,0:T(8,128)(2,1)}, bf16[128,2048]{1,0:T(8,128)(2,1)}, u32[]{:S(2)}, u32[]{:S(2)}) %collective-permute-start.1) | collective-permute-done | bytes 524320 | tf_op jit(solution)/shard_map/ppermute | solution.py:800
  37.5 10.9 %collective-permute-done.2.refs_1_ = bf16[128,2048]{1,0:T(8,128)(2,1)} collective-permute-done((bf16[128,2048]{1,0:T(8,128)(2,1)S(1)}, bf16[128,2048]{1,0:T(8,128)(2,1)}, u32[]{:S(2)}, u32[]{:S(2)}) %collective-permute-start.2) | collective-permute-done | bytes 524320 | tf_op jit(solution)/shard_map/ppermute | solution.py:800
  61.4 8.4 %collective-permute-done.4.refs_3_ = bf16[128,2048]{1,0:T(8,128)(2,1)} collective-permute-done((bf16[128,2048]{1,0:T(8,128)(2,1)}, bf16[128,2048]{1,0:T(8,128)(2,1)}, u32[]{:S(2)}, u32[]{:S(2)}) %collective-permute-start.4) | collective-permute-done | bytes 524320 | tf_op jit(solution)/shard_map/ppermute | solution.py:800
  69.8 11.4 %all-to-all-done = bf16[4,1040,256]{2,1,0:T(8,128)(2,1)S(1)} async-done(((bf16[4,1040,256]{2,1,0:T(8,128)(2,1)}), bf16[4,1040,256]{2,1,0:T(8,128)(2,1)S(1)}, u32[]{:S(2)}, u32[]{:S(2)}) %all-to-all-start) | async-done | bytes 2129952 | tf_op jit(solution)/shard_map/all_to_all | solution.py:853
  119.7 27.3 %delta_forward.1 = (bf16[512,256]{1,0:T(8,128)(2,1)}, bf16[512,256]{1,0:T(8,128)(2,1)}, bf16[512,256]{1,0:T(8,128)(2,1)}, bf16[512,256]{1,0:T(8,128)(2,1)}, bf16...) custom-call(f32[16]{0:T(128)} %pad_maximum_fusion.8.reset_ref, ...), custom_call_target="tpu_custom_call" | custom-call | tf_op jit(solution)/shard_map/delta_forward/pallas_call | solution.py:190
  159.5 20.6 %collective-permute-done.15 = bf16[128,2048]{1,0:T(8,128)(2,1)S(1)} collective-permute-done((bf16[128,2048]{1,0:T(8,128)(2,1)}, bf16[128,2048]{1,0:T(8,128)(2,1)S(1)}, u32[]{:S(2)}, u32[]{:S(2)}) %collective-permute-start.15) | collective-permute-done | bytes 524320 | tf_op jit(solution)/shard_map/ppermute | solution.py:800
  182.0 9.4 %collective-permute-done.14 = bf16[128,2048]{1,0:T(8,128)(2,1)S(1)} collective-permute-done((bf16[128,2048]{1,0:T(8,128)(2,1)}, bf16[128,2048]{1,0:T(8,128)(2,1)S(1)}, u32[]{:S(2)}, u32[]{:S(2)}) %collective-permute-start.14) | collective-permute-done | bytes 524320 | tf_op jit(solution)/shard_map/ppermute | solution.py:800
  195.7 7.7 %collective-permute-done.10.refs_1_ = bf16[128,2048]{1,0:T(8,128)(2,1)S(1)} collective-permute-done((bf16[128,2048]{1,0:T(8,128)(2,1)}, bf16[128,2048]{1,0:T(8,128)(2,1)S(1)}, u32[]{:S(2)}, u32[]{:S(2)}) %collective-permute-start.10) | collective-permute-done | bytes 524320 | tf_op jit(solution)/shard_map/ppermute | solution.py:800
  203.3 11.5 %collective-permute-done.12.refs_3_ = bf16[128,2048]{1,0:T(8,128)(2,1)S(1)} collective-permute-done((bf16[128,2048]{1,0:T(8,128)(2,1)}, bf16[128,2048]{1,0:T(8,128)(2,1)S(1)}, u32[]{:S(2)}, u32[]{:S(2)}) %collective-permute-start.12) | collective-permute-done | bytes 524320 | tf_op jit(solution)/shard_map/ppermute | solution.py:800
  226.4 10.9 %collective-permute-done.21.refs_0_ = bf16[128,2048]{1,0:T(8,128)(2,1)S(1)} collective-permute-done((bf16[128,2048]{1,0:T(8,128)(2,1)}, bf16[128,2048]{1,0:T(8,128)(2,1)S(1)}, u32[]{:S(2)}, u32[]{:S(2)}) %collective-permute-start.21) | collective-permute-done | bytes 524320 | tf_op jit(solution)/shard_map/ppermute | solution.py:800
  240.3 9.5 %collective-permute-done.19.refs_2_ = bf16[128,2048]{1,0:T(8,128)(2,1)S(1)} collective-permute-done((bf16[128,2048]{1,0:T(8,128)(2,1)}, bf16[128,2048]{1,0:T(8,128)(2,1)S(1)}, u32[]{:S(2)}, u32[]{:S(2)}) %collective-permute-start.19) | collective-permute-done | bytes 524320 | tf_op jit(solution)/shard_map/ppermute | solution.py:800
  251.3 15.3 %ffn_part.2 = (bf16[512,2048]{1,0:T(8,128)(2,1)}, bf16[512,2048]{1,0:T(8,128)(2,1)}, bf16[512,704]{1,0:T(8,128)(2,1)}, bf16[512,704]{1,0:T(8,128)(2,1)}, bf16[51...) custom-call(s32[1]{0:T(128)} %bitcast.3.place_ref.seq_ref, ...), custom_call_target="tpu_custom_call" | custom-call | flops 7381975040 | bytes 17039360 | tf_op jit(solution)/shard_map/ffn_part/pallas_call | solution.py:623
  275.8 15.5 %ffn_part.3 = (bf16[512,2048]{1,0:T(8,128)(2,1)}, bf16[512,2048]{1,0:T(8,128)(2,1)}, bf16[512,704]{1,0:T(8,128)(2,1)}, bf16[512,704]{1,0:T(8,128)(2,1)}, bf16[51...) custom-call(s32[1]{0:T(128)} %bitcast.3.place_ref.seq_ref, ...), custom_call_target="tpu_custom_call" | custom-call | flops 7381975040 | bytes 17039360 | tf_op jit(solution)/shard_map/ffn_part/pallas_call | solution.py:623
  291.3 7.1 %collective-permute-done.26.refs_2_ = bf16[128,2048]{1,0:T(8,128)(2,1)S(1)} collective-permute-done((bf16[128,2048]{1,0:T(8,128)(2,1)}, bf16[128,2048]{1,0:T(8,128)(2,1)S(1)}, u32[]{:S(2)}, u32[]{:S(2)}) %collective-permute-start.26) | collective-permute-done | bytes 524320 | tf_op jit(solution)/shard_map/ppermute | solution.py:800
  321.4 7.5 %collective-permute-done.29 = bf16[128,2048]{1,0:T(8,128)(2,1)S(1)} collective-permute-done((bf16[128,2048]{1,0:T(8,128)(2,1)S(1)}, bf16[128,2048]{1,0:T(8,128)(2,1)S(1)}, u32[]{:S(2)}, u32[]{:S(2)}) %collective-permute-start.29) | collective-permute-done | bytes 524320 | tf_op jit(solution)/shard_map/ppermute | solution.py:800
  348.7 11.0 %collective-permute-done.38.refs_0_ = bf16[128,2048]{1,0:T(8,128)(2,1)S(1)} collective-permute-done((bf16[128,2048]{1,0:T(8,128)(2,1)}, bf16[128,2048]{1,0:T(8,128)(2,1)S(1)}, u32[]{:S(2)}, u32[]{:S(2)}) %collective-permute-start.38) | collective-permute-done | bytes 524320 | tf_op jit(solution)/shard_map/ppermute | solution.py:800
  370.1 9.5 %collective-permute-done.39.refs_1_ = bf16[128,2048]{1,0:T(8,128)(2,1)S(1)} collective-permute-done((bf16[128,2048]{1,0:T(8,128)(2,1)S(1)}, bf16[128,2048]{1,0:T(8,128)(2,1)S(1)}, u32[]{:S(2)}, u32[]{:S(2)}) %collective-permute-start.39) | collective-permute-done | bytes 524320 | tf_op jit(solution)/shard_map/ppermute | solution.py:800
  381.0 9.0 %finish_product.1 = bf16[1024,2048]{1,0:T(8,128)(2,1)} custom-call(s32[1]{0:T(128)} %bitcast.3.place_ref.seq_ref, bf16[512,704]{1,0:T(8,128)(2,1)} %get-tuple-element.204.refs_0_, bf16[512,704]{1,0:T(8,128)(2,1)} %get-tuple-element.205.refs_1_, bf16[8448,256]{1,0:T(8,128)(2,1)} %bitcast.17.near.refs_2_, bf16[8448,256]{1,0:T(8,128)(2,1)} %collective-permute-done.17.far.refs_3_), custom_call_target="tpu_custom_call" | custom-call | flops 2952790016 | bytes 12845056 | tf_op jit(solution)/shard_map/finish_product/pallas_call | solution.py:744
  391.0 11.2 %collective-permute-done.35.refs_1_ = bf16[128,2048]{1,0:T(8,128)(2,1)S(1)} collective-permute-done((bf16[128,2048]{1,0:T(8,128)(2,1)S(1)}, bf16[128,2048]{1,0:T(8,128)(2,1)S(1)}, u32[]{:S(2)}, u32[]{:S(2)}) %collective-permute-start.35) | collective-permute-done | bytes 524320 | tf_op jit(solution)/shard_map/ppermute | solution.py:800
  416.2 23.5 %delta_backward.1 = (bf16[512,784]{1,0:T(8,128)(2,1)}, bf16[512,784]{1,0:T(8,128)(2,1)}, f32[12,256]{1,0:T(8,128)}, f32[1,128]{1,0:T(1,128)}) custom-call(f32[16]{0:T(128)} %pad_maximum_fusion.8.reset_ref, s32[1]{0:T(128)} %bitcast.3.place_ref.seq_ref, f32[12,256]{1,0:T(8,128)} %constant_dynamic-slice_fusion.1.conv_ref, ...), custom_call_target="tpu_custom_call" | custom-call | tf_op jit(solution)/shard_map/delta_backward/pallas_call | solution.py:370
  452.5 9.0 %team_product.3 = (bf16[128,2048]{1,0:T(8,128)(2,1)}, bf16[128,2048]{1,0:T(8,128)(2,1)}, bf16[128,2048]{1,0:T(8,128)(2,1)}, bf16[128,2048]{1,0:T(8,128)(2,1)}, b...) custom-call(bf16[512,784]{1,0:T(8,128)(2,1)} %get-tuple-element.230., ...), custom_call_target="tpu_custom_call" | custom-call | flops 3288334336 | bytes 8454144 | tf_op jit(solution)/shard_map/team_product/pallas_call | solution.py:681
  483.3 21.4 %collective-permute-done.43 = bf16[128,2048]{1,0:T(8,128)(2,1)S(1)} collective-permute-done((bf16[128,2048]{1,0:T(8,128)(2,1)}, bf16[128,2048]{1,0:T(8,128)(2,1)S(1)}, u32[]{:S(2)}, u32[]{:S(2)}) %collective-permute-start.43) | collective-permute-done | bytes 524320 | tf_op jit(solution)/shard_map/ppermute | solution.py:800
  506.0 20.3 %collective-permute-done.48.refs_2_ = bf16[128,2048]{1,0:T(8,128)(2,1)} collective-permute-done((bf16[128,2048]{1,0:T(8,128)(2,1)}, bf16[128,2048]{1,0:T(8,128)(2,1)}, u32[]{:S(2)}, u32[]{:S(2)}) %collective-permute-start.48) | collective-permute-done | bytes 524320 | tf_op jit(solution)/shard_map/ppermute | solution.py:800
  532.4 11.1 %collective-permute-done.51.refs_4_ = bf16[128,2048]{1,0:T(8,128)(2,1)S(1)} collective-permute-done((bf16[128,2048]{1,0:T(8,128)(2,1)}, bf16[128,2048]{1,0:T(8,128)(2,1)S(1)}, u32[]{:S(2)}, u32[]{:S(2)}) %collective-permute-start.51) | collective-permute-done | bytes 524320 | tf_op jit(solution)/shard_map/ppermute | solution.py:800
  (371 shorter events, 263.3 us)
Async XLA Ops:
  29.5 51.7 %all-to-all-start = ((bf16[4,1040,256]{2,1,0:T(8,128)(2,1)}), bf16[4,1040,256]{2,1,0:T(8,128)(2,1)S(1)}, u32[]{:S(2)}, u32[]{:S(2)}) async-start(bf16[4,1040,256]{2,1,0:T(8,128)(2,1)} %bitcast.113), calls=%async_computation | async-start | bytes 4259840 | tf_op jit(solution)/shard_map/all_to_all | solution.py:853
  37.0 32.8 %collective-permute-start.5 = (bf16[128,2048]{1,0:T(8,128)(2,1)}, bf16[128,2048]{1,0:T(8,128)(2,1)}, u32[]{:S(2)}, u32[]{:S(2)}) collective-permute-start(bf16[128,2048]{1,0:T(8,128)(2,1)} %collective-permute-done.1.refs_0_), channel_id=1, source_target_pairs={{0,1},{1,0},{2,3},{3,2},{4,5},{5,4},{6,7},{7,6},{8,9},{9,8},{10,11... | collective-permute-start | bytes 1572872 | tf_op jit(solution)/shard_map/ppermute | solution.py:800
  106.8 115.9 %all-to-all-start.1 = ((bf16[4,2112,256]{2,1,0:T(8,128)(2,1)}), bf16[4,2112,256]{2,1,0:T(8,128)(2,1)}, u32[]{:S(2)}, u32[]{:S(2)}) async-start(bf16[4,2112,256]{2,1,0:T(8,128)(2,1)} %bitcast.112), calls=%async_computation.1 | async-start | bytes 8650752 | tf_op jit(solution)/shard_map/all_to_all | solution.py:853
  111.8 139.4 %all-gather.2.cloned.1.call-start = ((), (), s32[]{:S(2)}) async-start(), calls=%async_computation.5 | async-start | bytes 5242880 | tf_op jit(solution)/shard_map/all_gather | solution.py:962
  152.9 27.2 %collective-permute-start.15 = (bf16[128,2048]{1,0:T(8,128)(2,1)}, bf16[128,2048]{1,0:T(8,128)(2,1)S(1)}, u32[]{:S(2)}, u32[]{:S(2)}) collective-permute-start(bf16[128,2048]{1,0:T(8,128)(2,1)} %get-tuple-element.158), channel_id=1, source_target_pairs={{0,3},{1,2},{2,1},{3,0},{4,7},{5,6},{6,5},{7,4},{8,11},{9,10},{10,... | collective-permute-start | bytes 1572872 | tf_op jit(solution)/shard_map/ppermute | solution.py:800
  155.4 36.0 %collective-permute-start.14 = (bf16[128,2048]{1,0:T(8,128)(2,1)}, bf16[128,2048]{1,0:T(8,128)(2,1)S(1)}, u32[]{:S(2)}, u32[]{:S(2)}) collective-permute-start(bf16[128,2048]{1,0:T(8,128)(2,1)} %get-tuple-element.157), channel_id=1, source_target_pairs={{0,2},{1,3},{2,0},{3,1},{4,6},{5,7},{6,4},{7,5},{8,10},{9,11},{10,... | collective-permute-start | bytes 1572872 | tf_op jit(solution)/shard_map/ppermute | solution.py:800
  156.0 36.2 %collective-permute-start.13 = (bf16[128,2048]{1,0:T(8,128)(2,1)}, bf16[128,2048]{1,0:T(8,128)(2,1)S(1)}, u32[]{:S(2)}, u32[]{:S(2)}) collective-permute-start(bf16[128,2048]{1,0:T(8,128)(2,1)} %get-tuple-element.156), channel_id=1, source_target_pairs={{0,1},{1,0},{2,3},{3,2},{4,5},{5,4},{6,7},{7,6},{8,9},{9,8},{10,11... | collective-permute-start | bytes 1572872 | tf_op jit(solution)/shard_map/ppermute | solution.py:800
  156.5 46.9 %collective-permute-start.10 = (bf16[128,2048]{1,0:T(8,128)(2,1)}, bf16[128,2048]{1,0:T(8,128)(2,1)S(1)}, u32[]{:S(2)}, u32[]{:S(2)}) collective-permute-start(bf16[128,2048]{1,0:T(8,128)(2,1)} %get-tuple-element.152), channel_id=1, source_target_pairs={{0,1},{1,0},{2,3},{3,2},{4,5},{5,4},{6,7},{7,6},{8,9},{9,8},{10,11... | collective-permute-start | bytes 1572872 | tf_op jit(solution)/shard_map/ppermute | solution.py:800
  158.0 45.4 %collective-permute-start.11 = (bf16[128,2048]{1,0:T(8,128)(2,1)}, bf16[128,2048]{1,0:T(8,128)(2,1)S(1)}, u32[]{:S(2)}, u32[]{:S(2)}) collective-permute-start(bf16[128,2048]{1,0:T(8,128)(2,1)} %get-tuple-element.153), channel_id=1, source_target_pairs={{0,2},{1,3},{2,0},{3,1},{4,6},{5,7},{6,4},{7,5},{8,10},{9,11},{10,... | collective-permute-start | bytes 1572872 | tf_op jit(solution)/shard_map/ppermute | solution.py:800
  180.1 34.7 %collective-permute-start.12 = (bf16[128,2048]{1,0:T(8,128)(2,1)}, bf16[128,2048]{1,0:T(8,128)(2,1)S(1)}, u32[]{:S(2)}, u32[]{:S(2)}) collective-permute-start(bf16[128,2048]{1,0:T(8,128)(2,1)} %get-tuple-element.154), channel_id=1, source_target_pairs={{0,3},{1,2},{2,1},{3,0},{4,7},{5,6},{6,5},{7,4},{8,11},{9,10},{10,... | collective-permute-start | bytes 1572872 | tf_op jit(solution)/shard_map/ppermute | solution.py:800
  222.7 28.5 %collective-permute-start.17 = (bf16[8448,256]{1,0:T(8,128)(2,1)}, bf16[8448,256]{1,0:T(8,128)(2,1)}, u32[]{:S(2)}, u32[]{:S(2)}) collective-permute-start(bf16[8448,256]{1,0:T(8,128)(2,1)} %bitcast.17.near.refs_2_), channel_id=1, source_target_pairs={{0,4},{4,0},{8,12},{12,8},{16,20},{20,16},{24,28},{28,24},{1,5},{5... | collective-permute-start | bytes 12976136 | tf_op jit(solution)/shard_map/ppermute | solution.py:800
  237.3 29.3 %collective-permute-start.22 = (bf16[128,2048]{1,0:T(8,128)(2,1)S(1)}, bf16[128,2048]{1,0:T(8,128)(2,1)S(1)}, u32[]{:S(2)}, u32[]{:S(2)}) collective-permute-start(bf16[128,2048]{1,0:T(8,128)(2,1)S(1)} %collective-permute-done.21.refs_0_), channel_id=1, source_target_pairs={{0,1},{1,0},{2,3},{3,2},{4,5},{5,4},{6,7},{7,6},{8,9},{9,8},{10,11... | collective-permute-start | bytes 1572872 | tf_op jit(solution)/shard_map/ppermute | solution.py:800
  238.8 33.4 %collective-permute-start.23 = (bf16[128,2048]{1,0:T(8,128)(2,1)S(1)}, bf16[128,2048]{1,0:T(8,128)(2,1)S(1)}, u32[]{:S(2)}, u32[]{:S(2)}) collective-permute-start(bf16[128,2048]{1,0:T(8,128)(2,1)S(1)} %collective-permute-done.21.refs_0_), channel_id=1, source_target_pairs={{0,2},{1,3},{2,0},{3,1},{4,6},{5,7},{6,4},{7,5},{8,10},{9,11},{10,... | collective-permute-start | bytes 1572872 | tf_op jit(solution)/shard_map/ppermute | solution.py:800
  359.7 103.4 %all-to-all-start.2 = ((bf16[4,2112,256]{2,1,0:T(8,128)(2,1)}), bf16[4,2112,256]{2,1,0:T(8,128)(2,1)}, u32[]{:S(2)}, u32[]{:S(2)}) async-start(bf16[4,2112,256]{2,1,0:T(8,128)(2,1)} %bitcast.102), calls=%async_computation.3 | async-start | bytes 8650752 | tf_op jit(solution)/shard_map/all_to_all | solution.py:853
  364.7 165.5 %reduce-scatter.2.cloned.1.call-start = ((), (), s32[]{:S(2)}) async-start(), calls=%async_computation.6 | async-start | bytes 5242880 | tf_op jit(solution)/shard_map/reduce_scatter | solution.py:1036
  368.3 33.9 %collective-permute-start.35 = (bf16[128,2048]{1,0:T(8,128)(2,1)S(1)}, bf16[128,2048]{1,0:T(8,128)(2,1)S(1)}, u32[]{:S(2)}, u32[]{:S(2)}) collective-permute-start(bf16[128,2048]{1,0:T(8,128)(2,1)S(1)} %copy-done.34), channel_id=1, source_target_pairs={{0,1},{1,0},{2,3},{3,2},{4,5},{5,4},{6,7},{7,6},{8,9},{9,8},{10,11... | collective-permute-start | bytes 1572872 | tf_op jit(solution)/shard_map/ppermute | solution.py:800
  368.4 40.6 %collective-permute-start.36 = (bf16[128,2048]{1,0:T(8,128)(2,1)S(1)}, bf16[128,2048]{1,0:T(8,128)(2,1)}, u32[]{:S(2)}, u32[]{:S(2)}) collective-permute-start(bf16[128,2048]{1,0:T(8,128)(2,1)S(1)} %copy-done.34), channel_id=1, source_target_pairs={{0,2},{1,3},{2,0},{3,1},{4,6},{5,7},{6,4},{7,5},{8,10},{9,11},{10,... | collective-permute-start | bytes 1572872 | tf_op jit(solution)/shard_map/ppermute | solution.py:800
  379.7 29.3 %collective-permute-start.37 = (bf16[128,2048]{1,0:T(8,128)(2,1)S(1)}, bf16[128,2048]{1,0:T(8,128)(2,1)}, u32[]{:S(2)}, u32[]{:S(2)}) collective-permute-start(bf16[128,2048]{1,0:T(8,128)(2,1)S(1)} %copy-done.34), channel_id=1, source_target_pairs={{0,3},{1,2},{2,1},{3,0},{4,7},{5,6},{6,5},{7,4},{8,11},{9,10},{10,... | collective-permute-start | bytes 1572872 | tf_op jit(solution)/shard_map/ppermute | solution.py:800
  473.3 102.9 %all-to-all-start.3 = ((bf16[4,1040,256]{2,1,0:T(8,128)(2,1)}), bf16[4,1040,256]{2,1,0:T(8,128)(2,1)S(1)}, u32[]{:S(2)}, u32[]{:S(2)}) async-start(bf16[4,1040,256]{2,1,0:T(8,128)(2,1)} %bitcast.103), calls=%async_computation.4 | async-start | bytes 4259840 | tf_op jit(solution)/shard_map/all_to_all | solution.py:853
  478.2 26.6 %collective-permute-start.43 = (bf16[128,2048]{1,0:T(8,128)(2,1)}, bf16[128,2048]{1,0:T(8,128)(2,1)S(1)}, u32[]{:S(2)}, u32[]{:S(2)}) collective-permute-start(bf16[128,2048]{1,0:T(8,128)(2,1)} %get-tuple-element.234), channel_id=1, source_target_pairs={{0,2},{1,3},{2,0},{3,1},{4,6},{5,7},{6,4},{7,5},{8,10},{9,11},{10,... | collective-permute-start | bytes 1572872 | tf_op jit(solution)/shard_map/ppermute | solution.py:800
  478.3 26.4 %collective-permute-start.44 = (bf16[128,2048]{1,0:T(8,128)(2,1)}, bf16[128,2048]{1,0:T(8,128)(2,1)S(1)}, u32[]{:S(2)}, u32[]{:S(2)}) collective-permute-start(bf16[128,2048]{1,0:T(8,128)(2,1)} %get-tuple-element.235), channel_id=1, source_target_pairs={{0,3},{1,2},{2,1},{3,0},{4,7},{5,6},{6,5},{7,4},{8,11},{9,10},{10,... | collective-permute-start | bytes 1572872 | tf_op jit(solution)/shard_map/ppermute | solution.py:800
  479.8 26.2 %collective-permute-start.47 = (bf16[128,2048]{1,0:T(8,128)(2,1)}, bf16[128,2048]{1,0:T(8,128)(2,1)}, u32[]{:S(2)}, u32[]{:S(2)}) collective-permute-start(bf16[128,2048]{1,0:T(8,128)(2,1)} %get-tuple-element.240), channel_id=1, source_target_pairs={{0,1},{1,0},{2,3},{3,2},{4,5},{5,4},{6,7},{7,6},{8,9},{9,8},{10,11... | collective-permute-start | bytes 1572872 | tf_op jit(solution)/shard_map/ppermute | solution.py:800
  481.7 44.6 %collective-permute-start.48 = (bf16[128,2048]{1,0:T(8,128)(2,1)}, bf16[128,2048]{1,0:T(8,128)(2,1)}, u32[]{:S(2)}, u32[]{:S(2)}) collective-permute-start(bf16[128,2048]{1,0:T(8,128)(2,1)} %get-tuple-element.241), channel_id=1, source_target_pairs={{0,2},{1,3},{2,0},{3,1},{4,6},{5,7},{6,4},{7,5},{8,10},{9,11},{10,... | collective-permute-start | bytes 1572872 | tf_op jit(solution)/shard_map/ppermute | solution.py:800
  481.8 44.5 %collective-permute-start.49 = (bf16[128,2048]{1,0:T(8,128)(2,1)}, bf16[128,2048]{1,0:T(8,128)(2,1)}, u32[]{:S(2)}, u32[]{:S(2)}) collective-permute-start(bf16[128,2048]{1,0:T(8,128)(2,1)} %get-tuple-element.242), channel_id=1, source_target_pairs={{0,3},{1,2},{2,1},{3,0},{4,7},{5,6},{6,5},{7,4},{8,11},{9,10},{10,... | collective-permute-start | bytes 1572872 | tf_op jit(solution)/shard_map/ppermute | solution.py:800
  (108 other events, 1282.9 us)
Sparse Core Ops, SparseCore 0:
  115.1 77.6 all-gather.1
  416.3 55.6 reduce-scatter.1

commit v3 on v2

--- a/solution.py
+++ b/solution.py
@@ -113,6 +113,9 @@
     r, c_, same = tri_masks(rows)
     strict = same & (r > c_)
     incl = same & (r >= c_)
+
+    def local_pair(i, carry):
+        return local(2 * i + 1, local(2 * i, carry))
 
     def local(c, carry):
         start = row_start(place_ref, c, per)
@@ -142,7 +145,7 @@
         k_s[c] = k.astype(bf16)
         return carry
 
-    lax.fori_loop(0, blocks, local, 0)
+    lax.fori_loop(0, blocks // 2, local_pair, 0)
     state[...] = jnp.zeros_like(state)
     gain = gain_ref[...]
 
@@ -229,6 +232,9 @@
 
     def stack(some, start):
         return jnp.concatenate([some[g][pl.ds(start, SPAN), pl.ds(h * DH, DH)] for g, h in pairs], axis=0)
+
+    def local_pair(i, total):
+        return local(2 * i + 1, local(2 * i, total))
 
     def local(c, total):
         start = row_start(place_ref, c, per)
@@ -268,7 +274,7 @@
         kt_s[c] = got[:, DH:].astype(bf16)
         return total
 
-    dgain_ref[...] = lax.fori_loop(0, blocks, local, jnp.zeros((1, DH), f32))
+    dgain_ref[...] = lax.fori_loop(0, blocks // 2, local_pair, jnp.zeros((1, DH), f32))
     dstate[...] = jnp.zeros_like(dstate)
 
     def scan(i, carry):
@@ -421,11 +427,17 @@
     )(core, *arrays)
 
 
-def first_kernel(parts, core_ref, x_ref, gain_ref, cot_ref, live_ref, hidden_ref, d_ffo_ref):
-    x = x_ref[...].astype(f32)
-    scale = lax.rsqrt(jnp.mean(x * x, axis=-1, keepdims=True) + epsilon)
-    put_columns((x * scale * gain_ref[...]).astype(bf16), hidden_ref, core_ref[0], parts)
-    put_columns((cot_ref[...].astype(f32) * live_ref[...]).astype(bf16), d_ffo_ref, core_ref[0], parts)
+def first_kernel(parts, core_ref, gain_ref, x_ref, y_ref, hidden_ref, twin_ref):
+    for rows_ref, out_ref in ((x_ref, hidden_ref), (y_ref, twin_ref)):
+        x = rows_ref[...].astype(f32)
+        scale = lax.rsqrt(jnp.mean(x * x, axis=-1, keepdims=True) + epsilon)
+        put_columns((x * scale * gain_ref[...]).astype(bf16), out_ref, core_ref[0], parts)
+
+
+def cot_kernel(parts, core_ref, x_ref, live_ref, y_ref, live_twin_ref, out_ref):
+    rows = x_ref.shape[0]
+    put_columns((x_ref[...].astype(f32) * live_ref[...]).astype(bf16), out_ref.at[:rows], core_ref[0], parts)
+    put_columns((y_ref[...].astype(f32) * live_twin_ref[...]).astype(bf16), out_ref.at[rows:], core_ref[0], parts)
 
 
 def middle_kernel(parts, core_ref, x_ref, gain_ref, *refs):
@@ -453,8 +465,8 @@
 
 
 def last_kernel(parts, core_ref, x_ref, gain_ref, d_resid_ref, *refs):
-    pieces, (grad_ref, d_gain_ref) = refs[:-2], refs[-2:]
-    d_norm, d_gain_ref[...] = norm_back(
+    pieces, grad_ref = refs[:-1], refs[-1]
+    d_norm, _ = norm_back(
         x_ref[...].astype(f32), gain_ref[...], column_sum(pieces, core_ref[0], parts)
     )
     grad_ref[...] = d_resid_ref[...] + d_norm
@@ -639,16 +651,19 @@
     )(seq, *packs, cots, *seconds)
 
 
-def product_kernel(halves, spans, steps, fold, stride, count, *refs):
+def product_kernel(halves, spans, steps, fold, stride, count, gains, *refs):
     terms = len(spans)
     lefts = refs[: halves * terms]
     near_ref, far_ref = refs[halves * terms : halves * terms + 2]
-    outs = refs[halves * terms + 2 :]
+    unit_refs = refs[halves * terms + 2 : halves * terms + 2 + gains]
+    outs = refs[halves * terms + 2 + gains :]
     step = pl.program_id(0)
     rows = outs[0].shape[0]
     depth = near_ref.shape[1]
 
     def run(pack):
+        if gains:
+            outs[-1][...] = jnp.zeros_like(outs[-1])
         for half in range(halves):
             for k in range(fold):
                 total = None
@@ -656,8 +671,12 @@
                     at = k * stride + first
                     part = lax.dot_general(left[...], pack[at : at + units, :], NN, preferred_element_type=f32)
                     total = part if total is None else total + part
+                cols = slice(k * depth, (k + 1) * depth)
+                if gains:
+                    unit = unit_refs[half][:, cols].astype(f32)
+                    outs[-1][:, cols] = outs[-1][:, cols] + jnp.sum(total * unit, axis=0, keepdims=True)
                 for j in range(count):
-                    outs[half * count + j][:, k * depth : (k + 1) * depth] = total[j * rows : (j + 1) * rows].astype(bf16)
+                    outs[half * count + j][:, cols] = total[j * rows : (j + 1) * rows].astype(bf16)
 
     @pl.when(step < steps)
     def _():
@@ -668,7 +687,7 @@
         run(far_ref)
 
 
-def team_product(lines, lefts, spans, packs, count):
+def team_product(lines, lefts, spans, packs, count, units=()):
     halves = len(lefts)
     flat = [left for half in lefts for left in half]
     tokens = flat[0].shape[0]
@@ -677,25 +696,30 @@
     depth = packs[0].shape[1]
     steps = lines // fold
     rows = tokens // count
-    units = sum(n for _, n in spans)
+    inner = sum(n for _, n in spans)
+    tile = pl.BlockSpec((tokens, fold * depth), lambda t: (0, t))
+    total = pl.BlockSpec((1, fold * depth), lambda t: (0, t))
     out = pl.pallas_call(
-        functools.partial(product_kernel, halves, spans, steps, fold, stride, count),
+        functools.partial(product_kernel, halves, spans, steps, fold, stride, count, len(units)),
         grid=(2 * steps,),
         in_specs=[pl.BlockSpec(left.shape, lambda t: (0, 0)) for left in flat]
         + [
             pl.BlockSpec((fold * stride, depth), lambda t: (jnp.minimum(t, steps - 1), 0)),
             pl.BlockSpec((fold * stride, depth), lambda t: (jnp.maximum(t - steps, 0), 0)),
-        ],
-        out_specs=[pl.BlockSpec((rows, fold * depth), lambda t: (0, t))] * (count * halves),
-        out_shape=[jax.ShapeDtypeStruct((rows, 2 * lines * depth), bf16)] * (count * halves),
+        ]
+        + [tile] * len(units),
+        out_specs=[pl.BlockSpec((rows, fold * depth), lambda t: (0, t))] * (count * halves)
+        + [total] * (len(units) > 0),
+        out_shape=[jax.ShapeDtypeStruct((rows, 2 * lines * depth), bf16)] * (count * halves)
+        + [jax.ShapeDtypeStruct((1, 2 * lines * depth), f32)] * (len(units) > 0),
         cost_estimate=pl.CostEstimate(
-            flops=4 * halves * tokens * units * lines * depth,
+            flops=4 * halves * tokens * inner * lines * depth,
             bytes_accessed=4 * stride * lines * depth + 4 * halves * tokens * lines * depth,
             transcendentals=0,
         ),
         name="team_product",
-    )(*flat, *packs)
-    return [out[half * count : (half + 1) * count] for half in range(halves)]
+    )(*flat, *packs, *units)
+    return [out[half * count : (half + 1) * count] for half in range(halves)] + list(out[halves * count :])
 
 
 def finish_product_kernel(halves, first, units, steps, fold, stride, count, seq_ref, *refs):
@@ -877,11 +901,13 @@
     return values
 
 
-def all_sum(values):
-    seq_parts, dp_parts = lax.axis_size("seq"), lax.axis_size("dp")
-    values = summed([values] + [swap(values, "seq", k) for k in range(1, seq_parts)])
-    values = summed([values] + [swap(values, "dp", k) for k in range(2, dp_parts, 2)])
+def chip_line_sum(values):
+    values = summed([values] + [swap(values, "dp", k) for k in range(2, lax.axis_size("dp"), 2)])
     return values + swap(values, "dp", 1)
+
+
+def group_sum(values):
+    return summed([values] + [swap(values, "seq", k) for k in range(1, lax.axis_size("seq"))])
 
 
 def shards(
@@ -937,30 +963,41 @@
     gain_one = attn_norm_gain.astype(f32)[None]
     gain_two = ffn_norm_gain.astype(f32)[None]
 
-    hidden_own, d_ffo_own = on_core(
-        functools.partial(first_kernel, dp_parts), "first_norm", (rows_b16,) * 2, core, tokens, gain_one, cotangent, live_col
-    )
-    hidden_twin = twin_rows(hidden_own)
-    reset_twin = twin_rows(reset_own)
+    tokens_twin = twin_rows(tokens)
+    reset_twin = twin_rows(jnp.concatenate([reset_own, live]))
+    cot_twin = twin_rows(cotangent)
+    reset_twin, live_twin = reset_twin[: reset_own.shape[0]], reset_twin[reset_own.shape[0] :]
+    live_twin_col = lax.dynamic_slice_in_dim(live_twin, seq_place * local, local)[:, None]
+    hidden_own, hidden_twin = on_core(
+        functools.partial(first_kernel, dp_parts), "first_norm", (rows_b16,) * 2, core, gain_one, tokens, tokens_twin
+    )
     pad = jnp.zeros((extra - heads, w_strength.shape[0]), bf16)
     strength_t = w_strength.T
     strength_rows = jnp.concatenate([strength_t[:heads], pad, strength_t[heads:], pad], axis=0)
     mix_in = line_pack(
-        (w_query.T, w_key.T, w_value.T, strength_rows, w_output), lines, hidden_twin, reset_twin
+        (w_query.T, w_key.T, w_value.T, strength_rows, w_output), lines, tokens_twin, reset_twin, cot_twin
     )
     near_hidden = seq_relayed(hidden_own, True)
     far_hidden = seq_relayed(hidden_twin, False)
     reset = jnp.concatenate([reset_own, reset_twin])
+    late_cot = on_core(
+        functools.partial(cot_kernel, dp_parts),
+        "live_rows",
+        (jax.ShapeDtypeStruct((2 * local, model), bf16),),
+        core,
+        cotangent,
+        live_col,
+        cot_twin,
+        live_twin_col,
+    )[0]
     mix_near = after(mix_in, tuple(near_hidden), tuple(far_hidden))
-    mix_packs = (mix_near, twin(mix_near))
+    mix_packs = (mix_near, twin(after(mix_near, late_cot)))
     o_first = 3 * width + extra
 
-    d_ffo_twin = twin_rows(after(d_ffo_own, mix_packs[1]))
+    ffn_in = line_pack((w_gate.T, w_up.T, w_down), lines, mix_packs[1])
+    cots_all = lax.all_gather(after(late_cot, mix_near), "seq", axis=0, tiled=True)
     hidden_0, x_0, logit_0 = mix_product(lines, near_hidden, mix_packs, 3 * width, extra)
-    late_cot = after(jnp.concatenate([d_ffo_own, d_ffo_twin], axis=0), x_0)
-    ffn_in = line_pack((w_gate.T, w_up.T, w_down), lines, late_cot)
-    cots_all = lax.all_gather(late_cot, "seq", axis=0, tiled=True)
-    hidden_1, x_1, logit_1 = mix_product(lines, after(tuple(far_hidden), late_cot), mix_packs, 3 * width, extra)
+    hidden_1, x_1, logit_1 = mix_product(lines, far_hidden, mix_packs, 3 * width, extra)
     normed, mixed, kept = delta_forward(per, reset, place, (x_0, x_1), (logit_0, logit_1), taps, gain_h)
     o_span = ((o_first, width),)
     far_chunks, near_chunks = team_product(lines, ((normed[1],), (normed[0],)), o_span, mix_packs, seq_parts)
@@ -1033,7 +1070,7 @@
     near_branch = after(tuple(near_branch), far_branch)
     b_0, d_normed_0 = branch_back(lines, near_branch, mix_packs, o_first, width)
     b_1, d_normed_1 = branch_back(lines, far_branch, mix_packs, o_first, width)
-    final_sums = lax.psum_scatter(after(final, d_normed_0, d_normed_1), "seq", scatter_dimension=0, tiled=True)
+    final_sums = lax.psum_scatter(after(final, tuple(far_branch), tuple(near_branch)), "seq", scatter_dimension=0, tiled=True)
     (d_x_0, d_x_1), d_taps, grad_head = delta_backward(
         per,
         reset,
@@ -1046,19 +1083,28 @@
         (d_normed_0, d_normed_1),
         kept,
     )
+    x_span = ((0, 3 * width + extra),)
+    far_chunks, near_chunks, gain_sum = team_product(
+        lines, ((d_x_1,), (d_x_0,)), x_span, mix_packs, seq_parts, (hidden_1, hidden_0)
+    )
+    far_got = returned(far_chunks)
+    near_got = returned(near_chunks)
+    d_x_0, d_x_1 = after((d_x_0, d_x_1), gain_sum)
     x_kept, x_sent = kept_sum((d_x_0, d_x_1), (hidden_0, hidden_1))
     x_got = twin(x_sent)
     o_kept, o_sent = kept_sum(normed, after((b_0, b_1), x_sent))
     o_got = twin(o_sent)
-    d_x_0, d_x_1 = lax.optimization_barrier((d_x_0, d_x_1, x_sent, x_kept, o_sent, o_kept))[:2]
-    x_span = ((0, 3 * width + extra),)
-    far_chunks, near_chunks = team_product(lines, ((d_x_1,), (d_x_0,)), x_span, mix_packs, seq_parts)
-    far_got = returned(far_chunks)
-    near_got = returned(near_chunks)
     grad_gate, grad_up, grad_down = line_total(
         ffn_back, lines, ((0, units), (units, units), (2 * units, units))
     )
-    mix_cut = line_cut(lines, (x_kept, o_kept), after((x_got, o_got), near_chunks[0], grad_gate, grad_up, grad_down))
+    by_core = gain_sum.reshape(2, lines, -1)
+    by_core = jnp.where((dp_place & 1) == 1, by_core[::-1], by_core)
+    grad_gain_one = by_core.transpose(1, 0, 2).reshape(1, model) / gain_one
+    early = jnp.zeros((3 * CONV, model), f32)
+    early = lax.dynamic_update_slice_in_dim(early, d_taps, seq_place * full_width + odd * width, 1)
+    gains = jnp.concatenate([grad_gain_one, grad_gain_two, early], axis=0).reshape(-1, DH)
+    gains = chip_line_sum(jnp.concatenate([gains, grad_head], axis=0))
+    mix_cut = line_cut(lines, (x_kept, o_kept), after((x_got, o_got), gains, tuple(far_got), grad_gate, grad_up, grad_down))
     mix_back = line_exchange(mix_cut)
     mix_spans = (
         (0, width),
@@ -1082,21 +1128,18 @@
         final_twin,
     )[0]
     back = after(back, grad_query)
-    input_grad, grad_gain_one = on_core(
+    input_grad = on_core(
         functools.partial(last_kernel, dp_parts),
         "last_norm",
-        (rows_f32, gain_f32),
+        (rows_f32,),
         core,
         tokens,
         gain_one,
         d_resid,
         *near_got,
         back,
-    )
-    early = jnp.zeros((3 * CONV, model), f32)
-    early = lax.dynamic_update_slice_in_dim(early, d_taps, seq_place * full_width + odd * width, 1)
-    gains = jnp.concatenate([grad_gain_one, grad_gain_two, early], axis=0).reshape(-1, DH)
-    gains = all_sum(after(jnp.concatenate([gains, grad_head], axis=0), final_twin))
+    )[0]
+    gains = group_sum(after(gains, far_sum))
     wide = gains[:-1].reshape(-1, model)
     conv_grad = lax.dynamic_slice_in_dim(wide[2:], seq_place * full_width, full_width, 1)
     conv_grad = conv_grad.reshape(3, CONV, full_width)

time: 599 us -> 577 us (0.963)
  waiting for transfers between devices: 251 us -> 226 us
  local copies, waits for them, and re-layouts: 42.3 us -> 48.3 us
    ppermute x59, waiting for transfers between devices: 239 us -> 217 us  [swap(): return lax.ppermute(values, axis, [(i, i ^ mask) for i in range(size)])]
    unnamed x174 -> x182, local copies, waits for them, and re-layouts: 33.8 us -> 37.3 us
    pallas_call x5 -> x6, Pallas kernels: 17.1 us -> 19.7 us  [on_core(): pl.pallas_call(kernel, out_shape=shapes, in_specs=[smem] + [vmem] * len(a...]
  transfers between devices with their start and end apart: 65 -> 65, of which waited for: 31 -> 31; matrix products, arithmetic and copies ran while one was open for 12% -> 13% of each run, Pallas kernels for 25% -> 26%
where the time goes in v3:
time: 577 us; the launch traced here: 567 us
  waiting for transfers between devices  226 us (39%)
  Pallas kernels  151 us (26%)
  starting transfers between devices  81.5 us (14%)
  local copies, waits for them, and re-layouts  48.3 us (8%)
  matrix products  26.1 us (5%)
  other arithmetic  18.1 us (3%)
  between operations  16.2 us (3%)
    ppermute x59, waiting for transfers between devices, swap(): return lax.ppermute(values, axis, [(i, i ^ mask) for i in range(size)])  217 us
    ppermute x59, starting transfers between devices, swap(): return lax.ppermute(values, axis, [(i, i ^ mask) for i in range(size)])  62.7 us
    unnamed x182, local copies, waits for them, and re-layouts  37.3 us
    pallas_call x2, Pallas kernels, ffn_part(): pl.pallas_call(functools.partial(ffn_kernel, lines, count, half), out_sha...  31.1 us
    dot_general x20, matrix products, dot(): lax.dot_general(left, right, dims, preferred_element_type=f32).astype(kind)  26.1 us
    pallas_call x1, Pallas kernels, delta_forward(): pl.pallas_call(functools.partial(fwd_kernel, per, groups), out_shape=(sha...  24.9 us
    pallas_call x1, Pallas kernels, delta_backward(): pl.pallas_call(functools.partial(bwd_kernel, per, groups), out_shape=(sha...  21.6 us
    pallas_call x6, Pallas kernels, on_core(): pl.pallas_call(kernel, out_shape=shapes, in_specs=[smem] + [vmem] * len(a...  19.7 us
  transfers between devices with their start and end apart: 65, of which 31 were waited for; matrix products, arithmetic and copies ran while one was open for 13% of the time, Pallas kernels for 26%

profile of v3, /device:TPU:0, one launch (start us, length us, event | category | flops | bytes accessed | tf_op | source)
XLA Modules:
  0.0 567.2 jit_solution(8620829975560413691)
XLA Ops:
  17.6 8.7 %collective-permute-done.1.y_ref = bf16[128,2048]{1,0:T(8,128)(2,1)} collective-permute-done((bf16[128,2048]{1,0:T(8,128)(2,1)}, bf16[128,2048]{1,0:T(8,128)(2,1)}, u32[]{:S(2)}, u32[]{:S(2)}) %collective-permute-start.1) | collective-permute-done | bytes 524320 | tf_op jit(solution)/shard_map/ppermute | solution.py:824
  26.3 9.8 %collective-permute-done.2.y_ref = bf16[128,2048]{1,0:T(8,128)(2,1)} collective-permute-done((bf16[128,2048]{1,0:T(8,128)(2,1)}, bf16[128,2048]{1,0:T(8,128)(2,1)}, u32[]{:S(2)}, u32[]{:S(2)}) %collective-permute-start.2) | collective-permute-done | bytes 524320 | tf_op jit(solution)/shard_map/ppermute | solution.py:824
  71.2 8.3 %collective-permute-done.5.refs_3_ = bf16[128,2048]{1,0:T(8,128)(2,1)} collective-permute-done((bf16[128,2048]{1,0:T(8,128)(2,1)}, bf16[128,2048]{1,0:T(8,128)(2,1)}, u32[]{:S(2)}, u32[]{:S(2)}) %collective-permute-start.5) | collective-permute-done | bytes 524320 | tf_op jit(solution)/shard_map/ppermute | solution.py:824
  79.5 8.3 %all-to-all-done = bf16[4,1040,256]{2,1,0:T(8,128)(2,1)S(1)} async-done(((bf16[4,1040,256]{2,1,0:T(8,128)(2,1)}), bf16[4,1040,256]{2,1,0:T(8,128)(2,1)S(1)}, u32[]{:S(2)}, u32[]{:S(2)}) %all-to-all-start) | async-done | bytes 2129952 | tf_op jit(solution)/shard_map/all_to_all | solution.py:877
  117.3 24.9 %delta_forward.1 = (bf16[512,256]{1,0:T(8,128)(2,1)}, bf16[512,256]{1,0:T(8,128)(2,1)}, bf16[512,256]{1,0:T(8,128)(2,1)}, bf16[512,256]{1,0:T(8,128)(2,1)}, bf16...) custom-call(f32[16]{0:T(128)} %pad_maximum_fusion.7.reset_ref, ...), custom_call_target="tpu_custom_call" | custom-call | tf_op jit(solution)/shard_map/delta_forward/pallas_call | solution.py:193
  154.8 18.3 %collective-permute-done.15 = bf16[128,2048]{1,0:T(8,128)(2,1)S(1)} collective-permute-done((bf16[128,2048]{1,0:T(8,128)(2,1)}, bf16[128,2048]{1,0:T(8,128)(2,1)S(1)}, u32[]{:S(2)}, u32[]{:S(2)}) %collective-permute-start.15) | collective-permute-done | bytes 524320 | tf_op jit(solution)/shard_map/ppermute | solution.py:824
  173.4 10.0 %collective-permute-done.14 = bf16[128,2048]{1,0:T(8,128)(2,1)S(1)} collective-permute-done((bf16[128,2048]{1,0:T(8,128)(2,1)}, bf16[128,2048]{1,0:T(8,128)(2,1)S(1)}, u32[]{:S(2)}, u32[]{:S(2)}) %collective-permute-start.14) | collective-permute-done | bytes 524320 | tf_op jit(solution)/shard_map/ppermute | solution.py:824
  187.1 7.6 %collective-permute-done.10.refs_1_ = bf16[128,2048]{1,0:T(8,128)(2,1)S(1)} collective-permute-done((bf16[128,2048]{1,0:T(8,128)(2,1)}, bf16[128,2048]{1,0:T(8,128)(2,1)S(1)}, u32[]{:S(2)}, u32[]{:S(2)}) %collective-permute-start.10) | collective-permute-done | bytes 524320 | tf_op jit(solution)/shard_map/ppermute | solution.py:824
  194.7 11.9 %collective-permute-done.12.refs_3_ = bf16[128,2048]{1,0:T(8,128)(2,1)S(1)} collective-permute-done((bf16[128,2048]{1,0:T(8,128)(2,1)}, bf16[128,2048]{1,0:T(8,128)(2,1)S(1)}, u32[]{:S(2)}, u32[]{:S(2)}) %collective-permute-start.12) | collective-permute-done | bytes 524320 | tf_op jit(solution)/shard_map/ppermute | solution.py:824
  219.2 10.9 %collective-permute-done.21.refs_0_ = bf16[128,2048]{1,0:T(8,128)(2,1)S(1)} collective-permute-done((bf16[128,2048]{1,0:T(8,128)(2,1)}, bf16[128,2048]{1,0:T(8,128)(2,1)S(1)}, u32[]{:S(2)}, u32[]{:S(2)}) %collective-permute-start.21) | collective-permute-done | bytes 524320 | tf_op jit(solution)/shard_map/ppermute | solution.py:824
  233.1 9.5 %collective-permute-done.19.refs_2_ = bf16[128,2048]{1,0:T(8,128)(2,1)S(1)} collective-permute-done((bf16[128,2048]{1,0:T(8,128)(2,1)}, bf16[128,2048]{1,0:T(8,128)(2,1)S(1)}, u32[]{:S(2)}, u32[]{:S(2)}) %collective-permute-start.19) | collective-permute-done | bytes 524320 | tf_op jit(solution)/shard_map/ppermute | solution.py:824
  244.0 15.3 %ffn_part.2 = (bf16[512,2048]{1,0:T(8,128)(2,1)}, bf16[512,2048]{1,0:T(8,128)(2,1)}, bf16[512,704]{1,0:T(8,128)(2,1)}, bf16[512,704]{1,0:T(8,128)(2,1)}, bf16[51...) custom-call(s32[1]{0:T(128)} %bitcast.4.place_ref.seq_ref, ...), custom_call_target="tpu_custom_call" | custom-call | flops 7381975040 | bytes 17039360 | tf_op jit(solution)/shard_map/ffn_part/pallas_call | solution.py:635
  269.3 15.8 %ffn_part.3 = (bf16[512,2048]{1,0:T(8,128)(2,1)}, bf16[512,2048]{1,0:T(8,128)(2,1)}, bf16[512,704]{1,0:T(8,128)(2,1)}, bf16[512,704]{1,0:T(8,128)(2,1)}, bf16[51...) custom-call(s32[1]{0:T(128)} %bitcast.4.place_ref.seq_ref, ...), custom_call_target="tpu_custom_call" | custom-call | flops 7381975040 | bytes 17039360 | tf_op jit(solution)/shard_map/ffn_part/pallas_call | solution.py:635
  314.6 7.7 %collective-permute-done.29 = bf16[128,2048]{1,0:T(8,128)(2,1)S(1)} collective-permute-done((bf16[128,2048]{1,0:T(8,128)(2,1)S(1)}, bf16[128,2048]{1,0:T(8,128)(2,1)S(1)}, u32[]{:S(2)}, u32[]{:S(2)}) %collective-permute-start.29) | collective-permute-done | bytes 524320 | tf_op jit(solution)/shard_map/ppermute | solution.py:824
  342.3 11.0 %collective-permute-done.35.refs_0_ = bf16[128,2048]{1,0:T(8,128)(2,1)S(1)} collective-permute-done((bf16[128,2048]{1,0:T(8,128)(2,1)}, bf16[128,2048]{1,0:T(8,128)(2,1)S(1)}, u32[]{:S(2)}, u32[]{:S(2)}) %collective-permute-start.35) | collective-permute-done | bytes 524320 | tf_op jit(solution)/shard_map/ppermute | solution.py:824
  363.7 9.5 %collective-permute-done.36.refs_1_ = bf16[128,2048]{1,0:T(8,128)(2,1)S(1)} collective-permute-done((bf16[128,2048]{1,0:T(8,128)(2,1)S(1)}, bf16[128,2048]{1,0:T(8,128)(2,1)S(1)}, u32[]{:S(2)}, u32[]{:S(2)}) %collective-permute-start.36) | collective-permute-done | bytes 524320 | tf_op jit(solution)/shard_map/ppermute | solution.py:824
  374.5 8.8 %finish_product.1 = bf16[1024,2048]{1,0:T(8,128)(2,1)} custom-call(s32[1]{0:T(128)} %bitcast.4.place_ref.seq_ref, bf16[512,704]{1,0:T(8,128)(2,1)} %get-tuple-element.195.refs_0_, bf16[512,704]{1,0:T(8,128)(2,1)} %get-tuple-element.196.refs_1_, bf16[8448,256]{1,0:T(8,128)(2,1)} %bitcast.18.near.refs_2_, bf16[8448,256]{1,0:T(8,128)(2,1)} %collective-permute-done.17.far.refs_3_), custom_call_target="tpu_custom_call" | custom-call | flops 2952790016 | bytes 12845056 | tf_op jit(solution)/shard_map/finish_product/pallas_call | solution.py:768
  384.6 11.2 %collective-permute-done.39.refs_1_ = bf16[128,2048]{1,0:T(8,128)(2,1)S(1)} collective-permute-done((bf16[128,2048]{1,0:T(8,128)(2,1)S(1)}, bf16[128,2048]{1,0:T(8,128)(2,1)S(1)}, u32[]{:S(2)}, u32[]{:S(2)}) %collective-permute-start.39) | collective-permute-done | bytes 524320 | tf_op jit(solution)/shard_map/ppermute | solution.py:824
  395.8 6.8 %collective-permute-done.40.refs_2_ = bf16[128,2048]{1,0:T(8,128)(2,1)} collective-permute-done((bf16[128,2048]{1,0:T(8,128)(2,1)S(1)}, bf16[128,2048]{1,0:T(8,128)(2,1)}, u32[]{:S(2)}, u32[]{:S(2)}) %collective-permute-start.40) | collective-permute-done | bytes 524320 | tf_op jit(solution)/shard_map/ppermute | solution.py:824
  409.8 21.6 %delta_backward.1 = (bf16[512,784]{1,0:T(8,128)(2,1)}, bf16[512,784]{1,0:T(8,128)(2,1)}, f32[12,256]{1,0:T(8,128)}, f32[1,128]{1,0:T(1,128)}) custom-call(f32[16]{0:T(128)} %pad_maximum_fusion.7.reset_ref, s32[1]{0:T(128)} %bitcast.4.place_ref.seq_ref, f32[12,256]{1,0:T(8,128)} %constant_dynamic-slice_fusion.1.conv_ref, ...), custom_call_target="tpu_custom_call" | custom-call | tf_op jit(solution)/shard_map/delta_backward/pallas_call | solution.py:376
  431.4 9.5 %team_product.3 = (bf16[128,2048]{1,0:T(8,128)(2,1)}, bf16[128,2048]{1,0:T(8,128)(2,1)}, bf16[128,2048]{1,0:T(8,128)(2,1)}, bf16[128,2048]{1,0:T(8,128)(2,1)}, b...) custom-call(bf16[512,784]{1,0:T(8,128)(2,1)} %get-tuple-element.223., ...), custom_call_target="tpu_custom_call" | custom-call | flops 3288334336 | bytes 8454144 | tf_op jit(solution)/shard_map/team_product/pallas_call | solution.py:702
  473.1 10.9 %collective-permute-done.43 = bf16[128,2048]{1,0:T(8,128)(2,1)S(1)} collective-permute-done((bf16[128,2048]{1,0:T(8,128)(2,1)}, bf16[128,2048]{1,0:T(8,128)(2,1)S(1)}, u32[]{:S(2)}, u32[]{:S(2)}) %collective-permute-start.43) | collective-permute-done | bytes 524320 | tf_op jit(solution)/shard_map/ppermute | solution.py:824
  497.2 11.7 %collective-permute-done.51.refs_1_ = bf16[128,2048]{1,0:T(8,128)(2,1)} collective-permute-done((bf16[128,2048]{1,0:T(8,128)(2,1)}, bf16[128,2048]{1,0:T(8,128)(2,1)}, u32[]{:S(2)}, u32[]{:S(2)}) %collective-permute-start.51) | collective-permute-done | bytes 524320 | tf_op jit(solution)/shard_map/ppermute | solution.py:824
  508.9 8.6 %collective-permute-done.52.refs_2_ = bf16[128,2048]{1,0:T(8,128)(2,1)} collective-permute-done((bf16[128,2048]{1,0:T(8,128)(2,1)}, bf16[128,2048]{1,0:T(8,128)(2,1)}, u32[]{:S(2)}, u32[]{:S(2)}) %collective-permute-start.52) | collective-permute-done | bytes 524320 | tf_op jit(solution)/shard_map/ppermute | solution.py:824
  (392 shorter events, 274.3 us)
Async XLA Ops:
  11.3 24.9 %collective-permute-start.2 = (bf16[128,2048]{1,0:T(8,128)(2,1)}, bf16[128,2048]{1,0:T(8,128)(2,1)}, u32[]{:S(2)}, u32[]{:S(2)}) collective-permute-start(bf16[128,2048]{1,0:T(8,128)(2,1)} %cot_ref.1), channel_id=1, source_target_pairs={{0,8},{4,12},{8,0},{12,4},{16,24},{20,28},{24,16},{28,20},{1,9},{5... | collective-permute-start | bytes 1572872 | tf_op jit(solution)/shard_map/ppermute | solution.py:824
  36.1 51.7 %all-to-all-start = ((bf16[4,1040,256]{2,1,0:T(8,128)(2,1)}), bf16[4,1040,256]{2,1,0:T(8,128)(2,1)S(1)}, u32[]{:S(2)}, u32[]{:S(2)}) async-start(bf16[4,1040,256]{2,1,0:T(8,128)(2,1)} %bitcast.119), calls=%async_computation | async-start | bytes 4259840 | tf_op jit(solution)/shard_map/all_to_all | solution.py:877
  98.6 116.9 %all-to-all-start.1 = ((bf16[4,2112,256]{2,1,0:T(8,128)(2,1)}), bf16[4,2112,256]{2,1,0:T(8,128)(2,1)}, u32[]{:S(2)}, u32[]{:S(2)}) async-start(bf16[4,2112,256]{2,1,0:T(8,128)(2,1)} %bitcast.17), calls=%async_computation.1 | async-start | bytes 8650752 | tf_op jit(solution)/shard_map/all_to_all | solution.py:877
  103.6 140.4 %all-gather.2.cloned.1.call-start = ((), (), s32[]{:S(2)}) async-start(), calls=%async_computation.5 | async-start | bytes 5242880 | tf_op jit(solution)/shard_map/all_gather | solution.py:998
  148.1 25.0 %collective-permute-start.15 = (bf16[128,2048]{1,0:T(8,128)(2,1)}, bf16[128,2048]{1,0:T(8,128)(2,1)S(1)}, u32[]{:S(2)}, u32[]{:S(2)}) collective-permute-start(bf16[128,2048]{1,0:T(8,128)(2,1)} %get-tuple-element.148), channel_id=1, source_target_pairs={{0,3},{1,2},{2,1},{3,0},{4,7},{5,6},{6,5},{7,4},{8,11},{9,10},{10,... | collective-permute-start | bytes 1572872 | tf_op jit(solution)/shard_map/ppermute | solution.py:824
  150.8 32.6 %collective-permute-start.14 = (bf16[128,2048]{1,0:T(8,128)(2,1)}, bf16[128,2048]{1,0:T(8,128)(2,1)S(1)}, u32[]{:S(2)}, u32[]{:S(2)}) collective-permute-start(bf16[128,2048]{1,0:T(8,128)(2,1)} %get-tuple-element.147), channel_id=1, source_target_pairs={{0,2},{1,3},{2,0},{3,1},{4,6},{5,7},{6,4},{7,5},{8,10},{9,11},{10,... | collective-permute-start | bytes 1572872 | tf_op jit(solution)/shard_map/ppermute | solution.py:824
  151.3 32.2 %collective-permute-start.13 = (bf16[128,2048]{1,0:T(8,128)(2,1)}, bf16[128,2048]{1,0:T(8,128)(2,1)S(1)}, u32[]{:S(2)}, u32[]{:S(2)}) collective-permute-start(bf16[128,2048]{1,0:T(8,128)(2,1)} %get-tuple-element.146), channel_id=1, source_target_pairs={{0,1},{1,0},{2,3},{3,2},{4,5},{5,4},{6,7},{7,6},{8,9},{9,8},{10,11... | collective-permute-start | bytes 1572872 | tf_op jit(solution)/shard_map/ppermute | solution.py:824
  151.7 43.0 %collective-permute-start.10 = (bf16[128,2048]{1,0:T(8,128)(2,1)}, bf16[128,2048]{1,0:T(8,128)(2,1)S(1)}, u32[]{:S(2)}, u32[]{:S(2)}) collective-permute-start(bf16[128,2048]{1,0:T(8,128)(2,1)} %get-tuple-element.142), channel_id=1, source_target_pairs={{0,1},{1,0},{2,3},{3,2},{4,5},{5,4},{6,7},{7,6},{8,9},{9,8},{10,11... | collective-permute-start | bytes 1572872 | tf_op jit(solution)/shard_map/ppermute | solution.py:824
  153.3 41.4 %collective-permute-start.11 = (bf16[128,2048]{1,0:T(8,128)(2,1)}, bf16[128,2048]{1,0:T(8,128)(2,1)S(1)}, u32[]{:S(2)}, u32[]{:S(2)}) collective-permute-start(bf16[128,2048]{1,0:T(8,128)(2,1)} %get-tuple-element.143), channel_id=1, source_target_pairs={{0,2},{1,3},{2,0},{3,1},{4,6},{5,7},{6,4},{7,5},{8,10},{9,11},{10,... | collective-permute-start | bytes 1572872 | tf_op jit(solution)/shard_map/ppermute | solution.py:824
  173.1 33.5 %collective-permute-start.12 = (bf16[128,2048]{1,0:T(8,128)(2,1)}, bf16[128,2048]{1,0:T(8,128)(2,1)S(1)}, u32[]{:S(2)}, u32[]{:S(2)}) collective-permute-start(bf16[128,2048]{1,0:T(8,128)(2,1)} %get-tuple-element.144), channel_id=1, source_target_pairs={{0,3},{1,2},{2,1},{3,0},{4,7},{5,6},{6,5},{7,4},{8,11},{9,10},{10,... | collective-permute-start | bytes 1572872 | tf_op jit(solution)/shard_map/ppermute | solution.py:824
  184.8 26.4 %collective-permute-start.16 = (bf16[128,2048]{1,0:T(8,128)(2,1)S(1)}, bf16[128,2048]{1,0:T(8,128)(2,1)S(1)}, u32[]{:S(2)}, u32[]{:S(2)}) collective-permute-start(bf16[128,2048]{1,0:T(8,128)(2,1)S(1)} %add_convert_fusion.10), channel_id=1, source_target_pairs={{0,8},{4,12},{8,0},{12,4},{16,24},{20,28},{24,16},{28,20},{1,9},{5... | collective-permute-start | bytes 1572872 | tf_op jit(solution)/shard_map/ppermute | solution.py:824
  215.5 28.5 %collective-permute-start.17 = (bf16[8448,256]{1,0:T(8,128)(2,1)}, bf16[8448,256]{1,0:T(8,128)(2,1)}, u32[]{:S(2)}, u32[]{:S(2)}) collective-permute-start(bf16[8448,256]{1,0:T(8,128)(2,1)} %bitcast.18.near.refs_2_), channel_id=1, source_target_pairs={{0,4},{4,0},{8,12},{12,8},{16,20},{20,16},{24,28},{28,24},{1,5},{5... | collective-permute-start | bytes 12976136 | tf_op jit(solution)/shard_map/ppermute | solution.py:824
  217.2 25.4 %collective-permute-start.19 = (bf16[128,2048]{1,0:T(8,128)(2,1)}, bf16[128,2048]{1,0:T(8,128)(2,1)S(1)}, u32[]{:S(2)}, u32[]{:S(2)}) collective-permute-start(bf16[128,2048]{1,0:T(8,128)(2,1)} %get-tuple-element.151.refs_0_), channel_id=1, source_target_pairs={{0,2},{1,3},{2,0},{3,1},{4,6},{5,7},{6,4},{7,5},{8,10},{9,11},{10,... | collective-permute-start | bytes 1572872 | tf_op jit(solution)/shard_map/ppermute | solution.py:824
  218.7 25.3 %collective-permute-start.20 = (bf16[128,2048]{1,0:T(8,128)(2,1)}, bf16[128,2048]{1,0:T(8,128)(2,1)}, u32[]{:S(2)}, u32[]{:S(2)}) collective-permute-start(bf16[128,2048]{1,0:T(8,128)(2,1)} %get-tuple-element.151.refs_0_), channel_id=1, source_target_pairs={{0,3},{1,2},{2,1},{3,0},{4,7},{5,6},{6,5},{7,4},{8,11},{9,10},{10,... | collective-permute-start | bytes 1572872 | tf_op jit(solution)/shard_map/ppermute | solution.py:824
  230.1 29.3 %collective-permute-start.22 = (bf16[128,2048]{1,0:T(8,128)(2,1)S(1)}, bf16[128,2048]{1,0:T(8,128)(2,1)S(1)}, u32[]{:S(2)}, u32[]{:S(2)}) collective-permute-start(bf16[128,2048]{1,0:T(8,128)(2,1)S(1)} %collective-permute-done.21.refs_0_), channel_id=1, source_target_pairs={{0,1},{1,0},{2,3},{3,2},{4,5},{5,4},{6,7},{7,6},{8,9},{9,8},{10,11... | collective-permute-start | bytes 1572872 | tf_op jit(solution)/shard_map/ppermute | solution.py:824
  231.6 33.4 %collective-permute-start.23 = (bf16[128,2048]{1,0:T(8,128)(2,1)S(1)}, bf16[128,2048]{1,0:T(8,128)(2,1)S(1)}, u32[]{:S(2)}, u32[]{:S(2)}) collective-permute-start(bf16[128,2048]{1,0:T(8,128)(2,1)S(1)} %collective-permute-done.21.refs_0_), channel_id=1, source_target_pairs={{0,2},{1,3},{2,0},{3,1},{4,6},{5,7},{6,4},{7,5},{8,10},{9,11},{10,... | collective-permute-start | bytes 1572872 | tf_op jit(solution)/shard_map/ppermute | solution.py:824
  353.3 110.6 %all-to-all-start.2 = ((bf16[4,2112,256]{2,1,0:T(8,128)(2,1)}), bf16[4,2112,256]{2,1,0:T(8,128)(2,1)}, u32[]{:S(2)}, u32[]{:S(2)}) async-start(bf16[4,2112,256]{2,1,0:T(8,128)(2,1)} %bitcast.109), calls=%async_computation.3 | async-start | bytes 8650752 | tf_op jit(solution)/shard_map/all_to_all | solution.py:877
  358.3 176.4 %reduce-scatter.2.cloned.1.call-start = ((), (), s32[]{:S(2)}) async-start(), calls=%async_computation.6 | async-start | bytes 5242880 | tf_op jit(solution)/shard_map/reduce_scatter | solution.py:1073
  358.4 26.1 %collective-permute-start.37 = (bf16[128,2048]{1,0:T(8,128)(2,1)S(1)}, bf16[128,2048]{1,0:T(8,128)(2,1)S(1)}, u32[]{:S(2)}, u32[]{:S(2)}) collective-permute-start(bf16[128,2048]{1,0:T(8,128)(2,1)S(1)} %collective-permute-done.35.refs_0_), channel_id=1, source_target_pairs={{0,2},{1,3},{2,0},{3,1},{4,6},{5,7},{6,4},{7,5},{8,10},{9,11},{10,... | collective-permute-start | bytes 1572872 | tf_op jit(solution)/shard_map/ppermute | solution.py:824
  361.9 33.9 %collective-permute-start.39 = (bf16[128,2048]{1,0:T(8,128)(2,1)S(1)}, bf16[128,2048]{1,0:T(8,128)(2,1)S(1)}, u32[]{:S(2)}, u32[]{:S(2)}) collective-permute-start(bf16[128,2048]{1,0:T(8,128)(2,1)S(1)} %copy-done.39), channel_id=1, source_target_pairs={{0,1},{1,0},{2,3},{3,2},{4,5},{5,4},{6,7},{7,6},{8,9},{9,8},{10,11... | collective-permute-start | bytes 1572872 | tf_op jit(solution)/shard_map/ppermute | solution.py:824
  362.0 40.6 %collective-permute-start.40 = (bf16[128,2048]{1,0:T(8,128)(2,1)S(1)}, bf16[128,2048]{1,0:T(8,128)(2,1)}, u32[]{:S(2)}, u32[]{:S(2)}) collective-permute-start(bf16[128,2048]{1,0:T(8,128)(2,1)S(1)} %copy-done.39), channel_id=1, source_target_pairs={{0,2},{1,3},{2,0},{3,1},{4,6},{5,7},{6,4},{7,5},{8,10},{9,11},{10,... | collective-permute-start | bytes 1572872 | tf_op jit(solution)/shard_map/ppermute | solution.py:824
  373.3 29.4 %collective-permute-start.41 = (bf16[128,2048]{1,0:T(8,128)(2,1)S(1)}, bf16[128,2048]{1,0:T(8,128)(2,1)}, u32[]{:S(2)}, u32[]{:S(2)}) collective-permute-start(bf16[128,2048]{1,0:T(8,128)(2,1)S(1)} %copy-done.39), channel_id=1, source_target_pairs={{0,3},{1,2},{2,1},{3,0},{4,7},{5,6},{6,5},{7,4},{8,11},{9,10},{10,... | collective-permute-start | bytes 1572872 | tf_op jit(solution)/shard_map/ppermute | solution.py:824
  451.3 32.8 %collective-permute-start.45 = (bf16[784,1024]{1,0:T(8,128)(2,1)}, bf16[784,1024]{1,0:T(8,128)(2,1)}, u32[]{:S(2)}, u32[]{:S(2)}) collective-permute-start(bf16[784,1024]{1,0:T(8,128)(2,1)} %add_convert_fusion), channel_id=1, source_target_pairs={{0,4},{4,0},{8,12},{12,8},{16,20},{20,16},{24,28},{28,24},{1,5},{5... | collective-permute-start | bytes 4816904 | tf_op jit(solution)/shard_map/ppermute | solution.py:824
  488.9 66.1 %all-to-all-start.3 = ((bf16[4,1040,256]{2,1,0:T(8,128)(2,1)}), bf16[4,1040,256]{2,1,0:T(8,128)(2,1)S(1)}, u32[]{:S(2)}, u32[]{:S(2)}) async-start(bf16[4,1040,256]{2,1,0:T(8,128)(2,1)} %bitcast.110), calls=%async_computation.4 | async-start | bytes 4259840 | tf_op jit(solution)/shard_map/all_to_all | solution.py:877
  (112 other events, 1331.6 us)
Sparse Core Ops, SparseCore 0:
  106.8 73.3 all-gather.1
  402.8 52.9 reduce-scatter.1

commit v4 on v3

--- a/solution.py
+++ b/solution.py
@@ -965,7 +965,6 @@
 
     tokens_twin = twin_rows(tokens)
     reset_twin = twin_rows(jnp.concatenate([reset_own, live]))
-    cot_twin = twin_rows(cotangent)
     reset_twin, live_twin = reset_twin[: reset_own.shape[0]], reset_twin[reset_own.shape[0] :]
     live_twin_col = lax.dynamic_slice_in_dim(live_twin, seq_place * local, local)[:, None]
     hidden_own, hidden_twin = on_core(
@@ -975,11 +974,12 @@
     strength_t = w_strength.T
     strength_rows = jnp.concatenate([strength_t[:heads], pad, strength_t[heads:], pad], axis=0)
     mix_in = line_pack(
-        (w_query.T, w_key.T, w_value.T, strength_rows, w_output), lines, tokens_twin, reset_twin, cot_twin
+        (w_query.T, w_key.T, w_value.T, strength_rows, w_output), lines, tokens_twin, reset_twin
     )
     near_hidden = seq_relayed(hidden_own, True)
     far_hidden = seq_relayed(hidden_twin, False)
     reset = jnp.concatenate([reset_own, reset_twin])
+    cot_twin = twin_rows(after(cotangent, tuple(far_hidden[:2])))
     late_cot = on_core(
         functools.partial(cot_kernel, dp_parts),
         "live_rows",
@@ -1064,13 +1064,13 @@
     far_branch = seq_pieces(d_branch_twin)
     ffn_back = line_exchange(after(ffn_cut, d_branch_twin))
     final = finish_product(
-        lines, place, after((act_0, act_1), d_branch_own), (2 * units, units), ffn_packs, seq_parts
-    )
-    far_branch = after(tuple(far_branch), final)
-    near_branch = after(tuple(near_branch), far_branch)
-    b_0, d_normed_0 = branch_back(lines, near_branch, mix_packs, o_first, width)
+        lines, place, after((act_0, act_1), tuple(near_branch)), (2 * units, units), ffn_packs, seq_parts
+    )
+    far_pieces = tuple(far_branch)
+    far_branch = after(far_pieces, final)
+    b_0, d_normed_0 = branch_back(lines, after(tuple(near_branch), final), mix_packs, o_first, width)
     b_1, d_normed_1 = branch_back(lines, far_branch, mix_packs, o_first, width)
-    final_sums = lax.psum_scatter(after(final, tuple(far_branch), tuple(near_branch)), "seq", scatter_dimension=0, tiled=True)
+    final_sums = lax.psum_scatter(after(final, far_pieces, tuple(near_branch)), "seq", scatter_dimension=0, tiled=True)
     (d_x_0, d_x_1), d_taps, grad_head = delta_backward(
         per,
         reset,

time: 577 us -> 567 us (0.983)
  waiting for transfers between devices: 226 us -> 214 us
    all_to_all x4, waiting for transfers between devices: 8.33 us -> 0.67 us  [line_exchange(): lax.all_to_all(values, 'dp', 0, 0, tiled=True, axis_index_groups=groups)]
  transfers between devices with their start and end apart: 65 -> 65, of which waited for: 31 -> 30; matrix products, arithmetic and copies ran while one was open for 13% -> 13% of each run, Pallas kernels for 26% -> 26%
where the time goes in v4:
time: 567 us; the launch traced here: 557 us
  waiting for transfers between devices  214 us (38%)
  Pallas kernels  152 us (27%)
  starting transfers between devices  82.3 us (15%)
  local copies, waits for them, and re-layouts  48.3 us (9%)
  matrix products  26.1 us (5%)
  other arithmetic  18.1 us (3%)
  between operations  16.2 us (3%)
    ppermute x59, waiting for transfers between devices, swap(): return lax.ppermute(values, axis, [(i, i ^ mask) for i in range(size)])  214 us
    ppermute x59, starting transfers between devices, swap(): return lax.ppermute(values, axis, [(i, i ^ mask) for i in range(size)])  62.6 us
    unnamed x182, local copies, waits for them, and re-layouts  37.3 us
    pallas_call x2, Pallas kernels, ffn_part(): pl.pallas_call(functools.partial(ffn_kernel, lines, count, half), out_sha...  31.1 us
    dot_general x20, matrix products, dot(): lax.dot_general(left, right, dims, preferred_element_type=f32).astype(kind)  26.1 us
    pallas_call x1, Pallas kernels, delta_forward(): pl.pallas_call(functools.partial(fwd_kernel, per, groups), out_shape=(sha...  24.9 us
    pallas_call x1, Pallas kernels, delta_backward(): pl.pallas_call(functools.partial(bwd_kernel, per, groups), out_shape=(sha...  21.6 us
    pallas_call x6, Pallas kernels, on_core(): pl.pallas_call(kernel, out_shape=shapes, in_specs=[smem] + [vmem] * len(a...  19.7 us
  transfers between devices with their start and end apart: 65, of which 30 were waited for; matrix products, arithmetic and copies ran while one was open for 13% of the time, Pallas kernels for 26%

profile of v4, /device:TPU:0, one launch (start us, length us, event | category | flops | bytes accessed | tf_op | source)
XLA Modules:
  0.0 557.2 jit_solution(5454001434092943647)
XLA Ops:
  15.7 9.2 %collective-permute-done.1.y_ref = bf16[128,2048]{1,0:T(8,128)(2,1)} collective-permute-done((bf16[128,2048]{1,0:T(8,128)(2,1)}, bf16[128,2048]{1,0:T(8,128)(2,1)}, u32[]{:S(2)}, u32[]{:S(2)}) %collective-permute-start.1) | collective-permute-done | bytes 524320 | tf_op jit(solution)/shard_map/ppermute | solution.py:824
  49.3 6.6 %collective-permute-done.2.refs_1_ = bf16[128,2048]{1,0:T(8,128)(2,1)} collective-permute-done((bf16[128,2048]{1,0:T(8,128)(2,1)}, bf16[128,2048]{1,0:T(8,128)(2,1)}, u32[]{:S(2)}, u32[]{:S(2)}) %collective-permute-start.2) | collective-permute-done | bytes 524320 | tf_op jit(solution)/shard_map/ppermute | solution.py:824
  62.3 11.1 %collective-permute-done.8.y_ref = bf16[128,2048]{1,0:T(8,128)(2,1)} collective-permute-done((bf16[128,2048]{1,0:T(8,128)(2,1)S(1)}, bf16[128,2048]{1,0:T(8,128)(2,1)}, u32[]{:S(2)}, u32[]{:S(2)}) %collective-permute-start.8) | collective-permute-done | bytes 524320 | tf_op jit(solution)/shard_map/ppermute | solution.py:824
  106.8 24.9 %delta_forward.1 = (bf16[512,256]{1,0:T(8,128)(2,1)}, bf16[512,256]{1,0:T(8,128)(2,1)}, bf16[512,256]{1,0:T(8,128)(2,1)}, bf16[512,256]{1,0:T(8,128)(2,1)}, bf16...) custom-call(f32[16]{0:T(128)} %pad_maximum_fusion.7.reset_ref, ...), custom_call_target="tpu_custom_call" | custom-call | tf_op jit(solution)/shard_map/delta_forward/pallas_call | solution.py:193
  144.4 18.7 %collective-permute-done.15 = bf16[128,2048]{1,0:T(8,128)(2,1)S(1)} collective-permute-done((bf16[128,2048]{1,0:T(8,128)(2,1)}, bf16[128,2048]{1,0:T(8,128)(2,1)S(1)}, u32[]{:S(2)}, u32[]{:S(2)}) %collective-permute-start.15) | collective-permute-done | bytes 524320 | tf_op jit(solution)/shard_map/ppermute | solution.py:824
  163.5 9.8 %collective-permute-done.14 = bf16[128,2048]{1,0:T(8,128)(2,1)S(1)} collective-permute-done((bf16[128,2048]{1,0:T(8,128)(2,1)}, bf16[128,2048]{1,0:T(8,128)(2,1)S(1)}, u32[]{:S(2)}, u32[]{:S(2)}) %collective-permute-start.14) | collective-permute-done | bytes 524320 | tf_op jit(solution)/shard_map/ppermute | solution.py:824
  177.0 7.7 %collective-permute-done.10.refs_1_ = bf16[128,2048]{1,0:T(8,128)(2,1)S(1)} collective-permute-done((bf16[128,2048]{1,0:T(8,128)(2,1)}, bf16[128,2048]{1,0:T(8,128)(2,1)S(1)}, u32[]{:S(2)}, u32[]{:S(2)}) %collective-permute-start.10) | collective-permute-done | bytes 524320 | tf_op jit(solution)/shard_map/ppermute | solution.py:824
  184.7 11.6 %collective-permute-done.12.refs_3_ = bf16[128,2048]{1,0:T(8,128)(2,1)S(1)} collective-permute-done((bf16[128,2048]{1,0:T(8,128)(2,1)}, bf16[128,2048]{1,0:T(8,128)(2,1)S(1)}, u32[]{:S(2)}, u32[]{:S(2)}) %collective-permute-start.12) | collective-permute-done | bytes 524320 | tf_op jit(solution)/shard_map/ppermute | solution.py:824
  209.1 10.9 %collective-permute-done.21.refs_0_ = bf16[128,2048]{1,0:T(8,128)(2,1)S(1)} collective-permute-done((bf16[128,2048]{1,0:T(8,128)(2,1)}, bf16[128,2048]{1,0:T(8,128)(2,1)S(1)}, u32[]{:S(2)}, u32[]{:S(2)}) %collective-permute-start.21) | collective-permute-done | bytes 524320 | tf_op jit(solution)/shard_map/ppermute | solution.py:824
  223.1 9.5 %collective-permute-done.19.refs_2_ = bf16[128,2048]{1,0:T(8,128)(2,1)S(1)} collective-permute-done((bf16[128,2048]{1,0:T(8,128)(2,1)}, bf16[128,2048]{1,0:T(8,128)(2,1)S(1)}, u32[]{:S(2)}, u32[]{:S(2)}) %collective-permute-start.19) | collective-permute-done | bytes 524320 | tf_op jit(solution)/shard_map/ppermute | solution.py:824
  234.0 15.3 %ffn_part.2 = (bf16[512,2048]{1,0:T(8,128)(2,1)}, bf16[512,2048]{1,0:T(8,128)(2,1)}, bf16[512,704]{1,0:T(8,128)(2,1)}, bf16[512,704]{1,0:T(8,128)(2,1)}, bf16[51...) custom-call(s32[1]{0:T(128)} %bitcast.4.place_ref.seq_ref, ...), custom_call_target="tpu_custom_call" | custom-call | flops 7381975040 | bytes 17039360 | tf_op jit(solution)/shard_map/ffn_part/pallas_call | solution.py:635
  259.3 15.8 %ffn_part.3 = (bf16[512,2048]{1,0:T(8,128)(2,1)}, bf16[512,2048]{1,0:T(8,128)(2,1)}, bf16[512,704]{1,0:T(8,128)(2,1)}, bf16[512,704]{1,0:T(8,128)(2,1)}, bf16[51...) custom-call(s32[1]{0:T(128)} %bitcast.4.place_ref.seq_ref, ...), custom_call_target="tpu_custom_call" | custom-call | flops 7381975040 | bytes 17039360 | tf_op jit(solution)/shard_map/ffn_part/pallas_call | solution.py:635
  304.6 7.7 %collective-permute-done.29 = bf16[128,2048]{1,0:T(8,128)(2,1)S(1)} collective-permute-done((bf16[128,2048]{1,0:T(8,128)(2,1)S(1)}, bf16[128,2048]{1,0:T(8,128)(2,1)S(1)}, u32[]{:S(2)}, u32[]{:S(2)}) %collective-permute-start.29) | collective-permute-done | bytes 524320 | tf_op jit(solution)/shard_map/ppermute | solution.py:824
  319.8 6.6 %line_cut.2 = bf16[8448,256]{1,0:T(8,128)(2,1)} custom-call(bf16[704,1024]{1,0:T(8,128)(2,1)} %add_convert_fusion.4.refs_0_, bf16[704,1024]{1,0:T(8,128)(2,1)} %add_convert_fusion.3.refs_1_, bf16[704,1024]{1,0:T(8,128)(2,1)} %add_convert_fusion.2.refs_2_, bf16[704,1024]{1,0:T(8,128)(2,1)} %copy-done.27, bf16[704,1024]{1,0:T(8,128)(2,1)} %copy-done.28, ...), custom_call_target="tpu_custom_call" | custom-call | tf_op jit(solution)/shard_map/line_cut/pallas_call | solution.py:799
  332.2 11.0 %collective-permute-done.38.refs_0_ = bf16[128,2048]{1,0:T(8,128)(2,1)S(1)} collective-permute-done((bf16[128,2048]{1,0:T(8,128)(2,1)}, bf16[128,2048]{1,0:T(8,128)(2,1)S(1)}, u32[]{:S(2)}, u32[]{:S(2)}) %collective-permute-start.38) | collective-permute-done | bytes 524320 | tf_op jit(solution)/shard_map/ppermute | solution.py:824
  353.6 9.6 %collective-permute-done.35.refs_1_ = bf16[128,2048]{1,0:T(8,128)(2,1)S(1)} collective-permute-done((bf16[128,2048]{1,0:T(8,128)(2,1)S(1)}, bf16[128,2048]{1,0:T(8,128)(2,1)S(1)}, u32[]{:S(2)}, u32[]{:S(2)}) %collective-permute-start.35) | collective-permute-done | bytes 524320 | tf_op jit(solution)/shard_map/ppermute | solution.py:824
  364.5 10.1 %collective-permute-done.36.refs_2_ = bf16[128,2048]{1,0:T(8,128)(2,1)S(1)} collective-permute-done((bf16[128,2048]{1,0:T(8,128)(2,1)S(1)}, bf16[128,2048]{1,0:T(8,128)(2,1)S(1)}, u32[]{:S(2)}, u32[]{:S(2)}) %collective-permute-start.36) | collective-permute-done | bytes 524320 | tf_op jit(solution)/shard_map/ppermute | solution.py:824
  374.5 9.2 %finish_product.1 = bf16[1024,2048]{1,0:T(8,128)(2,1)} custom-call(s32[1]{0:T(128)} %bitcast.4.place_ref.seq_ref, bf16[512,704]{1,0:T(8,128)(2,1)} %get-tuple-element.197.refs_0_, bf16[512,704]{1,0:T(8,128)(2,1)} %get-tuple-element.198.refs_1_, bf16[8448,256]{1,0:T(8,128)(2,1)} %bitcast.18.near.refs_2_, bf16[8448,256]{1,0:T(8,128)(2,1)} %collective-permute-done.17.far.refs_3_), custom_call_target="tpu_custom_call" | custom-call | flops 2952790016 | bytes 12845056 | tf_op jit(solution)/shard_map/finish_product/pallas_call | solution.py:768
  385.7 6.8 %collective-permute-done.40.refs_2_ = bf16[128,2048]{1,0:T(8,128)(2,1)} collective-permute-done((bf16[128,2048]{1,0:T(8,128)(2,1)S(1)}, bf16[128,2048]{1,0:T(8,128)(2,1)}, u32[]{:S(2)}, u32[]{:S(2)}) %collective-permute-start.40) | collective-permute-done | bytes 524320 | tf_op jit(solution)/shard_map/ppermute | solution.py:824
  399.7 21.6 %delta_backward.1 = (bf16[512,784]{1,0:T(8,128)(2,1)}, bf16[512,784]{1,0:T(8,128)(2,1)}, f32[12,256]{1,0:T(8,128)}, f32[1,128]{1,0:T(1,128)}) custom-call(f32[16]{0:T(128)} %pad_maximum_fusion.7.reset_ref, s32[1]{0:T(128)} %bitcast.4.place_ref.seq_ref, f32[12,256]{1,0:T(8,128)} %constant_dynamic-slice_fusion.1.conv_ref, ...), custom_call_target="tpu_custom_call" | custom-call | tf_op jit(solution)/shard_map/delta_backward/pallas_call | solution.py:376
  421.4 9.5 %team_product.3 = (bf16[128,2048]{1,0:T(8,128)(2,1)}, bf16[128,2048]{1,0:T(8,128)(2,1)}, bf16[128,2048]{1,0:T(8,128)(2,1)}, bf16[128,2048]{1,0:T(8,128)(2,1)}, b...) custom-call(bf16[512,784]{1,0:T(8,128)(2,1)} %get-tuple-element.225., ...), custom_call_target="tpu_custom_call" | custom-call | flops 3288334336 | bytes 8454144 | tf_op jit(solution)/shard_map/team_product/pallas_call | solution.py:702
  463.1 10.9 %collective-permute-done.43 = bf16[128,2048]{1,0:T(8,128)(2,1)S(1)} collective-permute-done((bf16[128,2048]{1,0:T(8,128)(2,1)}, bf16[128,2048]{1,0:T(8,128)(2,1)S(1)}, u32[]{:S(2)}, u32[]{:S(2)}) %collective-permute-start.43) | collective-permute-done | bytes 524320 | tf_op jit(solution)/shard_map/ppermute | solution.py:824
  487.1 11.7 %collective-permute-done.51.refs_1_ = bf16[128,2048]{1,0:T(8,128)(2,1)} collective-permute-done((bf16[128,2048]{1,0:T(8,128)(2,1)}, bf16[128,2048]{1,0:T(8,128)(2,1)}, u32[]{:S(2)}, u32[]{:S(2)}) %collective-permute-start.51) | collective-permute-done | bytes 524320 | tf_op jit(solution)/shard_map/ppermute | solution.py:824
  498.8 8.6 %collective-permute-done.52.refs_2_ = bf16[128,2048]{1,0:T(8,128)(2,1)} collective-permute-done((bf16[128,2048]{1,0:T(8,128)(2,1)}, bf16[128,2048]{1,0:T(8,128)(2,1)}, u32[]{:S(2)}, u32[]{:S(2)}) %collective-permute-start.52) | collective-permute-done | bytes 524320 | tf_op jit(solution)/shard_map/ppermute | solution.py:824
  (392 shorter events, 266.6 us)
Async XLA Ops:
  24.9 51.7 %all-to-all-start = ((bf16[4,1040,256]{2,1,0:T(8,128)(2,1)}), bf16[4,1040,256]{2,1,0:T(8,128)(2,1)S(1)}, u32[]{:S(2)}, u32[]{:S(2)}) async-start(bf16[4,1040,256]{2,1,0:T(8,128)(2,1)} %bitcast.119), calls=%async_computation | async-start | bytes 4259840 | tf_op jit(solution)/shard_map/all_to_all | solution.py:877
  40.7 35.2 %collective-permute-start.3 = (bf16[128,2048]{1,0:T(8,128)(2,1)}, bf16[128,2048]{1,0:T(8,128)(2,1)}, u32[]{:S(2)}, u32[]{:S(2)}) collective-permute-start(bf16[128,2048]{1,0:T(8,128)(2,1)} %get-tuple-element.132.refs_0_), channel_id=1, source_target_pairs={{0,2},{1,3},{2,0},{3,1},{4,6},{5,7},{6,4},{7,5},{8,10},{9,11},{10,... | collective-permute-start | bytes 1572872 | tf_op jit(solution)/shard_map/ppermute | solution.py:824
  47.3 26.1 %collective-permute-start.8 = (bf16[128,2048]{1,0:T(8,128)(2,1)S(1)}, bf16[128,2048]{1,0:T(8,128)(2,1)}, u32[]{:S(2)}, u32[]{:S(2)}) collective-permute-start(bf16[128,2048]{1,0:T(8,128)(2,1)S(1)} %copy-done.21), channel_id=1, source_target_pairs={{0,8},{4,12},{8,0},{12,4},{16,24},{20,28},{24,16},{28,20},{1,9},{5... | collective-permute-start | bytes 1572872 | tf_op jit(solution)/shard_map/ppermute | solution.py:824
  87.3 118.1 %all-to-all-start.1 = ((bf16[4,2112,256]{2,1,0:T(8,128)(2,1)}), bf16[4,2112,256]{2,1,0:T(8,128)(2,1)}, u32[]{:S(2)}, u32[]{:S(2)}) async-start(bf16[4,2112,256]{2,1,0:T(8,128)(2,1)} %bitcast.17), calls=%async_computation.1 | async-start | bytes 8650752 | tf_op jit(solution)/shard_map/all_to_all | solution.py:877
  93.2 140.8 %all-gather.2.cloned.1.call-start = ((), (), s32[]{:S(2)}) async-start(), calls=%async_computation.5 | async-start | bytes 5242880 | tf_op jit(solution)/shard_map/all_gather | solution.py:998
  137.7 25.4 %collective-permute-start.15 = (bf16[128,2048]{1,0:T(8,128)(2,1)}, bf16[128,2048]{1,0:T(8,128)(2,1)S(1)}, u32[]{:S(2)}, u32[]{:S(2)}) collective-permute-start(bf16[128,2048]{1,0:T(8,128)(2,1)} %get-tuple-element.150), channel_id=1, source_target_pairs={{0,3},{1,2},{2,1},{3,0},{4,7},{5,6},{6,5},{7,4},{8,11},{9,10},{10,... | collective-permute-start | bytes 1572872 | tf_op jit(solution)/shard_map/ppermute | solution.py:824
  140.4 32.9 %collective-permute-start.14 = (bf16[128,2048]{1,0:T(8,128)(2,1)}, bf16[128,2048]{1,0:T(8,128)(2,1)S(1)}, u32[]{:S(2)}, u32[]{:S(2)}) collective-permute-start(bf16[128,2048]{1,0:T(8,128)(2,1)} %get-tuple-element.149), channel_id=1, source_target_pairs={{0,2},{1,3},{2,0},{3,1},{4,6},{5,7},{6,4},{7,5},{8,10},{9,11},{10,... | collective-permute-start | bytes 1572872 | tf_op jit(solution)/shard_map/ppermute | solution.py:824
  140.9 32.6 %collective-permute-start.13 = (bf16[128,2048]{1,0:T(8,128)(2,1)}, bf16[128,2048]{1,0:T(8,128)(2,1)S(1)}, u32[]{:S(2)}, u32[]{:S(2)}) collective-permute-start(bf16[128,2048]{1,0:T(8,128)(2,1)} %get-tuple-element.148), channel_id=1, source_target_pairs={{0,1},{1,0},{2,3},{3,2},{4,5},{5,4},{6,7},{7,6},{8,9},{9,8},{10,11... | collective-permute-start | bytes 1572872 | tf_op jit(solution)/shard_map/ppermute | solution.py:824
  141.3 43.5 %collective-permute-start.10 = (bf16[128,2048]{1,0:T(8,128)(2,1)}, bf16[128,2048]{1,0:T(8,128)(2,1)S(1)}, u32[]{:S(2)}, u32[]{:S(2)}) collective-permute-start(bf16[128,2048]{1,0:T(8,128)(2,1)} %get-tuple-element.144), channel_id=1, source_target_pairs={{0,1},{1,0},{2,3},{3,2},{4,5},{5,4},{6,7},{7,6},{8,9},{9,8},{10,11... | collective-permute-start | bytes 1572872 | tf_op jit(solution)/shard_map/ppermute | solution.py:824
  142.9 41.8 %collective-permute-start.11 = (bf16[128,2048]{1,0:T(8,128)(2,1)}, bf16[128,2048]{1,0:T(8,128)(2,1)S(1)}, u32[]{:S(2)}, u32[]{:S(2)}) collective-permute-start(bf16[128,2048]{1,0:T(8,128)(2,1)} %get-tuple-element.145), channel_id=1, source_target_pairs={{0,2},{1,3},{2,0},{3,1},{4,6},{5,7},{6,4},{7,5},{8,10},{9,11},{10,... | collective-permute-start | bytes 1572872 | tf_op jit(solution)/shard_map/ppermute | solution.py:824
  163.1 33.2 %collective-permute-start.12 = (bf16[128,2048]{1,0:T(8,128)(2,1)}, bf16[128,2048]{1,0:T(8,128)(2,1)S(1)}, u32[]{:S(2)}, u32[]{:S(2)}) collective-permute-start(bf16[128,2048]{1,0:T(8,128)(2,1)} %get-tuple-element.146), channel_id=1, source_target_pairs={{0,3},{1,2},{2,1},{3,0},{4,7},{5,6},{6,5},{7,4},{8,11},{9,10},{10,... | collective-permute-start | bytes 1572872 | tf_op jit(solution)/shard_map/ppermute | solution.py:824
  174.9 26.4 %collective-permute-start.16 = (bf16[128,2048]{1,0:T(8,128)(2,1)S(1)}, bf16[128,2048]{1,0:T(8,128)(2,1)S(1)}, u32[]{:S(2)}, u32[]{:S(2)}) collective-permute-start(bf16[128,2048]{1,0:T(8,128)(2,1)S(1)} %add_convert_fusion.10), channel_id=1, source_target_pairs={{0,8},{4,12},{8,0},{12,4},{16,24},{20,28},{24,16},{28,20},{1,9},{5... | collective-permute-start | bytes 1572872 | tf_op jit(solution)/shard_map/ppermute | solution.py:824
  205.5 28.5 %collective-permute-start.17 = (bf16[8448,256]{1,0:T(8,128)(2,1)}, bf16[8448,256]{1,0:T(8,128)(2,1)}, u32[]{:S(2)}, u32[]{:S(2)}) collective-permute-start(bf16[8448,256]{1,0:T(8,128)(2,1)} %bitcast.18.near.refs_2_), channel_id=1, source_target_pairs={{0,4},{4,0},{8,12},{12,8},{16,20},{20,16},{24,28},{28,24},{1,5},{5... | collective-permute-start | bytes 12976136 | tf_op jit(solution)/shard_map/ppermute | solution.py:824
  207.1 25.4 %collective-permute-start.19 = (bf16[128,2048]{1,0:T(8,128)(2,1)}, bf16[128,2048]{1,0:T(8,128)(2,1)S(1)}, u32[]{:S(2)}, u32[]{:S(2)}) collective-permute-start(bf16[128,2048]{1,0:T(8,128)(2,1)} %get-tuple-element.153.refs_0_), channel_id=1, source_target_pairs={{0,2},{1,3},{2,0},{3,1},{4,6},{5,7},{6,4},{7,5},{8,10},{9,11},{10,... | collective-permute-start | bytes 1572872 | tf_op jit(solution)/shard_map/ppermute | solution.py:824
  220.0 29.3 %collective-permute-start.22 = (bf16[128,2048]{1,0:T(8,128)(2,1)S(1)}, bf16[128,2048]{1,0:T(8,128)(2,1)S(1)}, u32[]{:S(2)}, u32[]{:S(2)}) collective-permute-start(bf16[128,2048]{1,0:T(8,128)(2,1)S(1)} %collective-permute-done.21.refs_0_), channel_id=1, source_target_pairs={{0,1},{1,0},{2,3},{3,2},{4,5},{5,4},{6,7},{7,6},{8,9},{9,8},{10,11... | collective-permute-start | bytes 1572872 | tf_op jit(solution)/shard_map/ppermute | solution.py:824
  221.5 33.4 %collective-permute-start.23 = (bf16[128,2048]{1,0:T(8,128)(2,1)S(1)}, bf16[128,2048]{1,0:T(8,128)(2,1)S(1)}, u32[]{:S(2)}, u32[]{:S(2)}) collective-permute-start(bf16[128,2048]{1,0:T(8,128)(2,1)S(1)} %collective-permute-done.21.refs_0_), channel_id=1, source_target_pairs={{0,2},{1,3},{2,0},{3,1},{4,6},{5,7},{6,4},{7,5},{8,10},{9,11},{10,... | collective-permute-start | bytes 1572872 | tf_op jit(solution)/shard_map/ppermute | solution.py:824
  343.2 110.6 %all-to-all-start.2 = ((bf16[4,2112,256]{2,1,0:T(8,128)(2,1)}), bf16[4,2112,256]{2,1,0:T(8,128)(2,1)}, u32[]{:S(2)}, u32[]{:S(2)}) async-start(bf16[4,2112,256]{2,1,0:T(8,128)(2,1)} %bitcast.109), calls=%async_computation.3 | async-start | bytes 8650752 | tf_op jit(solution)/shard_map/all_to_all | solution.py:877
  348.2 176.3 %reduce-scatter.2.cloned.1.call-start = ((), (), s32[]{:S(2)}) async-start(), calls=%async_computation.6 | async-start | bytes 5242880 | tf_op jit(solution)/shard_map/reduce_scatter | solution.py:1073
  348.4 26.1 %collective-permute-start.36 = (bf16[128,2048]{1,0:T(8,128)(2,1)S(1)}, bf16[128,2048]{1,0:T(8,128)(2,1)S(1)}, u32[]{:S(2)}, u32[]{:S(2)}) collective-permute-start(bf16[128,2048]{1,0:T(8,128)(2,1)S(1)} %copy-done.39), channel_id=1, source_target_pairs={{0,2},{1,3},{2,0},{3,1},{4,6},{5,7},{6,4},{7,5},{8,10},{9,11},{10,... | collective-permute-start | bytes 1572872 | tf_op jit(solution)/shard_map/ppermute | solution.py:824
  351.8 33.9 %collective-permute-start.39 = (bf16[128,2048]{1,0:T(8,128)(2,1)S(1)}, bf16[128,2048]{1,0:T(8,128)(2,1)S(1)}, u32[]{:S(2)}, u32[]{:S(2)}) collective-permute-start(bf16[128,2048]{1,0:T(8,128)(2,1)S(1)} %collective-permute-done.38.refs_0_), channel_id=1, source_target_pairs={{0,1},{1,0},{2,3},{3,2},{4,5},{5,4},{6,7},{7,6},{8,9},{9,8},{10,11... | collective-permute-start | bytes 1572872 | tf_op jit(solution)/shard_map/ppermute | solution.py:824
  351.9 40.6 %collective-permute-start.40 = (bf16[128,2048]{1,0:T(8,128)(2,1)S(1)}, bf16[128,2048]{1,0:T(8,128)(2,1)}, u32[]{:S(2)}, u32[]{:S(2)}) collective-permute-start(bf16[128,2048]{1,0:T(8,128)(2,1)S(1)} %collective-permute-done.38.refs_0_), channel_id=1, source_target_pairs={{0,2},{1,3},{2,0},{3,1},{4,6},{5,7},{6,4},{7,5},{8,10},{9,11},{10,... | collective-permute-start | bytes 1572872 | tf_op jit(solution)/shard_map/ppermute | solution.py:824
  363.2 29.4 %collective-permute-start.41 = (bf16[128,2048]{1,0:T(8,128)(2,1)S(1)}, bf16[128,2048]{1,0:T(8,128)(2,1)}, u32[]{:S(2)}, u32[]{:S(2)}) collective-permute-start(bf16[128,2048]{1,0:T(8,128)(2,1)S(1)} %collective-permute-done.38.refs_0_), channel_id=1, source_target_pairs={{0,3},{1,2},{2,1},{3,0},{4,7},{5,6},{6,5},{7,4},{8,11},{9,10},{10,... | collective-permute-start | bytes 1572872 | tf_op jit(solution)/shard_map/ppermute | solution.py:824
  441.3 32.8 %collective-permute-start.45 = (bf16[784,1024]{1,0:T(8,128)(2,1)}, bf16[784,1024]{1,0:T(8,128)(2,1)}, u32[]{:S(2)}, u32[]{:S(2)}) collective-permute-start(bf16[784,1024]{1,0:T(8,128)(2,1)} %add_convert_fusion), channel_id=1, source_target_pairs={{0,4},{4,0},{8,12},{12,8},{16,20},{20,16},{24,28},{28,24},{1,5},{5... | collective-permute-start | bytes 4816904 | tf_op jit(solution)/shard_map/ppermute | solution.py:824
  478.9 66.2 %all-to-all-start.3 = ((bf16[4,1040,256]{2,1,0:T(8,128)(2,1)}), bf16[4,1040,256]{2,1,0:T(8,128)(2,1)S(1)}, u32[]{:S(2)}, u32[]{:S(2)}) async-start(bf16[4,1040,256]{2,1,0:T(8,128)(2,1)} %bitcast.110), calls=%async_computation.4 | async-start | bytes 4259840 | tf_op jit(solution)/shard_map/all_to_all | solution.py:877
  (112 other events, 1342.0 us)
Sparse Core Ops, SparseCore 0:
  96.4 74.0 all-gather.1
  392.7 52.9 reduce-scatter.1

commit v5 on v4

--- a/solution.py
+++ b/solution.py
@@ -513,38 +513,44 @@
         copy.wait()
 
 
-def mix_kernel(lines, count, width, near, far, *refs):
-    pieces, (rows_ref, x_ref, logit_ref, buf, row_sems, sems) = refs[:count], refs[count:]
-    copies = started(row_copies(pieces, rows_ref, row_sems))
-    copies += started(weight_copies((near, far), buf, sems, lines, 0, buf.shape[0]))
-    waited(copies)
-    out = lax.dot_general(rows_ref[...], buf[...], NT, preferred_element_type=f32)
-    x_ref[...] = out[:, :width].astype(bf16)
-    logit_ref[...] = out[:, width:]
+def mix_kernel(lines, count, halves, width, near, far, *refs):
+    pieces, outs = refs[: halves * count], refs[halves * count : halves * count + 3 * halves]
+    buf, row_sems, sems = refs[halves * count + 3 * halves :]
+    weights = started(weight_copies((near, far), buf, sems, lines, 0, buf.shape[0]))
+    rows = [
+        started(row_copies(pieces[half * count : (half + 1) * count], outs[half], row_sems.at[half]))
+        for half in range(halves)
+    ]
+    waited(weights)
+    for half in range(halves):
+        waited(rows[half])
+        out = lax.dot_general(outs[half][...], buf[...], NT, preferred_element_type=f32)
+        outs[halves + half][...] = out[:, :width].astype(bf16)
+        outs[2 * halves + half][...] = out[:, width:]
 
 
 def mix_product(lines, pieces, packs, width, extra):
     vmem = pl.BlockSpec(memory_space=pltpu.VMEM)
-    smem = pl.BlockSpec(memory_space=pltpu.SMEM)
     hbm = pl.BlockSpec(memory_space=pl.ANY)
-    tokens = pieces[0].shape[0] * len(pieces)
-    model = pieces[0].shape[1]
+    halves, count = len(pieces), len(pieces[0])
+    rows, model = pieces[0][0].shape
+    tokens = rows * count
     shape = jax.ShapeDtypeStruct
-    return pl.pallas_call(
-        functools.partial(mix_kernel, lines, len(pieces), width),
-        out_shape=(shape((tokens, model), bf16), shape((tokens, width), bf16), shape((tokens, extra), f32)),
-        in_specs=[hbm] * (2 + len(pieces)),
-        out_specs=(vmem,) * 3,
+    out = pl.pallas_call(
+        functools.partial(mix_kernel, lines, count, halves, width),
+        out_shape=(shape((tokens, model), bf16),) * halves
+        + (shape((tokens, width), bf16),) * halves
+        + (shape((tokens, extra), f32),) * halves,
+        in_specs=[hbm] * (2 + halves * count),
+        out_specs=(vmem,) * (3 * halves),
         scratch_shapes=[
             pltpu.VMEM((width + extra, model), bf16),
-            pltpu.SemaphoreType.DMA((len(pieces),)),
+            pltpu.SemaphoreType.DMA((halves, count)),
             pltpu.SemaphoreType.DMA((2 * lines,)),
         ],
-        cost_estimate=pl.CostEstimate(
-            flops=2 * tokens * model * (width + extra), bytes_accessed=2 * model * (2 * tokens + width), transcendentals=0
-        ),
         name="mix_product",
-    )(*packs, *pieces)
+    )(*packs, *[piece for half in pieces for piece in half])
+    return out[:halves], out[halves : 2 * halves], out[2 * halves :]
 
 
 def branch_kernel(lines, count, first, near, far, *refs):
@@ -572,9 +578,6 @@
             pltpu.SemaphoreType.DMA((len(pieces),)),
             pltpu.SemaphoreType.DMA((2 * lines,)),
         ],
-        cost_estimate=pl.CostEstimate(
-            flops=2 * tokens * model * units, bytes_accessed=2 * model * (2 * tokens + units), transcendentals=0
-        ),
         name="branch_back",
     )(*packs, *pieces)
 
@@ -644,9 +647,6 @@
             pltpu.SemaphoreType.DMA((2, count)),
             pltpu.SemaphoreType.DMA((3, 2 * lines)),
         ],
-        cost_estimate=pl.CostEstimate(
-            flops=10 * tokens * units * model, bytes_accessed=6 * units * model + 8 * tokens * model, transcendentals=tokens * units
-        ),
         name="ffn_part",
     )(seq, *packs, cots, *seconds)
 
@@ -712,11 +712,6 @@
         + [total] * (len(units) > 0),
         out_shape=[jax.ShapeDtypeStruct((rows, 2 * lines * depth), bf16)] * (count * halves)
         + [jax.ShapeDtypeStruct((1, 2 * lines * depth), f32)] * (len(units) > 0),
-        cost_estimate=pl.CostEstimate(
-            flops=4 * halves * tokens * inner * lines * depth,
-            bytes_accessed=4 * stride * lines * depth + 4 * halves * tokens * lines * depth,
-            transcendentals=0,
-        ),
         name="team_product",
     )(*flat, *packs, *units)
     return [out[half * count : (half + 1) * count] for half in range(halves)] + list(out[halves * count :])
@@ -769,11 +764,6 @@
         functools.partial(finish_product_kernel, len(lefts), first, units, steps, fold, stride, count),
         grid_spec=grid_spec,
         out_shape=jax.ShapeDtypeStruct((whole, 2 * lines * depth), bf16),
-        cost_estimate=pl.CostEstimate(
-            flops=4 * whole * units * lines * depth,
-            bytes_accessed=4 * stride * lines * depth + 4 * whole * lines * depth,
-            transcendentals=0,
-        ),
         name="finish_product",
     )(seq, *lefts, *packs)
 
@@ -996,8 +986,9 @@
 
     ffn_in = line_pack((w_gate.T, w_up.T, w_down), lines, mix_packs[1])
     cots_all = lax.all_gather(after(late_cot, mix_near), "seq", axis=0, tiled=True)
-    hidden_0, x_0, logit_0 = mix_product(lines, near_hidden, mix_packs, 3 * width, extra)
-    hidden_1, x_1, logit_1 = mix_product(lines, far_hidden, mix_packs, 3 * width, extra)
+    (hidden_0, hidden_1), (x_0, x_1), (logit_0, logit_1) = mix_product(
+        lines, (near_hidden, far_hidden), mix_packs, 3 * width, extra
+    )
     normed, mixed, kept = delta_forward(per, reset, place, (x_0, x_1), (logit_0, logit_1), taps, gain_h)
     o_span = ((o_first, width),)
     far_chunks, near_chunks = team_product(lines, ((normed[1],), (normed[0],)), o_span, mix_packs, seq_parts)
@@ -1104,7 +1095,7 @@
     early = lax.dynamic_update_slice_in_dim(early, d_taps, seq_place * full_width + odd * width, 1)
     gains = jnp.concatenate([grad_gain_one, grad_gain_two, early], axis=0).reshape(-1, DH)
     gains = chip_line_sum(jnp.concatenate([gains, grad_head], axis=0))
-    mix_cut = line_cut(lines, (x_kept, o_kept), after((x_got, o_got), gains, tuple(far_got), grad_gate, grad_up, grad_down))
+    mix_cut = line_cut(lines, (x_kept, o_kept), after((x_got, o_got), gains, tuple(far_got[:3]), grad_gate, grad_up, grad_down))
     mix_back = line_exchange(mix_cut)
     mix_spans = (
         (0, width),

time: 567 us -> 564 us (level)
    pallas_call x2 -> x1, Pallas kernels: 11.9 us -> 8.86 us  [mix_product(): pl.pallas_call(functools.partial(mix_kernel, lines, count, halves, width)...]
    unnamed x182 -> x180, local copies, waits for them, and re-layouts: 37.3 us -> 37.3 us
  transfers between devices with their start and end apart: 65 -> 65, of which waited for: 30 -> 32; matrix products, arithmetic and copies ran while one was open for 13% -> 13% of each run, Pallas kernels for 26% -> 26%
where the time goes in v5:
time: 564 us; the launch traced here: 554 us
  waiting for transfers between devices  210 us (37%)
  Pallas kernels  149 us (26%)
  starting transfers between devices  86.6 us (15%)
  local copies, waits for them, and re-layouts  48.3 us (9%)
  matrix products  26 us (5%)
  other arithmetic  18.2 us (3%)
  between operations  16.2 us (3%)
    ppermute x59, waiting for transfers between devices, swap(): return lax.ppermute(values, axis, [(i, i ^ mask) for i in range(size)])  209 us
    ppermute x59, starting transfers between devices, swap(): return lax.ppermute(values, axis, [(i, i ^ mask) for i in range(size)])  67 us
    unnamed x180, local copies, waits for them, and re-layouts  37.3 us
    pallas_call x2, Pallas kernels, ffn_part(): pl.pallas_call(functools.partial(ffn_kernel, lines, count, half), out_sha...  30.9 us
    dot_general x20, matrix products, dot(): lax.dot_general(left, right, dims, preferred_element_type=f32).astype(kind)  26 us
    pallas_call x1, Pallas kernels, delta_forward(): pl.pallas_call(functools.partial(fwd_kernel, per, groups), out_shape=(sha...  25.1 us
    pallas_call x1, Pallas kernels, delta_backward(): pl.pallas_call(functools.partial(bwd_kernel, per, groups), out_shape=(sha...  21.6 us
    pallas_call x6, Pallas kernels, on_core(): pl.pallas_call(kernel, out_shape=shapes, in_specs=[smem] + [vmem] * len(a...  19.7 us
  transfers between devices with their start and end apart: 65, of which 32 were waited for; matrix products, arithmetic and copies ran while one was open for 13% of the time, Pallas kernels for 26%

profile of v5, /device:TPU:0, one launch (start us, length us, event | category | flops | bytes accessed | tf_op | source)
XLA Modules:
  0.0 553.8 jit_solution(4942105054798385496)
XLA Ops:
  15.7 9.2 %collective-permute-done.1.y_ref = bf16[128,2048]{1,0:T(8,128)(2,1)} collective-permute-done((bf16[128,2048]{1,0:T(8,128)(2,1)}, bf16[128,2048]{1,0:T(8,128)(2,1)}, u32[]{:S(2)}, u32[]{:S(2)}) %collective-permute-start.1) | collective-permute-done | bytes 524320 | tf_op jit(solution)/shard_map/ppermute | solution.py:814
  49.3 6.6 %collective-permute-done.2.refs_1_ = bf16[128,2048]{1,0:T(8,128)(2,1)} collective-permute-done((bf16[128,2048]{1,0:T(8,128)(2,1)}, bf16[128,2048]{1,0:T(8,128)(2,1)}, u32[]{:S(2)}, u32[]{:S(2)}) %collective-permute-start.2) | collective-permute-done | bytes 524320 | tf_op jit(solution)/shard_map/ppermute | solution.py:814
  62.3 11.1 %collective-permute-done.8.y_ref = bf16[128,2048]{1,0:T(8,128)(2,1)} collective-permute-done((bf16[128,2048]{1,0:T(8,128)(2,1)S(1)}, bf16[128,2048]{1,0:T(8,128)(2,1)}, u32[]{:S(2)}, u32[]{:S(2)}) %collective-permute-start.8) | collective-permute-done | bytes 524320 | tf_op jit(solution)/shard_map/ppermute | solution.py:814
  95.5 8.9 %mix_product.1 = (bf16[512,2048]{1,0:T(8,128)(2,1)}, bf16[512,2048]{1,0:T(8,128)(2,1)}, bf16[512,768]{1,0:T(8,128)(2,1)}, bf16[512,768]{1,0:T(8,128)(2,1)}, f32[512,16]{1,0:T(8,128)}, /*index=5*/f32[512,16]{1,0:T(8,128)}) custom-call(bf16[4160,256]{1,0:T(8,128)(2,1)} %bitcast.103, bf16[4160,256]{1,0:T(8,128)(2,1)} %copy-done.1, ...), custom_call_target="tpu_custom_call" | custom-call | tf_op jit(solution)/shard_map/mix_product/pallas_call | solution.py:539
  104.4 25.1 %delta_forward.1 = (bf16[512,256]{1,0:T(8,128)(2,1)}, bf16[512,256]{1,0:T(8,128)(2,1)}, bf16[512,256]{1,0:T(8,128)(2,1)}, bf16[512,256]{1,0:T(8,128)(2,1)}, bf16...) custom-call(f32[16]{0:T(128)} %pad_maximum_fusion.7.reset_ref, ...), custom_call_target="tpu_custom_call" | custom-call | tf_op jit(solution)/shard_map/delta_forward/pallas_call | solution.py:193
  142.0 20.6 %collective-permute-done.15 = bf16[128,2048]{1,0:T(8,128)(2,1)S(1)} collective-permute-done((bf16[128,2048]{1,0:T(8,128)(2,1)}, bf16[128,2048]{1,0:T(8,128)(2,1)S(1)}, u32[]{:S(2)}, u32[]{:S(2)}) %collective-permute-start.15) | collective-permute-done | bytes 524320 | tf_op jit(solution)/shard_map/ppermute | solution.py:814
  163.1 9.8 %collective-permute-done.14 = bf16[128,2048]{1,0:T(8,128)(2,1)S(1)} collective-permute-done((bf16[128,2048]{1,0:T(8,128)(2,1)}, bf16[128,2048]{1,0:T(8,128)(2,1)S(1)}, u32[]{:S(2)}, u32[]{:S(2)}) %collective-permute-start.14) | collective-permute-done | bytes 524320 | tf_op jit(solution)/shard_map/ppermute | solution.py:814
  176.8 7.6 %collective-permute-done.10.refs_1_ = bf16[128,2048]{1,0:T(8,128)(2,1)S(1)} collective-permute-done((bf16[128,2048]{1,0:T(8,128)(2,1)}, bf16[128,2048]{1,0:T(8,128)(2,1)S(1)}, u32[]{:S(2)}, u32[]{:S(2)}) %collective-permute-start.10) | collective-permute-done | bytes 524320 | tf_op jit(solution)/shard_map/ppermute | solution.py:814
  184.4 11.6 %collective-permute-done.12.refs_3_ = bf16[128,2048]{1,0:T(8,128)(2,1)S(1)} collective-permute-done((bf16[128,2048]{1,0:T(8,128)(2,1)}, bf16[128,2048]{1,0:T(8,128)(2,1)S(1)}, u32[]{:S(2)}, u32[]{:S(2)}) %collective-permute-start.12) | collective-permute-done | bytes 524320 | tf_op jit(solution)/shard_map/ppermute | solution.py:814
  209.0 10.9 %collective-permute-done.21.refs_0_ = bf16[128,2048]{1,0:T(8,128)(2,1)S(1)} collective-permute-done((bf16[128,2048]{1,0:T(8,128)(2,1)}, bf16[128,2048]{1,0:T(8,128)(2,1)S(1)}, u32[]{:S(2)}, u32[]{:S(2)}) %collective-permute-start.21) | collective-permute-done | bytes 524320 | tf_op jit(solution)/shard_map/ppermute | solution.py:814
  222.9 9.5 %collective-permute-done.19.refs_2_ = bf16[128,2048]{1,0:T(8,128)(2,1)S(1)} collective-permute-done((bf16[128,2048]{1,0:T(8,128)(2,1)}, bf16[128,2048]{1,0:T(8,128)(2,1)S(1)}, u32[]{:S(2)}, u32[]{:S(2)}) %collective-permute-start.19) | collective-permute-done | bytes 524320 | tf_op jit(solution)/shard_map/ppermute | solution.py:814
  234.6 15.2 %ffn_part.2 = (bf16[512,2048]{1,0:T(8,128)(2,1)}, bf16[512,2048]{1,0:T(8,128)(2,1)}, bf16[512,704]{1,0:T(8,128)(2,1)}, bf16[512,704]{1,0:T(8,128)(2,1)}, bf16[51...) custom-call(s32[1]{0:T(128)} %bitcast.4.place_ref.seq_ref, ...), custom_call_target="tpu_custom_call" | custom-call | tf_op jit(solution)/shard_map/ffn_part/pallas_call | solution.py:638
  255.5 15.7 %ffn_part.3 = (bf16[512,2048]{1,0:T(8,128)(2,1)}, bf16[512,2048]{1,0:T(8,128)(2,1)}, bf16[512,704]{1,0:T(8,128)(2,1)}, bf16[512,704]{1,0:T(8,128)(2,1)}, bf16[51...) custom-call(s32[1]{0:T(128)} %bitcast.4.place_ref.seq_ref, ...), custom_call_target="tpu_custom_call" | custom-call | tf_op jit(solution)/shard_map/ffn_part/pallas_call | solution.py:638
  300.3 8.5 %collective-permute-done.29 = bf16[128,2048]{1,0:T(8,128)(2,1)S(1)} collective-permute-done((bf16[128,2048]{1,0:T(8,128)(2,1)S(1)}, bf16[128,2048]{1,0:T(8,128)(2,1)S(1)}, u32[]{:S(2)}, u32[]{:S(2)}) %collective-permute-start.29) | collective-permute-done | bytes 524320 | tf_op jit(solution)/shard_map/ppermute | solution.py:814
  328.3 10.3 %collective-permute-done.38.refs_0_ = bf16[128,2048]{1,0:T(8,128)(2,1)S(1)} collective-permute-done((bf16[128,2048]{1,0:T(8,128)(2,1)}, bf16[128,2048]{1,0:T(8,128)(2,1)S(1)}, u32[]{:S(2)}, u32[]{:S(2)}) %collective-permute-start.38) | collective-permute-done | bytes 524320 | tf_op jit(solution)/shard_map/ppermute | solution.py:814
  350.4 8.2 %collective-permute-done.35.refs_1_ = bf16[128,2048]{1,0:T(8,128)(2,1)S(1)} collective-permute-done((bf16[128,2048]{1,0:T(8,128)(2,1)S(1)}, bf16[128,2048]{1,0:T(8,128)(2,1)S(1)}, u32[]{:S(2)}, u32[]{:S(2)}) %collective-permute-start.35) | collective-permute-done | bytes 524320 | tf_op jit(solution)/shard_map/ppermute | solution.py:814
  361.2 9.8 %collective-permute-done.36.refs_2_ = bf16[128,2048]{1,0:T(8,128)(2,1)S(1)} collective-permute-done((bf16[128,2048]{1,0:T(8,128)(2,1)S(1)}, bf16[128,2048]{1,0:T(8,128)(2,1)S(1)}, u32[]{:S(2)}, u32[]{:S(2)}) %collective-permute-start.36) | collective-permute-done | bytes 524320 | tf_op jit(solution)/shard_map/ppermute | solution.py:814
  371.0 9.3 %finish_product.1 = bf16[1024,2048]{1,0:T(8,128)(2,1)} custom-call(s32[1]{0:T(128)} %bitcast.4.place_ref.seq_ref, bf16[512,704]{1,0:T(8,128)(2,1)} %get-tuple-element.197.refs_0_, bf16[512,704]{1,0:T(8,128)(2,1)} %get-tuple-element.198.refs_1_, bf16[8448,256]{1,0:T(8,128)(2,1)} %bitcast.18.near.refs_2_, bf16[8448,256]{1,0:T(8,128)(2,1)} %collective-permute-done.17.far.refs_3_), custom_call_target="tpu_custom_call" | custom-call | tf_op jit(solution)/shard_map/finish_product/pallas_call | solution.py:763
  381.2 8.5 %collective-permute-done.40.refs_2_ = bf16[128,2048]{1,0:T(8,128)(2,1)} collective-permute-done((bf16[128,2048]{1,0:T(8,128)(2,1)S(1)}, bf16[128,2048]{1,0:T(8,128)(2,1)}, u32[]{:S(2)}, u32[]{:S(2)}) %collective-permute-start.40) | collective-permute-done | bytes 524320 | tf_op jit(solution)/shard_map/ppermute | solution.py:814
  396.9 21.6 %delta_backward.1 = (bf16[512,784]{1,0:T(8,128)(2,1)}, bf16[512,784]{1,0:T(8,128)(2,1)}, f32[12,256]{1,0:T(8,128)}, f32[1,128]{1,0:T(1,128)}) custom-call(f32[16]{0:T(128)} %pad_maximum_fusion.7.reset_ref, s32[1]{0:T(128)} %bitcast.4.place_ref.seq_ref, f32[12,256]{1,0:T(8,128)} %constant_dynamic-slice_fusion.1.conv_ref, ...), custom_call_target="tpu_custom_call" | custom-call | tf_op jit(solution)/shard_map/delta_backward/pallas_call | solution.py:376
  418.5 9.5 %team_product.3 = (bf16[128,2048]{1,0:T(8,128)(2,1)}, bf16[128,2048]{1,0:T(8,128)(2,1)}, bf16[128,2048]{1,0:T(8,128)(2,1)}, bf16[128,2048]{1,0:T(8,128)(2,1)}, b...) custom-call(bf16[512,784]{1,0:T(8,128)(2,1)} %get-tuple-element.225., ...), custom_call_target="tpu_custom_call" | custom-call | tf_op jit(solution)/shard_map/team_product/pallas_call | solution.py:702
  474.4 11.0 %collective-permute-done.44 = bf16[128,2048]{1,0:T(8,128)(2,1)} collective-permute-done((bf16[128,2048]{1,0:T(8,128)(2,1)}, bf16[128,2048]{1,0:T(8,128)(2,1)}, u32[]{:S(2)}, u32[]{:S(2)}) %collective-permute-start.44) | collective-permute-done | bytes 524320 | tf_op jit(solution)/shard_map/ppermute | solution.py:814
  485.4 10.9 %collective-permute-done.51.refs_1_ = bf16[128,2048]{1,0:T(8,128)(2,1)} collective-permute-done((bf16[128,2048]{1,0:T(8,128)(2,1)}, bf16[128,2048]{1,0:T(8,128)(2,1)}, u32[]{:S(2)}, u32[]{:S(2)}) %collective-permute-start.51) | collective-permute-done | bytes 524320 | tf_op jit(solution)/shard_map/ppermute | solution.py:814
  496.5 8.2 %collective-permute-done.53.refs_3_ = bf16[128,2048]{1,0:T(8,128)(2,1)} collective-permute-done((bf16[128,2048]{1,0:T(8,128)(2,1)}, bf16[128,2048]{1,0:T(8,128)(2,1)}, u32[]{:S(2)}, u32[]{:S(2)}) %collective-permute-start.53) | collective-permute-done | bytes 524320 | tf_op jit(solution)/shard_map/ppermute | solution.py:814
  (389 shorter events, 260.2 us)
Async XLA Ops:
  24.9 51.7 %all-to-all-start = ((bf16[4,1040,256]{2,1,0:T(8,128)(2,1)}), bf16[4,1040,256]{2,1,0:T(8,128)(2,1)S(1)}, u32[]{:S(2)}, u32[]{:S(2)}) async-start(bf16[4,1040,256]{2,1,0:T(8,128)(2,1)} %bitcast.118), calls=%async_computation | async-start | bytes 4259840 | tf_op jit(solution)/shard_map/all_to_all | solution.py:867
  40.7 35.2 %collective-permute-start.3 = (bf16[128,2048]{1,0:T(8,128)(2,1)}, bf16[128,2048]{1,0:T(8,128)(2,1)}, u32[]{:S(2)}, u32[]{:S(2)}) collective-permute-start(bf16[128,2048]{1,0:T(8,128)(2,1)} %get-tuple-element.132.refs_0_), channel_id=1, source_target_pairs={{0,2},{1,3},{2,0},{3,1},{4,6},{5,7},{6,4},{7,5},{8,10},{9,11},{10,... | collective-permute-start | bytes 1572872 | tf_op jit(solution)/shard_map/ppermute | solution.py:814
  47.2 26.1 %collective-permute-start.8 = (bf16[128,2048]{1,0:T(8,128)(2,1)S(1)}, bf16[128,2048]{1,0:T(8,128)(2,1)}, u32[]{:S(2)}, u32[]{:S(2)}) collective-permute-start(bf16[128,2048]{1,0:T(8,128)(2,1)S(1)} %copy-done.22), channel_id=1, source_target_pairs={{0,8},{4,12},{8,0},{12,4},{16,24},{20,28},{24,16},{28,20},{1,9},{5... | collective-permute-start | bytes 1572872 | tf_op jit(solution)/shard_map/ppermute | solution.py:814
  87.2 118.1 %all-to-all-start.1 = ((bf16[4,2112,256]{2,1,0:T(8,128)(2,1)}), bf16[4,2112,256]{2,1,0:T(8,128)(2,1)}, u32[]{:S(2)}, u32[]{:S(2)}) async-start(bf16[4,2112,256]{2,1,0:T(8,128)(2,1)} %bitcast.17), calls=%async_computation.1 | async-start | bytes 8650752 | tf_op jit(solution)/shard_map/all_to_all | solution.py:867
  93.0 140.8 %all-gather.2.cloned.1.call-start = ((), (), s32[]{:S(2)}) async-start(), calls=%async_computation.5 | async-start | bytes 5242880 | tf_op jit(solution)/shard_map/all_gather | solution.py:988
  135.4 27.2 %collective-permute-start.15 = (bf16[128,2048]{1,0:T(8,128)(2,1)}, bf16[128,2048]{1,0:T(8,128)(2,1)S(1)}, u32[]{:S(2)}, u32[]{:S(2)}) collective-permute-start(bf16[128,2048]{1,0:T(8,128)(2,1)} %get-tuple-element.150), channel_id=1, source_target_pairs={{0,3},{1,2},{2,1},{3,0},{4,7},{5,6},{6,5},{7,4},{8,11},{9,10},{10,... | collective-permute-start | bytes 1572872 | tf_op jit(solution)/shard_map/ppermute | solution.py:814
  137.9 35.0 %collective-permute-start.14 = (bf16[128,2048]{1,0:T(8,128)(2,1)}, bf16[128,2048]{1,0:T(8,128)(2,1)S(1)}, u32[]{:S(2)}, u32[]{:S(2)}) collective-permute-start(bf16[128,2048]{1,0:T(8,128)(2,1)} %get-tuple-element.149), channel_id=1, source_target_pairs={{0,2},{1,3},{2,0},{3,1},{4,6},{5,7},{6,4},{7,5},{8,10},{9,11},{10,... | collective-permute-start | bytes 1572872 | tf_op jit(solution)/shard_map/ppermute | solution.py:814
  138.4 34.7 %collective-permute-start.13 = (bf16[128,2048]{1,0:T(8,128)(2,1)}, bf16[128,2048]{1,0:T(8,128)(2,1)S(1)}, u32[]{:S(2)}, u32[]{:S(2)}) collective-permute-start(bf16[128,2048]{1,0:T(8,128)(2,1)} %get-tuple-element.148), channel_id=1, source_target_pairs={{0,1},{1,0},{2,3},{3,2},{4,5},{5,4},{6,7},{7,6},{8,9},{9,8},{10,11... | collective-permute-start | bytes 1572872 | tf_op jit(solution)/shard_map/ppermute | solution.py:814
  139.0 45.4 %collective-permute-start.10 = (bf16[128,2048]{1,0:T(8,128)(2,1)}, bf16[128,2048]{1,0:T(8,128)(2,1)S(1)}, u32[]{:S(2)}, u32[]{:S(2)}) collective-permute-start(bf16[128,2048]{1,0:T(8,128)(2,1)} %get-tuple-element.144), channel_id=1, source_target_pairs={{0,1},{1,0},{2,3},{3,2},{4,5},{5,4},{6,7},{7,6},{8,9},{9,8},{10,11... | collective-permute-start | bytes 1572872 | tf_op jit(solution)/shard_map/ppermute | solution.py:814
  140.5 43.9 %collective-permute-start.11 = (bf16[128,2048]{1,0:T(8,128)(2,1)}, bf16[128,2048]{1,0:T(8,128)(2,1)S(1)}, u32[]{:S(2)}, u32[]{:S(2)}) collective-permute-start(bf16[128,2048]{1,0:T(8,128)(2,1)} %get-tuple-element.145), channel_id=1, source_target_pairs={{0,2},{1,3},{2,0},{3,1},{4,6},{5,7},{6,4},{7,5},{8,10},{9,11},{10,... | collective-permute-start | bytes 1572872 | tf_op jit(solution)/shard_map/ppermute | solution.py:814
  162.6 33.4 %collective-permute-start.12 = (bf16[128,2048]{1,0:T(8,128)(2,1)}, bf16[128,2048]{1,0:T(8,128)(2,1)S(1)}, u32[]{:S(2)}, u32[]{:S(2)}) collective-permute-start(bf16[128,2048]{1,0:T(8,128)(2,1)} %get-tuple-element.146), channel_id=1, source_target_pairs={{0,3},{1,2},{2,1},{3,0},{4,7},{5,6},{6,5},{7,4},{8,11},{9,10},{10,... | collective-permute-start | bytes 1572872 | tf_op jit(solution)/shard_map/ppermute | solution.py:814
  174.5 26.5 %collective-permute-start.16 = (bf16[128,2048]{1,0:T(8,128)(2,1)S(1)}, bf16[128,2048]{1,0:T(8,128)(2,1)S(1)}, u32[]{:S(2)}, u32[]{:S(2)}) collective-permute-start(bf16[128,2048]{1,0:T(8,128)(2,1)S(1)} %add_convert_fusion.10), channel_id=1, source_target_pairs={{0,8},{4,12},{8,0},{12,4},{16,24},{20,28},{24,16},{28,20},{1,9},{5... | collective-permute-start | bytes 1572872 | tf_op jit(solution)/shard_map/ppermute | solution.py:814
  205.3 28.5 %collective-permute-start.17 = (bf16[8448,256]{1,0:T(8,128)(2,1)}, bf16[8448,256]{1,0:T(8,128)(2,1)}, u32[]{:S(2)}, u32[]{:S(2)}) collective-permute-start(bf16[8448,256]{1,0:T(8,128)(2,1)} %bitcast.18.near.refs_2_), channel_id=1, source_target_pairs={{0,4},{4,0},{8,12},{12,8},{16,20},{20,16},{24,28},{28,24},{1,5},{5... | collective-permute-start | bytes 12976136 | tf_op jit(solution)/shard_map/ppermute | solution.py:814
  207.0 25.4 %collective-permute-start.19 = (bf16[128,2048]{1,0:T(8,128)(2,1)}, bf16[128,2048]{1,0:T(8,128)(2,1)S(1)}, u32[]{:S(2)}, u32[]{:S(2)}) collective-permute-start(bf16[128,2048]{1,0:T(8,128)(2,1)} %get-tuple-element.153.refs_0_), channel_id=1, source_target_pairs={{0,2},{1,3},{2,0},{3,1},{4,6},{5,7},{6,4},{7,5},{8,10},{9,11},{10,... | collective-permute-start | bytes 1572872 | tf_op jit(solution)/shard_map/ppermute | solution.py:814
  219.9 32.4 %collective-permute-start.22 = (bf16[128,2048]{1,0:T(8,128)(2,1)S(1)}, bf16[128,2048]{1,0:T(8,128)(2,1)S(1)}, u32[]{:S(2)}, u32[]{:S(2)}) collective-permute-start(bf16[128,2048]{1,0:T(8,128)(2,1)S(1)} %collective-permute-done.21.refs_0_), channel_id=1, source_target_pairs={{0,1},{1,0},{2,3},{3,2},{4,5},{5,4},{6,7},{7,6},{8,9},{9,8},{10,11... | collective-permute-start | bytes 1572872 | tf_op jit(solution)/shard_map/ppermute | solution.py:814
  221.4 33.3 %collective-permute-start.23 = (bf16[128,2048]{1,0:T(8,128)(2,1)S(1)}, bf16[128,2048]{1,0:T(8,128)(2,1)S(1)}, u32[]{:S(2)}, u32[]{:S(2)}) collective-permute-start(bf16[128,2048]{1,0:T(8,128)(2,1)S(1)} %collective-permute-done.21.refs_0_), channel_id=1, source_target_pairs={{0,2},{1,3},{2,0},{3,1},{4,6},{5,7},{6,4},{7,5},{8,10},{9,11},{10,... | collective-permute-start | bytes 1572872 | tf_op jit(solution)/shard_map/ppermute | solution.py:814
  338.6 110.7 %all-to-all-start.2 = ((bf16[4,2112,256]{2,1,0:T(8,128)(2,1)}), bf16[4,2112,256]{2,1,0:T(8,128)(2,1)}, u32[]{:S(2)}, u32[]{:S(2)}) async-start(bf16[4,2112,256]{2,1,0:T(8,128)(2,1)} %bitcast.108), calls=%async_computation.3 | async-start | bytes 8650752 | tf_op jit(solution)/shard_map/all_to_all | solution.py:867
  343.6 178.2 %reduce-scatter.2.cloned.1.call-start = ((), (), s32[]{:S(2)}) async-start(), calls=%async_computation.6 | async-start | bytes 5242880 | tf_op jit(solution)/shard_map/reduce_scatter | solution.py:1064
  344.3 26.7 %collective-permute-start.36 = (bf16[128,2048]{1,0:T(8,128)(2,1)S(1)}, bf16[128,2048]{1,0:T(8,128)(2,1)S(1)}, u32[]{:S(2)}, u32[]{:S(2)}) collective-permute-start(bf16[128,2048]{1,0:T(8,128)(2,1)S(1)} %copy-done.38), channel_id=1, source_target_pairs={{0,2},{1,3},{2,0},{3,1},{4,6},{5,7},{6,4},{7,5},{8,10},{9,11},{10,... | collective-permute-start | bytes 1572872 | tf_op jit(solution)/shard_map/ppermute | solution.py:814
  347.3 33.9 %collective-permute-start.39 = (bf16[128,2048]{1,0:T(8,128)(2,1)S(1)}, bf16[128,2048]{1,0:T(8,128)(2,1)S(1)}, u32[]{:S(2)}, u32[]{:S(2)}) collective-permute-start(bf16[128,2048]{1,0:T(8,128)(2,1)S(1)} %collective-permute-done.38.refs_0_), channel_id=1, source_target_pairs={{0,1},{1,0},{2,3},{3,2},{4,5},{5,4},{6,7},{7,6},{8,9},{9,8},{10,11... | collective-permute-start | bytes 1572872 | tf_op jit(solution)/shard_map/ppermute | solution.py:814
  348.4 41.3 %collective-permute-start.40 = (bf16[128,2048]{1,0:T(8,128)(2,1)S(1)}, bf16[128,2048]{1,0:T(8,128)(2,1)}, u32[]{:S(2)}, u32[]{:S(2)}) collective-permute-start(bf16[128,2048]{1,0:T(8,128)(2,1)S(1)} %collective-permute-done.38.refs_0_), channel_id=1, source_target_pairs={{0,2},{1,3},{2,0},{3,1},{4,6},{5,7},{6,4},{7,5},{8,10},{9,11},{10,... | collective-permute-start | bytes 1572872 | tf_op jit(solution)/shard_map/ppermute | solution.py:814
  358.6 31.0 %collective-permute-start.41 = (bf16[128,2048]{1,0:T(8,128)(2,1)S(1)}, bf16[128,2048]{1,0:T(8,128)(2,1)}, u32[]{:S(2)}, u32[]{:S(2)}) collective-permute-start(bf16[128,2048]{1,0:T(8,128)(2,1)S(1)} %collective-permute-done.38.refs_0_), channel_id=1, source_target_pairs={{0,3},{1,2},{2,1},{3,0},{4,7},{5,6},{6,5},{7,4},{8,11},{9,10},{10,... | collective-permute-start | bytes 1572872 | tf_op jit(solution)/shard_map/ppermute | solution.py:814
  464.6 77.1 %all-to-all-start.3 = ((bf16[4,1040,256]{2,1,0:T(8,128)(2,1)}), bf16[4,1040,256]{2,1,0:T(8,128)(2,1)S(1)}, u32[]{:S(2)}, u32[]{:S(2)}) async-start(bf16[4,1040,256]{2,1,0:T(8,128)(2,1)} %bitcast.109), calls=%async_computation.4 | async-start | bytes 4259840 | tf_op jit(solution)/shard_map/all_to_all | solution.py:867
  472.8 31.9 %collective-permute-start.53 = (bf16[128,2048]{1,0:T(8,128)(2,1)}, bf16[128,2048]{1,0:T(8,128)(2,1)}, u32[]{:S(2)}, u32[]{:S(2)}) collective-permute-start(bf16[128,2048]{1,0:T(8,128)(2,1)} %get-tuple-element.239), channel_id=1, source_target_pairs={{0,3},{1,2},{2,1},{3,0},{4,7},{5,6},{6,5},{7,4},{8,11},{9,10},{10,... | collective-permute-start | bytes 1572872 | tf_op jit(solution)/shard_map/ppermute | solution.py:814
  (111 other events, 1340.9 us)
Sparse Core Ops, SparseCore 0:
  96.3 76.0 all-gather.1
  389.8 53.0 reduce-scatter.1
